TPU v7x, 32 devices: a whole 2x2x4 slice. The times are simulated.
32 devices in a mesh: gx: 8 (over z, x), gy: 4 (over y, core).
Axes of the slice: x: 2, y: 2, z: 4, core: 2. Of those that a mesh axis runs over, the one named last changes fastest.
Arguments:
- phase_frac: float32 [8, 64, 64, 128], P(None, 'gx', 'gy'), may hold values from 0 to 1, as said below
- phase_ids: int32 [8, 64, 64, 128], P(None, 'gx', 'gy'), may hold values from 0 to 15, as said below
- conc: float32 [64, 64, 128], P('gx', 'gy'), may hold values from -6 to 6
- pair_class: int32 [16, 16], replicated, may hold values from 0 to 3, as said below
- mobility: float32 [4], replicated, may hold values from 0.01 to 0.06
- drive: float32 [16], replicated, may hold values from -4 to 4
- diffusivity: float32 [16], replicated, may hold values from 8 to 800
Outputs:
- new_frac: float32 [8, 64, 64, 128], P(None, 'gx', 'gy')
- new_conc: float32 [64, 64, 128], P('gx', 'gy')
Inputs may be any that keep to these rules, and one draw needn't show every extreme that they name: `phase_frac`: for every voxel the 8 fractions are positive and sum to 1. `phase_ids`: the 8 ids of one voxel are distinct. `pair_class`: Symmetric.
All inputs are finite; a program needn't handle non-finite values.
Results may differ from a plain program's by a relative error of at most 0.0003.
Values sent between devices are 32-bit elements; how exact they have to be, the bound alone decides.
No kernel may reach another device: no remote copies, remote signals or barrier semaphores. Data moves between devices by JAX's collectives and lax.ppermute only.
A program may use at most 64 MiB of HBM per device.

v0:
```python
import jax
import jax.numpy as jnp
from jax import lax
from jax.sharding import PartitionSpec as P

KAPPA = 2.0
DRIVE = 4.0


def with_halo(cells, sides, width, closed):
    for axis, dim in sides:
        count = lax.axis_size(axis)
        ends = count if closed else count - 1
        head = lax.slice_in_dim(cells, 0, width, axis=dim)
        tail = lax.slice_in_dim(cells, cells.shape[dim] - width, cells.shape[dim], axis=dim)
        cells = jnp.concatenate(
            [
                lax.ppermute(tail, axis, [(i, (i + 1) % count) for i in range(ends)]),
                cells,
                lax.ppermute(head, axis, [((i + 1) % count, i) for i in range(ends)]),
            ],
            axis=dim,
        )
    return cells


def thomas(sub_diag, main_diag, super_diag, rhs_lines):
    sub_diag = jnp.broadcast_to(sub_diag, rhs_lines.shape)
    main_diag = jnp.broadcast_to(main_diag, rhs_lines.shape)
    super_diag = jnp.broadcast_to(super_diag, rhs_lines.shape)
    anchor = jnp.zeros(rhs_lines.shape[1:], jnp.float32)

    def forward(running, coeffs):
        ratio_prev, value_prev = running
        sub_term, main_term, super_term, source_term = coeffs
        pivot_term = main_term - sub_term * ratio_prev
        ratio_now = super_term / pivot_term
        value_now = (source_term - sub_term * value_prev) / pivot_term
        return ((ratio_now, value_now), (ratio_now, value_now))

    _, (ratios, values) = lax.scan(
        forward, (anchor, anchor), (sub_diag, main_diag, super_diag, rhs_lines)
    )

    def backward(following, coeffs):
        ratio_now, value_now = coeffs
        current = value_now - ratio_now * following
        return (current, current)

    _, solved = lax.scan(backward, anchor, (ratios, values), reverse=True)
    return solved


def line_parts(diffus, field):
    face = 0.5 * (diffus[1:] + diffus[:-1])
    flux = face * (field[1:] - field[:-1])
    border = jnp.zeros_like(face[:1])
    face_left = jnp.concatenate([border, face])
    face_right = jnp.concatenate([face, border])
    flux_left = jnp.concatenate([border, flux])
    flux_right = jnp.concatenate([flux, border])
    return (flux_right - flux_left, -face_left, 1.0 + face_left + face_right, -face_right)


def side_parts(diff_line, conc_line, diffus, field, position, total):
    face_left = jnp.where(position > 0, 0.5 * (diff_line[:-2] + diffus), 0.0)
    face_right = jnp.where(position < total - 1, 0.5 * (diffus + diff_line[2:]), 0.0)
    flux_left = face_left * (field - conc_line[:-2])
    flux_right = face_right * (conc_line[2:] - field)
    return (flux_right - flux_left, -face_left, 1.0 + face_left + face_right, -face_right)


def partition(sub_diag, main_diag, super_diag, source, collect, position):
    lines, batch = source.shape
    blank = jnp.zeros((1, batch), jnp.float32)
    sub_inner = jnp.concatenate([blank, sub_diag[1 : lines - 1]])
    super_inner = jnp.concatenate([super_diag[: lines - 2], blank])
    left_unit = jnp.zeros((lines - 1, batch), jnp.float32).at[0].set(-sub_diag[0])
    right_unit = (
        jnp.zeros((lines - 1, batch), jnp.float32).at[lines - 2].set(-super_diag[lines - 2])
    )
    stacked = jnp.stack([source[: lines - 1], left_unit, right_unit], axis=1)
    solved = thomas(
        sub_inner[:, None], main_diag[: lines - 1][:, None], super_inner[:, None], stacked
    )
    base_part, left_part, right_part = (solved[:, 0], solved[:, 1], solved[:, 2])
    payload = jnp.stack(
        [
            base_part[0],
            left_part[0],
            right_part[0],
            base_part[-1],
            left_part[-1],
            right_part[-1],
            sub_diag[lines - 1],
            main_diag[lines - 1],
            super_diag[lines - 1],
            source[lines - 1],
        ]
    )[None]
    every = collect(payload)
    following = jnp.concatenate([every[1:, 0:3], jnp.zeros((1, 3, batch), jnp.float32)])
    reduced_sub = every[:, 6] * every[:, 4]
    reduced_main = every[:, 6] * every[:, 5] + every[:, 7] + every[:, 8] * following[:, 1]
    reduced_super = every[:, 8] * following[:, 2]
    reduced_source = every[:, 9] - every[:, 6] * every[:, 3] - every[:, 8] * following[:, 0]
    joints = thomas(reduced_sub, reduced_main, reduced_super, reduced_source)
    joints_pad = jnp.concatenate([blank, joints])
    joint_prev = lax.dynamic_index_in_dim(joints_pad, position, 0, keepdims=False)
    joint_own = lax.dynamic_index_in_dim(joints_pad, position + 1, 0, keepdims=False)
    inner = base_part + joint_prev * left_part + joint_own * right_part
    return jnp.concatenate([inner, joint_own[None]])


def gather_x(payload):
    return lax.all_gather(payload, "gx", axis=0, tiled=True)


def gather_y(payload):
    return lax.all_gather(payload, "gy", axis=0, tiled=True)


def body(phase_frac, phase_ids, conc, pair_class, mobility, drive, diffusivity):
    slot_count, width_x, width_y, width_z = phase_frac.shape
    count_x = lax.axis_size("gx")
    count_y = lax.axis_size("gy")
    classes = jnp.arange(mobility.shape[0], dtype=jnp.int32)
    mob_table = jnp.sum(jnp.where(pair_class[:, :, None] == classes, mobility, 0.0), axis=2)
    phase_list = jnp.arange(drive.shape[0], dtype=jnp.int32)
    one_hot = (phase_ids[:, None] == phase_list[None, :, None, None, None]).astype(jnp.float32)
    dense = jnp.sum(one_hot * phase_frac[:, None], axis=0)
    padded = with_halo(dense, (("gx", 1), ("gy", 2)), 1, True)
    neighbours = (
        padded[:, 2:, 1:-1]
        + padded[:, :-2, 1:-1]
        + (padded[:, 1:-1, 2:] + padded[:, 1:-1, :-2])
        + (jnp.roll(dense, -1, 3) + jnp.roll(dense, 1, 3))
    )
    lap_dense = neighbours - 6.0 * dense
    curvature = jnp.sum(one_hot * lap_dense[None], axis=1)
    drive_slot = jnp.sum(one_hot * drive[None, :, None, None, None], axis=1)
    diff_slot = jnp.sum(one_hot * diffusivity[None, :, None, None, None], axis=1)
    level = curvature + KAPPA * phase_frac
    pieces = []
    for slot_index in range(slot_count):
        mob_rows = jnp.einsum(
            "pq,pxyz->qxyz", mob_table, one_hot[slot_index], precision=lax.Precision.HIGHEST
        )
        pair_mob = jnp.sum(one_hot * mob_rows[None], axis=1)
        term = (
            level[slot_index]
            - level
            + DRIVE
            * phase_frac[slot_index]
            * phase_frac
            * (drive_slot[slot_index] - drive_slot)
            * conc
        )
        pieces.append(jnp.sum(pair_mob * term, axis=0))
    new_frac = phase_frac + jnp.stack(pieces)
    diffus = 1.0 + jnp.sum(new_frac * new_frac * diff_slot, axis=0)
    diff_pad, conc_pad = (
        with_halo(diffus, (("gx", 0), ("gy", 1)), 1, False),
        with_halo(conc, (("gx", 0), ("gy", 1)), 1, False),
    )
    pos_x = lax.axis_index("gx") * width_x + jnp.arange(width_x, dtype=jnp.int32)
    pos_y = lax.axis_index("gy") * width_y + jnp.arange(width_y, dtype=jnp.int32)
    apply_x, sub_x, main_x, super_x = side_parts(
        diff_pad[:, 1:-1], conc_pad[:, 1:-1], diffus, conc, pos_x[:, None, None], width_x * count_x
    )
    apply_yt, sub_y, main_y, super_y = side_parts(
        jnp.moveaxis(diff_pad[1:-1], 1, 0),
        jnp.moveaxis(conc_pad[1:-1], 1, 0),
        jnp.moveaxis(diffus, 1, 0),
        jnp.moveaxis(conc, 1, 0),
        pos_y[:, None, None],
        width_y * count_y,
    )
    apply_y = jnp.moveaxis(apply_yt, 0, 1)
    apply_zt, sub_z, main_z, super_z = line_parts(
        jnp.moveaxis(diffus, 2, 0), jnp.moveaxis(conc, 2, 0)
    )
    apply_z = jnp.moveaxis(apply_zt, 0, 2)
    batch_x = width_y * width_z
    source_x = (conc + apply_y + apply_z).reshape(width_x, batch_x)
    coeffs_x = (
        sub_x.reshape(width_x, batch_x),
        main_x.reshape(width_x, batch_x),
        super_x.reshape(width_x, batch_x),
    )
    section_x = partition(
        coeffs_x[0], coeffs_x[1], coeffs_x[2], source_x, gather_x, lax.axis_index("gx")
    )
    section_x = section_x.reshape(width_x, width_y, width_z)
    batch_y = width_x * width_z
    source_y = jnp.moveaxis(section_x - apply_y, 1, 0).reshape(width_y, batch_y)
    coeffs_y = (
        sub_y.reshape(width_y, batch_y),
        main_y.reshape(width_y, batch_y),
        super_y.reshape(width_y, batch_y),
    )
    section_y = partition(
        coeffs_y[0], coeffs_y[1], coeffs_y[2], source_y, gather_y, lax.axis_index("gy")
    )
    section_y = jnp.moveaxis(section_y.reshape(width_y, width_x, width_z), 0, 1)
    batch_z = width_x * width_y
    source_z = jnp.moveaxis(section_y - apply_z, 2, 0).reshape(width_z, batch_z)
    solved_z = thomas(
        sub_z.reshape(width_z, batch_z),
        main_z.reshape(width_z, batch_z),
        super_z.reshape(width_z, batch_z),
        source_z,
    )
    new_conc = jnp.moveaxis(solved_z.reshape(width_z, width_x, width_y), 0, 2)
    return (new_frac, new_conc)


def solution(mesh):
    placed = (
        P(None, "gx", "gy", None),
        P(None, "gx", "gy", None),
        P("gx", "gy", None),
        P(),
        P(),
        P(),
        P(),
    )
    return jax.shard_map(
        body,
        mesh=mesh,
        in_specs=placed,
        out_specs=(P(None, "gx", "gy", None), P("gx", "gy", None)),
        check_vma=False,
    )
```

profile of v0, /device:TPU:0, one launch (start us, length us, event | category | flops | bytes accessed | tf_op | source)
XLA Modules:
  0.0 167.9 jit_solution(1445376874611321396)
XLA Ops:
  0.6 2.9 %select_reduce_fusion.10 = f32[16,8,16,128]{3,0,2,1:T(8,128)S(1)} fusion(f32[8,8,16,128]{3,2,1,0:T(8,128)} %param.35, s32[8,8,16,128]{3,2,1,0:T(8,128)} %param.36), kind=kLoop, calls=%fused_computation.83 | loop fusion | flops 6029312 | bytes 2097152 | tf_op jit(solution)/shard_map/reduce_sum | solution.py:131
  3.6 0.7 fusion.112
  4.3 6.0 %collective-permute-start = (f32[16,1,16,128]{3,0,2,1:T(8,128)}, f32[16,1,16,128]{3,0,2,1:T(8,128)}, u32[]{:S(2)}, u32[]{:S(2)}) collective-permute-start(f32[16,1,16,128]{3,0,2,1:T(8,128)} %get-tuple-element.1362), channel_id=1, source_target_pairs={{4,0},{8,4},{12,8},{16,12},{20,16},{24,20},{28,24},{0,28},{5,1},{9... | collective-permute-start | bytes 393224 | tf_op jit(solution)/shard_map/ppermute | solution.py:20
  10.3 1.8 %collective-permute-start.8 = (f32[1,16,128]{2,1,0:T(8,128)S(1)}, f32[1,16,128]{2,1,0:T(8,128)S(1)}, u32[]{:S(2)}, u32[]{:S(2)}) collective-permute-start(f32[1,16,128]{2,1,0:T(8,128)S(1)} %get-tuple-element.1428), channel_id=1, source_target_pairs={{0,4},{4,8},{8,12},{12,16},{16,20},{20,24},{24,28},{1,5},{5,9},{9,... | collective-permute-start | bytes 24584 | tf_op jit(solution)/shard_map/ppermute | solution.py:18
  12.1 1.3 collective-permute-start.9
  13.4 1.7 %fusion.110 = (f32[16,8,16,1]{3,0,2,1:T(8,128)}, f32[16,8,16,1]{3,0,2,1:T(8,128)}) fusion(f32[16,8,16,128]{3,0,2,1:T(8,128)S(1)} %select_reduce_fusion.10), kind=kLoop, calls=%fused_computation.322 | loop fusion | bytes 32768 | tf_op jit(solution)/shard_map/jit(_roll_static)/slice | solution.py:137
  15.1 1.7 %fusion.111 = (f32[16,8,16,127]{3,0,2,1:T(8,128)}, f32[16,8,16,127]{3,0,2,1:T(8,128)}) fusion(f32[16,8,16,128]{3,0,2,1:T(8,128)S(1)} %select_reduce_fusion.10), kind=kLoop, calls=%fused_computation.323 | loop fusion | bytes 4161536 | tf_op jit(solution)/shard_map/jit(_roll_static)/slice | solution.py:137
  16.8 1.3 iota_compare_fusion
  18.3 0.6 fusion.35
  18.9 1.6 fusion.36
  20.5 1.6 fusion.37
  22.1 1.6 fusion.38
  23.7 1.6 fusion.39
  25.3 1.6 fusion.40
  27.0 1.6 fusion.41
  28.6 1.6 fusion.42
  30.2 0.8 multiply_bitcast_fusion.2
  31.0 0.5 fusion.97
  31.5 0.6 fusion.99
  32.2 1.4 collective-permute-start.10
  33.7 1.3 collective-permute-start.11
  35.0 0.8 pad_maximum_fusion.16
  35.9 2.9 %collective-permute-start.2 = (f32[16,10,1,128]{3,0,2,1:T(8,128)S(1)}, f32[16,10,1,128]{3,0,2,1:T(8,128)S(1)}, u32[]{:S(2)}, u32[]{:S(2)}) collective-permute-start(f32[16,10,1,128]{3,0,2,1:T(8,128)S(1)} %get-tuple-element.1351), channel_id=1, source_target_pairs={{1,0},{2,1},{3,2},{0,3},{5,4},{6,5},{7,6},{4,7},{9,8},{10,9},{11,1... | collective-permute-start | bytes 245768 | tf_op jit(solution)/shard_map/ppermute | solution.py:20
  38.8 0.3 collective-permute-start.3
  39.1 1.8 %collective-permute-done.2 = f32[16,10,1,128]{3,0,2,1:T(8,128)S(1)} collective-permute-done((f32[16,10,1,128]{3,0,2,1:T(8,128)S(1)}, f32[16,10,1,128]{3,0,2,1:T(8,128)S(1)}, u32[]{:S(2)}, u32[]{:S(2)}) %collective-permute-start.2) | collective-permute-done | bytes 81952 | tf_op jit(solution)/shard_map/ppermute | solution.py:20
  40.8 2.5 %collective-permute-done.3 = f32[16,10,1,128]{3,0,2,1:T(8,128)S(1)} collective-permute-done((f32[16,10,1,128]{3,0,2,1:T(8,128)S(1)}, f32[16,10,1,128]{3,0,2,1:T(8,128)S(1)}, u32[]{:S(2)}, u32[]{:S(2)}) %collective-permute-start.3) | collective-permute-done | bytes 81952 | tf_op jit(solution)/shard_map/ppermute | solution.py:18
  43.4 2.8 %fusion.33 = f32[16,8,16,128]{3,0,2,1:T(8,128)S(1)} fusion(f32[16,10,1,128]{3,0,2,1:T(8,128)S(1)} %collective-permute-done.3, f32[16,1,16,128]{3,0,2,1:T(8,128)} %collective-permute-done, f32[16,8,16,128]{3,0,2,1:T(8,128)S(1)} %select_reduce_fusion.10, f32[16,1,16,128]{3,0,2,1:T(8,128)} %collective-permute-done.1, ...), kind=kLoop, calls=%fused_computation.90 | loop fusion | flops 4456448 | bytes 4620288 | tf_op jit(solution)/shard_map/sub | solution.py:139
  46.3 0.3 copy-done.5
  46.6 0.3 copy-done.6
  46.9 0.3 copy-done.7
  47.2 20.2 %select_reduce_fusion = (f32[8,8,16,128]{3,2,1,0:T(8,128)S(1)}, f32[8,8,16,128]{3,2,1,0:T(8,128)S(1)}, f32[8,8,16,128]{3,2,1,0:T(8,128)S(1)}, f32[8,8,16,128]{3,...) fusion(f32[16]{0:T(128)S(1)} %copy-done.23, ...), kind=kLoop, calls=%fused_computation.73 | loop fusion | flops 46792704 | bytes 15728768 | tf_op jit(solution)/shard_map/reduce_sum | solution.py:142
  67.7 0.6 copy-done.17
  68.3 0.3 multiply_reduce_fusion.7
  68.7 0.5 multiply_reduce_fusion.4
  69.2 0.3 copy-done.12
  69.6 0.5 multiply_reduce_fusion.1
  70.1 0.9 multiply_reduce_fusion
  71.0 4.5 %collective-permute-start.4 = (f32[1,16,128]{2,1,0:T(8,128)S(1)}, f32[1,16,128]{2,1,0:T(8,128)S(1)}, u32[]{:S(2)}, u32[]{:S(2)}) collective-permute-start(f32[1,16,128]{2,1,0:T(8,128)S(1)} %get-tuple-element.1423), channel_id=1, source_target_pairs={{0,4},{4,8},{8,12},{12,16},{16,20},{20,24},{24,28},{1,5},{5,9},{9,... | collective-permute-start | bytes 24584 | tf_op jit(solution)/shard_map/ppermute | solution.py:18
  75.6 1.3 collective-permute-start.5
  77.4 3.7 %collective-permute-done.5 = f32[1,16,128]{2,1,0:T(8,128)S(1)} collective-permute-done((f32[1,16,128]{2,1,0:T(8,128)S(1)}, f32[1,16,128]{2,1,0:T(8,128)S(1)}, u32[]{:S(2)}, u32[]{:S(2)}) %collective-permute-start.5) | collective-permute-done | bytes 8224 | tf_op jit(solution)/shard_map/ppermute | solution.py:20
  81.3 1.3 collective-permute-start.6
  82.6 1.3 collective-permute-start.7
  84.1 3.0 %collective-permute-done.7 = f32[10,1,128]{2,1,0:T(1,128)S(1)} collective-permute-done((f32[10,1,128]{2,1,0:T(1,128)S(1)}, f32[10,1,128]{2,1,0:T(1,128)S(1)}, u32[]{:S(2)}, u32[]{:S(2)}) %collective-permute-start.7) | collective-permute-done | bytes 5152 | tf_op jit(solution)/shard_map/ppermute | solution.py:20
  87.5 0.8 while.174
  88.4 0.4 while.175
  89.2 34.8 %all-gather.2 = f32[8,10,2048]{2,1,0:T(8,128)S(1)} all-gather(f32[1,10,2048]{2,1,0:T(8,128)S(1)} %bitcast.508), channel_id=2, replica_groups=mesh['gx'=8,'gy'=4] {'gx'}, dimensions={0}, use_global_device_ids=true | all-gather | bytes 737280 | tf_op jit(solution)/shard_map/all_gather | solution.py:116
  124.0 0.4 fusion.51
  124.6 4.1 %while.176 = (s32[]{:T(128)}, f32[2048]{0:T(1024)S(1)}, f32[2048]{0:T(1024)S(1)}, f32[8,2048]{1,0:T(8,128)S(1)}, f32[8,2048]{1,0:T(8,128)S(1)}, /*index=5*/f32[8...) while((s32[]{:T(128)}, f32[2048]{0:T(1024)S(1)}, ...), condition=%wide.region_27.28_spmd.clone, body=%wide.region_26.27_spmd.clone.sunk | while | flops 16387 | bytes 163975 | solution.py:41
  128.7 2.2 %while.177 = (s32[]{:T(128)}, f32[2048]{0:T(1024)S(1)}, f32[8,2048]{1,0:T(8,128)S(1)}, f32[8,2048]{1,0:T(8,128)S(1)}, f32[8,2048]{1,0:T(8,128)S(1)}, /*index=5*/s32[]{:T(128)}, s32[]{:T(128)}, s32[]{:T(128)}) while((s32[]{:T(128)}, f32[2048]{0:T(1024)S(1)}, f32[8,2048]{1,0:T(8,128)S(1)}, f32[8,2048]{1,0:T(8,128)S(1)}, ...), condition=%wide.region_29.30_spmd.clone, body=%wide.region_28.29_spmd.clone.sunk | while | flops 6148 | bytes 82035 | solution.py:50
  128.8 0.2 dynamic_update_slice.118
  129.0 0.2 dynamic_update_slice.118
  129.3 0.2 dynamic_update_slice.118
  129.6 0.2 dynamic_update_slice.118
  129.9 0.2 dynamic_update_slice.118
  130.4 0.2 dynamic_update_slice.118
  130.7 0.2 dynamic_update_slice.118
  131.7 1.3 while.178
  133.0 0.7 while.179
  134.0 6.8 %all-gather.3 = f32[4,10,1024]{2,1,0:T(8,128)S(1)} all-gather(f32[1,10,1024]{2,1,0:T(8,128)S(1)} %bitcast.523), channel_id=3, replica_groups=mesh['gx'=8,'gy'=4] {'gy'}, dimensions={0}, use_global_device_ids=true | all-gather | bytes 204800 | tf_op jit(solution)/shard_map/all_gather | solution.py:120
  141.1 1.0 while.180
  142.0 0.5 while.181
  142.9 14.6 %while.182 = (s32[]{:T(128)}, f32[128]{0:T(128)S(1)}, f32[128]{0:T(128)S(1)}, f32[128,128]{1,0:T(8,128)S(1)}, f32[128,128]{1,0:T(8,128)S(1)}, /*index=5*/f32[128...) while((s32[]{:T(128)}, f32[128]{0:T(128)S(1)}, ...), condition=%wide.region_39.40_spmd.clone, body=%wide.region_38.39_spmd.clone.sunk | while | flops 1027 | bytes 6275 | solution.py:41
  157.6 9.6 %while.183 = (s32[]{:T(128)}, f32[128]{0:T(128)S(1)}, f32[128,128]{1,0:T(8,128)S(1)}, f32[128,128]{1,0:T(8,128)S(1)}, f32[128,128]{1,0:T(8,128)S(1)}, /*index=5*/s32[]{:T(128)}, s32[]{:T(128)}, s32[]{:T(128)}) while((s32[]{:T(128)}, f32[128]{0:T(128)S(1)}, f32[128,128]{1,0:T(8,128)S(1)}, f32[128,128]{1,0:T(8,128)S(1)}, ...), condition=%wide.region_41.42_spmd.clone, body=%wide.region_40.41_spmd.clone.sunk | while | flops 388 | bytes 3187 | solution.py:50
  167.2 0.7 copy.101
  (985 shorter events, 30.4 us)
Async XLA Ops:
  0.6 9.6 %copy-start.10 = (f32[8,16,128]{2,1,0:T(8,128)S(1)}, f32[8,16,128]{2,1,0:T(8,128)}, u32[]{:S(2)}) copy-start(f32[8,16,128]{2,1,0:T(8,128)} %param.37) | copy-start | bytes 196612
  4.3 30.7 %collective-permute-start = (f32[16,1,16,128]{3,0,2,1:T(8,128)}, f32[16,1,16,128]{3,0,2,1:T(8,128)}, u32[]{:S(2)}, u32[]{:S(2)}) collective-permute-start(f32[16,1,16,128]{3,0,2,1:T(8,128)} %get-tuple-element.1362), channel_id=1, source_target_pairs={{4,0},{8,4},{12,8},{16,12},{20,16},{24,20},{28,24},{0,28},{5,1},{9... | collective-permute-start | bytes 393224 | tf_op jit(solution)/shard_map/ppermute | solution.py:20
  10.3 24.7 %collective-permute-start.1 = (f32[16,1,16,128]{3,0,2,1:T(8,128)}, f32[16,1,16,128]{3,0,2,1:T(8,128)}, u32[]{:S(2)}, u32[]{:S(2)}) collective-permute-start(f32[16,1,16,128]{3,0,2,1:T(8,128)} %get-tuple-element.1361), channel_id=1, source_target_pairs={{0,4},{4,8},{8,12},{12,16},{16,20},{20,24},{24,28},{28,0},{1,5},{5... | collective-permute-start | bytes 393224 | tf_op jit(solution)/shard_map/ppermute | solution.py:18
  10.3 21.9 %collective-permute-start.8 = (f32[1,16,128]{2,1,0:T(8,128)S(1)}, f32[1,16,128]{2,1,0:T(8,128)S(1)}, u32[]{:S(2)}, u32[]{:S(2)}) collective-permute-start(f32[1,16,128]{2,1,0:T(8,128)S(1)} %get-tuple-element.1428), channel_id=1, source_target_pairs={{0,4},{4,8},{8,12},{12,16},{16,20},{20,24},{24,28},{1,5},{5,9},{9,... | collective-permute-start | bytes 24584 | tf_op jit(solution)/shard_map/ppermute | solution.py:18
  12.1 20.1 %collective-permute-start.9 = (f32[1,16,128]{2,1,0:T(8,128)S(1)}, f32[1,16,128]{2,1,0:T(8,128)S(1)}, u32[]{:S(2)}, u32[]{:S(2)}) collective-permute-start(f32[1,16,128]{2,1,0:T(8,128)S(1)} %get-tuple-element.1427), channel_id=1, source_target_pairs={{4,0},{8,4},{12,8},{16,12},{20,16},{24,20},{28,24},{5,1},{9,5},{13... | collective-permute-start | bytes 24584 | tf_op jit(solution)/shard_map/ppermute | solution.py:20
  15.1 1.7 %copy-start.1 = (s32[8,8,16,128]{3,2,1,0:T(8,128)S(1)}, s32[8,8,16,128]{3,2,1,0:T(8,128)}, u32[]{:S(2)}) copy-start(s32[8,8,16,128]{3,2,1,0:T(8,128)} %param.36) | copy-start | bytes 1572868
  16.8 1.4 copy-start.22
  16.8 1.4 copy-start.27
  25.3 4.9 %copy-start = (f32[8,8,16,128]{3,2,1,0:T(8,128)S(1)}, f32[8,8,16,128]{3,2,1,0:T(8,128)}, u32[]{:S(2)}) copy-start(f32[8,8,16,128]{3,2,1,0:T(8,128)} %param.35) | copy-start | bytes 1572868
  32.2 11.2 %copy-start.9 = (f32[16,8,16,1]{3,0,2,1:T(8,128)S(1)}, f32[16,8,16,1]{3,0,2,1:T(8,128)}, u32[]{:S(2)}) copy-start(f32[16,8,16,1]{3,0,2,1:T(8,128)} %get-tuple-element.1357) | copy-start | bytes 24580
  32.2 6.8 %collective-permute-start.10 = (f32[10,1,128]{2,1,0:T(1,128)S(1)}, f32[10,1,128]{2,1,0:T(1,128)S(1)}, u32[]{:S(2)}, u32[]{:S(2)}) collective-permute-start(f32[10,1,128]{2,1,0:T(1,128)S(1)} %get-tuple-element.1405), channel_id=1, source_target_pairs={{0,1},{1,2},{2,3},{4,5},{5,6},{6,7},{8,9},{9,10},{10,11},{12,13},{... | collective-permute-start | bytes 15368 | tf_op jit(solution)/shard_map/ppermute | solution.py:18
  33.7 5.4 %collective-permute-start.11 = (f32[10,1,128]{2,1,0:T(1,128)S(1)}, f32[10,1,128]{2,1,0:T(1,128)S(1)}, u32[]{:S(2)}, u32[]{:S(2)}) collective-permute-start(f32[10,1,128]{2,1,0:T(1,128)S(1)} %get-tuple-element.1406), channel_id=1, source_target_pairs={{1,0},{2,1},{3,2},{5,4},{6,5},{7,6},{9,8},{10,9},{11,10},{13,12},{... | collective-permute-start | bytes 15368 | tf_op jit(solution)/shard_map/ppermute | solution.py:20
  35.0 11.2 %copy-start.8 = (f32[16,8,16,128]{3,0,2,1:T(8,128)S(1)}, f32[16,8,16,128]{3,0,2,1:T(8,128)}, u32[]{:S(2)}) copy-start(f32[16,8,16,128]{3,0,2,1:T(8,128)} %fusion.42) | copy-start | bytes 3145732
  35.9 5.0 %collective-permute-start.2 = (f32[16,10,1,128]{3,0,2,1:T(8,128)S(1)}, f32[16,10,1,128]{3,0,2,1:T(8,128)S(1)}, u32[]{:S(2)}, u32[]{:S(2)}) collective-permute-start(f32[16,10,1,128]{3,0,2,1:T(8,128)S(1)} %get-tuple-element.1351), channel_id=1, source_target_pairs={{1,0},{2,1},{3,2},{0,3},{5,4},{6,5},{7,6},{4,7},{9,8},{10,9},{11,1... | collective-permute-start | bytes 245768 | tf_op jit(solution)/shard_map/ppermute | solution.py:20
  38.8 4.6 %collective-permute-start.3 = (f32[16,10,1,128]{3,0,2,1:T(8,128)S(1)}, f32[16,10,1,128]{3,0,2,1:T(8,128)S(1)}, u32[]{:S(2)}, u32[]{:S(2)}) collective-permute-start(f32[16,10,1,128]{3,0,2,1:T(8,128)S(1)} %get-tuple-element.1352), channel_id=1, source_target_pairs={{0,1},{1,2},{2,3},{3,0},{4,5},{5,6},{6,7},{7,4},{8,9},{9,10},{10,1... | collective-permute-start | bytes 245768 | tf_op jit(solution)/shard_map/ppermute | solution.py:18
  43.3 2.9 %copy-start.2 = (f32[16,8,16,128]{3,0,2,1:T(8,128)S(1)}, f32[16,8,16,128]{3,0,2,1:T(8,128)}, u32[]{:S(2)}) copy-start(f32[16,8,16,128]{3,0,2,1:T(8,128)} %fusion.36) | copy-start | bytes 3145732
  43.3 2.9 %copy-start.3 = (f32[16,8,16,128]{3,0,2,1:T(8,128)S(1)}, f32[16,8,16,128]{3,0,2,1:T(8,128)}, u32[]{:S(2)}) copy-start(f32[16,8,16,128]{3,0,2,1:T(8,128)} %fusion.37) | copy-start | bytes 3145732
  43.3 2.9 %copy-start.4 = (f32[16,8,16,128]{3,0,2,1:T(8,128)S(1)}, f32[16,8,16,128]{3,0,2,1:T(8,128)}, u32[]{:S(2)}) copy-start(f32[16,8,16,128]{3,0,2,1:T(8,128)} %fusion.38) | copy-start | bytes 3145732
  43.4 3.2 %copy-start.5 = (f32[16,8,16,128]{3,0,2,1:T(8,128)S(1)}, f32[16,8,16,128]{3,0,2,1:T(8,128)}, u32[]{:S(2)}) copy-start(f32[16,8,16,128]{3,0,2,1:T(8,128)} %fusion.39) | copy-start | bytes 3145732
  43.4 3.5 %copy-start.6 = (f32[16,8,16,128]{3,0,2,1:T(8,128)S(1)}, f32[16,8,16,128]{3,0,2,1:T(8,128)}, u32[]{:S(2)}) copy-start(f32[16,8,16,128]{3,0,2,1:T(8,128)} %fusion.40) | copy-start | bytes 3145732
  43.4 3.8 %copy-start.7 = (f32[16,8,16,128]{3,0,2,1:T(8,128)S(1)}, f32[16,8,16,128]{3,0,2,1:T(8,128)}, u32[]{:S(2)}) copy-start(f32[16,8,16,128]{3,0,2,1:T(8,128)} %fusion.41) | copy-start | bytes 3145732
  43.4 3.8 %copy-start.23 = (f32[16]{0:T(128)S(1)}, f32[16]{0:T(128)}, u32[]{:S(2)}) copy-start(f32[16]{0:T(128)} %param.41) | copy-start | bytes 196
  43.4 3.8 %copy-start.24 = (f32[16]{0:T(128)S(1)}, f32[16]{0:T(128)}, u32[]{:S(2)}) copy-start(f32[16]{0:T(128)} %param.40) | copy-start | bytes 196
  67.4 0.8 copy-start.17
  67.5 0.9 copy-start.18
  67.6 1.0 copy-start.14
  67.6 1.0 copy-start.15
  67.6 1.0 copy-start.16
  68.7 0.8 copy-start.12
  68.7 0.9 copy-start.13
  70.0 11.1 %copy-start.25 = (pred[8]{0:T(512)(128)(4,1)S(1)}, pred[8]{0:T(512)(128)(4,1)}, u32[]{:S(2)}) copy-start(pred[8]{0:T(512)(128)(4,1)} %get-tuple-element.1444) | copy-start | bytes 28
  70.0 11.1 %copy-start.26 = (pred[8]{0:T(512)(128)(4,1)S(1)}, pred[8]{0:T(512)(128)(4,1)}, u32[]{:S(2)}) copy-start(pred[8]{0:T(512)(128)(4,1)} %get-tuple-element.1445) | copy-start | bytes 28
  70.1 17.0 %copy-start.28 = (pred[16]{0:T(512)(128)(4,1)S(1)}, pred[16]{0:T(512)(128)(4,1)}, u32[]{:S(2)}) copy-start(pred[16]{0:T(512)(128)(4,1)} %get-tuple-element.1442) | copy-start | bytes 52
  70.1 17.0 %copy-start.29 = (pred[16]{0:T(512)(128)(4,1)S(1)}, pred[16]{0:T(512)(128)(4,1)}, u32[]{:S(2)}) copy-start(pred[16]{0:T(512)(128)(4,1)} %get-tuple-element.1443) | copy-start | bytes 52
  71.0 6.4 %collective-permute-start.4 = (f32[1,16,128]{2,1,0:T(8,128)S(1)}, f32[1,16,128]{2,1,0:T(8,128)S(1)}, u32[]{:S(2)}, u32[]{:S(2)}) collective-permute-start(f32[1,16,128]{2,1,0:T(8,128)S(1)} %get-tuple-element.1423), channel_id=1, source_target_pairs={{0,4},{4,8},{8,12},{12,16},{16,20},{20,24},{24,28},{1,5},{5,9},{9,... | collective-permute-start | bytes 24584 | tf_op jit(solution)/shard_map/ppermute | solution.py:18
  75.6 5.5 %collective-permute-start.5 = (f32[1,16,128]{2,1,0:T(8,128)S(1)}, f32[1,16,128]{2,1,0:T(8,128)S(1)}, u32[]{:S(2)}, u32[]{:S(2)}) collective-permute-start(f32[1,16,128]{2,1,0:T(8,128)S(1)} %get-tuple-element.1424), channel_id=1, source_target_pairs={{4,0},{8,4},{12,8},{16,12},{20,16},{24,20},{28,24},{5,1},{9,5},{13... | collective-permute-start | bytes 24584 | tf_op jit(solution)/shard_map/ppermute | solution.py:20
  81.3 2.8 %collective-permute-start.6 = (f32[10,1,128]{2,1,0:T(1,128)S(1)}, f32[10,1,128]{2,1,0:T(1,128)S(1)}, u32[]{:S(2)}, u32[]{:S(2)}) collective-permute-start(f32[10,1,128]{2,1,0:T(1,128)S(1)} %get-tuple-element.1403), channel_id=1, source_target_pairs={{0,1},{1,2},{2,3},{4,5},{5,6},{6,7},{8,9},{9,10},{10,11},{12,13},{... | collective-permute-start | bytes 15368 | tf_op jit(solution)/shard_map/ppermute | solution.py:18
  82.6 4.5 %collective-permute-start.7 = (f32[10,1,128]{2,1,0:T(1,128)S(1)}, f32[10,1,128]{2,1,0:T(1,128)S(1)}, u32[]{:S(2)}, u32[]{:S(2)}) collective-permute-start(f32[10,1,128]{2,1,0:T(1,128)S(1)} %get-tuple-element.1404), channel_id=1, source_target_pairs={{1,0},{2,1},{3,2},{5,4},{6,5},{7,6},{9,8},{10,9},{11,10},{13,12},{... | collective-permute-start | bytes 15368 | tf_op jit(solution)/shard_map/ppermute | solution.py:20
  131.6 9.5 %copy-start.11 = (f32[1024]{0:T(1024)S(1)}, f32[1024]{0:T(1024)}, u32[]{:S(2)}) copy-start(f32[1024]{0:T(1024)} %custom-call.9) | copy-start | bytes 12292
  133.0 9.9 %copy-start.19 = (f32[128]{0:T(128)S(1)}, f32[128]{0:T(128)}, u32[]{:S(2)}) copy-start(f32[128]{0:T(128)} %custom-call.12) | copy-start | bytes 1540
  133.0 9.9 %copy-start.20 = (f32[128]{0:T(128)S(1)}, f32[128]{0:T(128)}, u32[]{:S(2)}) copy-start(f32[128]{0:T(128)} %custom-call.13) | copy-start | bytes 1540
  133.0 24.5 %copy-start.21 = (f32[128]{0:T(128)S(1)}, f32[128]{0:T(128)}, u32[]{:S(2)}) copy-start(f32[128]{0:T(128)} %custom-call.14) | copy-start | bytes 1540
where the time goes:
time: 168 us
  blocking collectives  41.7 us (25%)
  other arithmetic  40.5 us (24%)
  local copies, waits for them, and re-layouts  30.7 us (18%)
  starting transfers between devices  23.4 us (14%)
  matrix products  11.9 us (7%)
  waiting for transfers between devices  11 us (7%)
  loops' own time  6.73 us (4%)
  between operations  2.05 us (1%)
    all_gather x1, blocking collectives, gather_x(): return lax.all_gather(payload, 'gx', axis=0, tiled=True)  34.8 us
    dynamic_update_slice x420, local copies, waits for them, and re-layouts, thomas(): lax.scan(forward, (anchor, anchor), (sub_diag, main_diag, super_diag, rhs...  20.5 us
    reduce_sum x1, other arithmetic, body(): jnp.sum(one_hot * diffusivity[None, :, None, None, None], axis=1)  20.2 us
    ppermute x6, starting transfers between devices, with_halo(): lax.ppermute(head, axis, [((i + 1) % count, i) for i in range(ends)])  14.1 us
    dot_general x8, matrix products, body(): jnp.einsum('pq,pxyz->qxyz', mob_table, one_hot[slot_index], precision=lax...  11.9 us
    ppermute x6, starting transfers between devices, with_halo(): lax.ppermute(tail, axis, [(i, (i + 1) % count) for i in range(ends)])  9.29 us
    ppermute x6, waiting for transfers between devices, with_halo(): lax.ppermute(head, axis, [((i + 1) % count, i) for i in range(ends)])  8.52 us
    all_gather x1, blocking collectives, gather_y(): return lax.all_gather(payload, 'gy', axis=0, tiled=True)  6.85 us
  transfers between devices with their start and end apart: 12, of which 4 were waited for; matrix products, arithmetic and copies ran while one was open for 12% of the time, Pallas kernels for 0%

commit v1 on v0

v1 whole, which is shorter than its diff:
```python
import functools

import jax
import jax.numpy as jnp
from jax import lax
from jax.experimental import pallas as pl
from jax.experimental.pallas import tpu as pltpu
from jax.sharding import PartitionSpec as P

KAPPA = 2.0
DRIVE = 4.0
SUB = 8

VMEM = pl.BlockSpec(memory_space=pltpu.VMEM)
SMEM = pl.BlockSpec(memory_space=pltpu.SMEM)


def call(kernel, name, outs, ins, scratch=(), aliases={}, cost=20000, scalars=()):
    f32 = jnp.float32
    return pl.pallas_call(
        kernel,
        name=name,
        out_shape=[jax.ShapeDtypeStruct(s, f32) for s in outs],
        in_specs=[SMEM if i in scalars else VMEM for i in range(len(ins))],
        out_specs=[VMEM] * len(outs),
        scratch_shapes=[pltpu.VMEM(s, f32) for s in scratch],
        input_output_aliases=aliases,
        compiler_params=pltpu.CompilerParams(vmem_limit_bytes=12 << 20),
        cost_estimate=pl.CostEstimate(flops=cost * 1000, bytes_accessed=1 << 20, transcendentals=0),
    )(*ins)


def lookup(table, index):
    dims = lax.GatherDimensionNumbers(
        offset_dims=(),
        collapsed_slice_dims=(1,),
        start_index_map=(1,),
        operand_batching_dims=(0,),
        start_indices_batching_dims=(0,),
    )
    return lax.gather(
        table, index[..., None], dims, (1, 1), mode=lax.GatherScatterMode.PROMISE_IN_BOUNDS
    )


def scalar_table(ref, shape):
    lane = lax.broadcasted_iota(jnp.int32, shape, 1)
    table = jnp.zeros(shape, jnp.float32)
    for k in range(ref.shape[0]):
        table = jnp.where(lane == k, ref[k], table)
    return table


def even(axis):
    return lax.rem(lax.axis_index(axis), 2) == 0


def pick_rows(ids, fields, count):
    rows = []
    for phase in range(count):
        total = jnp.zeros(fields[0].shape, jnp.float32)
        for slot_id, field in zip(ids, fields):
            total = jnp.where(slot_id == phase, field, total)
        rows.append(total)
    return rows


def pick_slots(ids, rows):
    picked = [jnp.zeros(ids[0].shape, jnp.float32) for _ in ids]
    for phase, row in enumerate(rows):
        picked = [jnp.where(i == phase, row, t) for i, t in zip(ids, picked)]
    return picked


def exchange(level, ids, tables, phases, source=None):
    width = tables.shape[1]
    per_row = width // phases
    count = tables.shape[0] // SUB
    lane_of = [lax.rem(i, per_row) * phases if per_row & (per_row - 1) else (i & (per_row - 1)) * phases for i in ids]
    sums = [jnp.zeros(level[0].shape, jnp.float32) for _ in level]
    for a in range(len(level)):
        above = [ids[a] >= t * per_row for t in range(1, count)]
        for b in range(a + 1, len(level)):
            index = lane_of[a] + ids[b]
            mob = lookup(tables[0:SUB], index)
            for t in range(1, count):
                mob = jnp.where(above[t - 1], lookup(tables[t * SUB : (t + 1) * SUB], index), mob)
            term = level[a] - level[b]
            if source is not None:
                frac, drive, conc = source
                term = term + (conc * frac[a]) * (frac[b] * (drive[a] - drive[b]))
            term = mob * term
            sums[a] = sums[a] + term
            sums[b] = sums[b] - term
    return sums


def faces_kernel(phases, shape, frac, ids, conc, x_a, x_b, y_a, y_b):
    nx, ny, _ = shape
    slots = frac.shape[0]
    right = even("gx")
    for out, upper in ((x_a, right), (x_b, jnp.logical_not(right))):
        base = jnp.where(upper, (nx - 1) * ny, 0)
        for part in range(ny // SUB):
            rows = pl.ds(pl.multiple_of(base + part * SUB, SUB), SUB)
            held = pick_rows(
                [ids[s, rows, :] for s in range(slots)],
                [frac[s, rows, :] for s in range(slots)],
                phases,
            )
            for phase in range(phases):
                out[phase, part * SUB : (part + 1) * SUB, :] = held[phase]
    up = even("gy")
    for out, upper in ((y_a, up), (y_b, jnp.logical_not(up))):
        rows = pl.ds(jnp.where(upper, ny - 1, 0), nx, stride=ny)
        held = pick_rows(
            [ids[s, rows, :] for s in range(slots)],
            [frac[s, rows, :] for s in range(slots)],
            phases,
        )
        for phase in range(phases):
            out[phase] = held[phase]
        out[phases] = conc[rows, :]


def interior_kernel(
    phases, shape, frac, ids, conc, pair_class, mobility, drive, diffusivity,
    new_out, diff_out, table_out, dense,
):
    nx, ny, nz = shape
    slots = frac.shape[0]
    pitch = ny + 2 * SUB
    parts = ny // SUB
    per_row = nz // phases
    count = -(-phases // per_row)
    lane = lax.broadcasted_iota(jnp.int32, (per_row, nz), 1)
    row = lax.broadcasted_iota(jnp.int32, (per_row, nz), 0)
    for t in range(count):
        block = pair_class[t * per_row : (t + 1) * per_row, :]
        wide = jnp.concatenate([block] * per_row, axis=1)
        values = jnp.zeros(wide.shape, jnp.float32)
        for k in range(mobility.shape[0]):
            values = jnp.where(wide == k, mobility[k], values)
        line = jnp.sum(
            jnp.where((lane >= row * phases) & (lane < (row + 1) * phases), values, 0.0),
            axis=0,
            keepdims=True,
        )
        table_out[t * SUB : (t + 1) * SUB, :] = jnp.broadcast_to(line, (SUB, nz))
    drive_table = scalar_table(drive, (SUB, nz))
    diff_table = scalar_table(diffusivity, (SUB, nz))
    nothing = jnp.zeros((SUB, nz), jnp.float32)

    def clear(phase, carry):
        for plane in range(nx + 2):
            for part in range(parts + 2):
                if plane in (0, nx + 1) or part in (0, parts + 1):
                    dense[phase, plane * pitch + part * SUB : plane * pitch + (part + 1) * SUB, :] = nothing
        return carry

    lax.fori_loop(0, phases, clear, 0)

    def build(x, carry):
        for part in range(parts):
            rows = pl.ds(pl.multiple_of(x * ny, SUB) + part * SUB, SUB)
            held = pick_rows(
                [ids[s, rows, :] for s in range(slots)],
                [frac[s, rows, :] for s in range(slots)],
                phases,
            )
            into = pl.ds(pl.multiple_of((x + 1) * pitch, SUB) + (part + 1) * SUB, SUB)
            for phase in range(phases):
                dense[phase, into, :] = held[phase]
        return carry

    lax.fori_loop(0, nx, build, 0)

    def update(x, carry):
        for part in range(parts):
            rows = pl.ds(pl.multiple_of(x * ny, SUB) + part * SUB, SUB)
            at = pl.multiple_of((x + 1) * pitch, SUB) + (part + 1) * SUB

            def laplacian():
                for phase in range(phases):
                    centre = dense[phase, pl.ds(at, SUB), :]
                    along_x = dense[phase, pl.ds(at + pitch, SUB), :] + dense[phase, pl.ds(at - pitch, SUB), :]
                    along_y = dense[phase, pl.ds(at + 1, SUB), :] + dense[phase, pl.ds(at - 1, SUB), :]
                    along_z = pltpu.roll(centre, nz - 1, 1) + pltpu.roll(centre, 1, 1)
                    yield (along_x + along_y + along_z) - 6.0 * centre

            slot_ids = [ids[s, rows, :] for s in range(slots)]
            curvature = pick_slots(slot_ids, laplacian())
            slot_frac = [frac[s, rows, :] for s in range(slots)]
            level = [c + KAPPA * f for c, f in zip(curvature, slot_frac)]
            slot_drive = [lookup(drive_table, i) for i in slot_ids]
            sums = exchange(
                level, slot_ids, table_out, phases, (slot_frac, slot_drive, DRIVE * conc[rows, :])
            )
            diffus = jnp.ones((SUB, nz), jnp.float32)
            for s in range(slots):
                new = slot_frac[s] + sums[s]
                new_out[s, rows, :] = new
                diffus = diffus + new * new * lookup(diff_table, slot_ids[s])
            diff_out[rows, :] = diffus
        return carry

    lax.fori_loop(0, nx, update, 0)


def outer_kernel(
    phases, shape, new_in, diff_in, table, ids, x_a, x_b, y_a, y_b, diffusivity,
    new_out, diff_out, face_a, face_b,
):
    nx, ny, nz = shape
    slots = new_in.shape[0]
    diff_table = scalar_table(diffusivity, (SUB, nz))
    new_out[...] = new_in[...]
    diff_out[...] = diff_in[...]

    def add(rows, halo):
        slot_ids = [ids[s, rows, :] for s in range(slots)]
        level = pick_slots(slot_ids, (halo(p) for p in range(phases)))
        sums = exchange(level, slot_ids, table, phases)
        diffus = jnp.ones(sums[0].shape, jnp.float32)
        for s in range(slots):
            new = new_out[s, rows, :] + sums[s]
            new_out[s, rows, :] = new
            diffus = diffus + new * new * lookup(diff_table, slot_ids[s])
        diff_out[rows, :] = diffus
        return diffus

    right = even("gx")
    for halo, upper in ((x_a, right), (x_b, jnp.logical_not(right))):
        base = jnp.where(upper, (nx - 1) * ny, 0)
        for part in range(ny // SUB):
            add(
                pl.ds(pl.multiple_of(base + part * SUB, SUB), SUB),
                lambda p, halo=halo, part=part: halo[p, part * SUB : (part + 1) * SUB, :],
            )
    up = even("gy")
    for halo, upper, face in ((y_a, up, face_a), (y_b, jnp.logical_not(up), face_b)):
        rows = pl.ds(jnp.where(upper, ny - 1, 0), nx, stride=ny)
        face[...] = add(rows, lambda p, halo=halo: halo[p])


def chain_ends(source, face):
    one = jnp.ones_like(source[0])

    def sweep(values, faces):
        mass, total, through = one, values[0], one
        for value, f in zip(values[1:], faces):
            share = f / (mass + f)
            total = value + share * total
            mass = 1.0 + share * mass
            through = share * through
        unit = 1.0 / mass
        return total * unit, unit, through * unit

    last, g_last, g_through = sweep(source, face)
    first, g_first, _ = sweep(source[::-1], face[::-1])
    return first, last, g_first, g_through, g_last


def join(left, right):
    first_a, last_a, gff_a, gfl_a, gll_a, d_first, d_last = left
    first_b, last_b, gff_b, gfl_b, gll_b, d_next, d_end = right
    face = 0.5 * (d_last + d_next)
    link = face / (1.0 + face * (gll_a + gff_b))
    flux = link * (first_b - last_a)
    return (
        first_a + flux * gfl_a,
        last_b - flux * gfl_b,
        gff_a - link * gfl_a * gfl_a,
        gfl_a * link * gfl_b,
        gll_b - link * gfl_b * gfl_b,
        d_first,
        d_end,
    )


def fluxes(blocks, flux_left, flux_right):
    count = len(blocks)
    views_left = []
    first, last, gff, gfl, gll, _, d_last = blocks[0]
    view = (last - flux_left * gfl, gll, d_last)
    for m in range(count - 1):
        views_left.append(view)
        if m + 1 < count - 1:
            first, last, gff, gfl, gll, d_first, d_last = blocks[m + 1]
            face = 0.5 * (view[2] + d_first)
            link = face / (1.0 + face * (view[1] + gff))
            flux = link * (first - view[0])
            view = (last - flux * gfl, gll - link * gfl * gfl, d_last)
    views_right = []
    first, last, gff, gfl, gll, d_first, _ = blocks[-1]
    view = (first + flux_right * gfl, gff, d_first)
    for m in range(count - 1, 0, -1):
        views_right.append(view)
        if m - 1 > 0:
            first, last, gff, gfl, gll, d_first, d_last = blocks[m - 1]
            face = 0.5 * (d_last + view[2])
            link = face / (1.0 + face * (gll + view[1]))
            flux = link * (view[0] - last)
            view = (first + flux * gfl, gff - link * gfl * gfl, d_first)
    views_right = views_right[::-1]
    inner = []
    for left, right in zip(views_left, views_right):
        face = 0.5 * (left[2] + right[2])
        inner.append(face * (right[0] - left[0]) / (1.0 + face * (left[1] + right[1])))
    return [flux_left] + inner + [flux_right]


def choose(options, number):
    out = options[0]
    for k in range(1, len(options)):
        out = jnp.where(number == k, options[k], out)
    return out


def members(axis, level, refs):
    stride, radix = level
    own = lax.rem(lax.axis_index(axis) // stride, radix)
    blocks = []
    for m in range(radix):
        number = own ^ m
        blocks.append(tuple(choose([r[q] for r in refs], number) for q in range(7)))
    return own, blocks


def solve_levels(axis, levels, refs):
    position = 0
    groups = []
    for level in levels:
        groups.append(members(axis, level, refs[position : position + level[1]]))
        position += level[1]
    zero = jnp.zeros(refs[0].shape[1:], jnp.float32)
    lower, upper = zero, zero
    for own, blocks in groups[::-1]:
        between = fluxes(blocks, lower, upper)
        lower, upper = choose(between[:-1], own), choose(between[1:], own)
    return lower, upper


def join_kernel(axis, level, *refs):
    out = refs[-1]
    _, blocks = members(axis, level, refs[:-1])
    total = blocks[0]
    for block in blocks[1:]:
        total = join(total, block)
    for q in range(7):
        out[q] = total[q]


def gather_levels(axis, payload, shape):
    count = lax.axis_size(axis)
    levels, refs = [], []
    stride = 1
    while stride < count:
        radix = 2
        level = (stride, radix)
        group = [payload]
        for k in range(1, radix):
            pairs = [(i, i ^ (k * stride)) for i in range(count)]
            group.append(lax.ppermute(payload, axis, pairs))
        levels.append(level)
        refs += group
        stride *= radix
        if stride < count:
            (payload,) = call(
                functools.partial(join_kernel, axis, level), "join_" + axis, [shape], group
            )
    return levels, refs


def flux_x_kernel(shape, diff, conc, y_a, y_b, halo_a, halo_b, payload, source, applied):
    nx, ny, nz = shape
    up = even("gy")
    place = lax.axis_index("gy")
    count = lax.axis_size("gy")
    last = y_a.shape[0] - 1

    def side(a, b, flag):
        return jnp.where(jnp.full((nx, nz), flag.astype(jnp.int32)) == 1, a, b)

    has_low = jnp.where(place > 0, 0.5, 0.0)
    has_high = jnp.where(place < count - 1, 0.5, 0.0)
    d_low = side(halo_b[...], halo_a[...], up)
    d_high = side(halo_a[...], halo_b[...], up)
    c_low = side(y_b[last], y_a[last], up)
    c_high = side(y_a[last], y_b[last], up)
    d_prev, c_prev = diff[pl.ds(0, nx, stride=ny), :], conc[pl.ds(0, nx, stride=ny), :]
    below = has_low * (d_low + d_prev) * (c_prev - c_low)
    for y in range(ny):
        if y + 1 < ny:
            d_next, c_next = diff[pl.ds(y + 1, nx, stride=ny), :], conc[pl.ds(y + 1, nx, stride=ny), :]
            above = 0.5 * (d_prev + d_next) * (c_next - c_prev)
        else:
            d_next, c_next = d_high, c_high
            above = has_high * (d_prev + d_next) * (c_next - c_prev)
        applied[pl.ds(y, nx, stride=ny), :] = above - below
        d_prev, c_prev, below = d_next, c_next, above

    inside = lax.broadcasted_iota(jnp.int32, (ny, nz), 1) < nz - 1
    rows = [slice(x * ny, (x + 1) * ny) for x in range(nx)]
    values, d = [], []
    for x in range(nx):
        here, c = diff[rows[x], :], conc[rows[x], :]
        flux = jnp.where(
            inside, 0.5 * (here + pltpu.roll(here, nz - 1, 1)) * (pltpu.roll(c, nz - 1, 1) - c), 0.0
        )
        value = (c + applied[rows[x], :]) + (flux - pltpu.roll(flux, 1, 1))
        source[rows[x], :] = value
        values.append(value)
        d.append(here)
    face = [0.5 * (a + b) for a, b in zip(d[:-1], d[1:])]
    ends = chain_ends(values, face)
    for q in range(5):
        payload[q] = ends[q]
    payload[5] = d[0]
    payload[6] = d[-1]


def inside_chain(values, face):
    one = jnp.ones_like(face[0])
    mass, total, through = one, values[0], one
    shares, totals, throughs, inverses = [], [], [], []
    for value, f in zip(values[1:], face):
        inverse = 1.0 / (mass + f)
        share = f * inverse
        shares.append(share)
        inverses.append(inverse)
        totals.append(total)
        throughs.append(through)
        total = value + share * total
        mass = 1.0 + share * mass
        through = share * through
    unit = 1.0 / mass
    base, first, last = [total * unit], [through * unit], [unit]
    for share, inverse, total, through in zip(
        shares[::-1], inverses[::-1], totals[::-1], throughs[::-1]
    ):
        base.append(inverse * total + share * base[-1])
        first.append(inverse * through + share * first[-1])
        last.append(share * last[-1])
    return base[::-1], first[::-1], last[::-1]


def inner_x_kernel(shape, diff, source, base_out, first_out, last_out):
    nx, ny, nz = shape
    for part in range(ny // SUB):
        rows = [slice(x * ny + part * SUB, x * ny + (part + 1) * SUB) for x in range(nx)]
        d = [diff[r, :] for r in rows]
        face = [0.5 * (a + b) for a, b in zip(d[:-1], d[1:])]
        base, first, last = inside_chain([source[r, :] for r in rows], face)
        for r, u, f, l in zip(rows, base, first, last):
            base_out[r, :] = u
            first_out[r, :] = f
            last_out[r, :] = l


def flux_y_kernel(shape, levels, diff, base, first, last, applied, *refs):
    nx, ny, nz = shape
    payload, source, section = refs[-3:]
    lower, upper = solve_levels("gx", levels, refs[:-3])
    for x in range(nx):
        r = slice(x * ny, (x + 1) * ny)
        section[r, :] = (base[r, :] + upper * last[r, :] - lower * first[r, :]) - applied[r, :]
    values = [section[pl.ds(y, nx, stride=ny), :] for y in range(ny)]
    d = [diff[pl.ds(y, nx, stride=ny), :] for y in range(ny)]
    for y in range(ny):
        source[y] = values[y]
    face = [0.5 * (a + b) for a, b in zip(d[:-1], d[1:])]
    ends = chain_ends(values, face)
    for q in range(5):
        payload[q] = ends[q]
    payload[5] = d[0]
    payload[6] = d[-1]


def inner_y_kernel(shape, diff, source, base_out, first_out, last_out):
    nx, ny, nz = shape
    d = [diff[pl.ds(y, nx, stride=ny), :] for y in range(ny)]
    face = [0.5 * (a + b) for a, b in zip(d[:-1], d[1:])]
    base, first, last = inside_chain([source[y] for y in range(ny)], face)
    for y in range(ny):
        base_out[y] = base[y]
        first_out[y] = first[y]
        last_out[y] = last[y]


def last_kernel(shape, levels, diff, conc, base, first, last, *refs):
    nx, ny, nz = shape
    out = refs[-1]
    lower, upper = solve_levels("gy", levels, refs[:-1])
    lane = lax.broadcasted_iota(jnp.int32, (nx, nz), 1)
    for y in range(ny):
        rows = pl.ds(y, nx, stride=ny)
        d, c = diff[rows, :], conc[rows, :]
        right = jnp.where(lane < nz - 1, 0.5 * (d + pltpu.roll(d, nz - 1, 1)), 0.0)
        left = pltpu.roll(right, 1, 1)
        flux = right * (pltpu.roll(c, nz - 1, 1) - c)
        value = (base[y] + upper * last[y] - lower * first[y]) - (flux - pltpu.roll(flux, 1, 1))
        mass = jnp.ones((nx, nz), jnp.float32)
        shift = 1
        while True:
            unit = 1.0 / (mass + left + right)
            mass, left, right, value = mass * unit, left * unit, right * unit, value * unit
            value = (
                value + left * pltpu.roll(value, shift, 1) + right * pltpu.roll(value, nz - shift, 1)
            )
            mass = mass + left * pltpu.roll(mass, shift, 1) + right * pltpu.roll(mass, nz - shift, 1)
            if 2 * shift >= nz:
                break
            left = left * pltpu.roll(left, shift, 1)
            right = right * pltpu.roll(right, nz - shift, 1)
            shift *= 2
        out[rows, :] = value / mass


def pair_exchange(axis, first, second):
    count = lax.axis_size(axis)
    near = [(i, i ^ 1) for i in range(count)]
    far = [(i, (i - 1) % count if i % 2 == 0 else (i + 1) % count) for i in range(count)]
    return lax.ppermute(first, axis, near), lax.ppermute(second, axis, far)


def body(phase_frac, phase_ids, conc, pair_class, mobility, drive, diffusivity):
    slots, nx, ny, nz = phase_frac.shape
    phases = drive.shape[0]
    shape = (nx, ny, nz)
    cells = nx * ny
    flat = (cells, nz)
    frac = phase_frac.reshape(slots, cells, nz)
    ids = phase_ids.reshape(slots, cells, nz)
    field = conc.reshape(cells, nz)

    x_a, x_b, y_a, y_b = call(
        functools.partial(faces_kernel, phases, shape),
        "faces",
        [(phases, ny, nz)] * 2 + [(phases + 1, nx, nz)] * 2,
        [frac, ids, field],
    )
    x_a, x_b = pair_exchange("gx", x_a, x_b)
    y_a, y_b = pair_exchange("gy", y_a, y_b)
    count = -(-phases // (nz // phases))
    new, diffus, table = call(
        functools.partial(interior_kernel, phases, shape),
        "interior",
        [(slots, cells, nz), flat, (count * SUB, nz)],
        [frac, ids, field, pair_class, mobility, drive, diffusivity],
        scratch=[(phases, (nx + 2) * (ny + 2 * SUB), nz)],
        scalars=(4, 5, 6),
    )
    new, diffus, face_a, face_b = call(
        functools.partial(outer_kernel, phases, shape),
        "outer",
        [(slots, cells, nz), flat, (nx, nz), (nx, nz)],
        [new, diffus, table, ids, x_a, x_b, y_a, y_b, diffusivity],
        scalars=(8,),
    )
    face_a, face_b = pair_exchange("gy", face_a, face_b)
    payload, source, applied = call(
        functools.partial(flux_x_kernel, shape),
        "flux_x",
        [(7, ny, nz), flat, flat],
        [diffus, field, y_a, y_b, face_a, face_b],
    )
    levels, refs = gather_levels("gx", payload, (7, ny, nz))
    base, first, last = call(
        functools.partial(inner_x_kernel, shape), "inner_x", [flat] * 3, [diffus, source]
    )
    payload, source = call(
        functools.partial(flux_y_kernel, shape, levels),
        "flux_y",
        [(7, nx, nz), (ny, nx, nz)],
        [diffus, base, first, last, applied] + refs,
        scratch=[flat],
    )
    levels, refs = gather_levels("gy", payload, (7, nx, nz))
    base, first, last = call(
        functools.partial(inner_y_kernel, shape), "inner_y", [(ny, nx, nz)] * 3, [diffus, source]
    )
    (out,) = call(
        functools.partial(last_kernel, shape, levels),
        "last",
        [flat],
        [diffus, field, base, first, last] + refs,
    )
    return new.reshape(slots, nx, ny, nz), out.reshape(nx, ny, nz)


def solution(mesh):
    split = P(None, "gx", "gy", None)
    return jax.shard_map(
        body,
        mesh=mesh,
        in_specs=(split, split, P("gx", "gy", None), P(), P(), P(), P()),
        out_specs=(split, P("gx", "gy", None)),
        check_vma=False,
    )
```

time: 168 us -> 44.6 us (0.27)
  blocking collectives: 41.7 us -> 0 us
  other arithmetic: 40.5 us -> 0 us
  local copies, waits for them, and re-layouts: 30.7 us -> 2.94 us
  starting transfers between devices: 23.4 us -> 10.1 us
  matrix products: 11.9 us -> 0 us
  Pallas kernels: 0 us -> 10.6 us
  waiting for transfers between devices: 11 us -> 19.9 us
  loops' own time: 6.73 us -> 0 us
    all_gather x2 -> x0, blocking collectives: 41.7 us -> none  [the longest x1 34.8 us: gather_x(): return lax.all_gather(payload, 'gx', axis=0, tiled=True)]
    reduce_sum x7 -> x0, other arithmetic: 25.3 us -> none  [the longest x1 20.2 us: body(): jnp.sum(one_hot * diffusivity[None, :, None, None, None], axis=1)]
    dynamic_update_slice x420 -> x0, local copies, waits for them, and re-layouts: 20.5 us -> none  [thomas(): lax.scan(forward, (anchor, anchor), (sub_diag, main_diag, super_diag, rhs...]
    ppermute x12 -> x11, starting transfers between devices: 23.4 us -> 10.1 us  [the longest x6 8.88 us: pair_exchange(): return (lax.ppermute(first, axis, near), lax.ppermute(second, axis, far))]
    dot_general x8 -> x0, matrix products: 11.9 us -> none  [body(): jnp.einsum('pq,pxyz->qxyz', mob_table, one_hot[slot_index], precision=lax...]
    pallas_call x0 -> x11, Pallas kernels: none -> 10.6 us  [call(): pl.pallas_call(kernel, name=name, out_shape=[jax.ShapeDtypeStruct(s, f32)...]
    ppermute x12 -> x11, waiting for transfers between devices: 11 us -> 19.9 us  [the longest x5 17.4 us: gather_levels(): group.append(lax.ppermute(payload, axis, pairs))]
    another operation x10 -> x0, loops' own time: 6.73 us -> none  [the longest x5 3.6 us: thomas(): lax.scan(forward, (anchor, anchor), (sub_diag, main_diag, super_diag, rhs...]
  transfers between devices with their start and end apart: 12 -> 11, of which waited for: 4 -> 7; matrix products, arithmetic and copies ran while one was open for 12% -> 0% of each run, Pallas kernels for 0% -> 13%
where the time goes in v1:
time: 44.6 us; the launch traced here: 44.3 us
  waiting for transfers between devices  19.9 us (45%)
  Pallas kernels  10.6 us (24%)
  starting transfers between devices  10.1 us (23%)
  local copies, waits for them, and re-layouts  2.94 us (7%)
  between operations  0.77 us (2%)
    ppermute x5, waiting for transfers between devices, gather_levels(): group.append(lax.ppermute(payload, axis, pairs))  17.4 us
    pallas_call x11, Pallas kernels, call(): pl.pallas_call(kernel, name=name, out_shape=[jax.ShapeDtypeStruct(s, f32)...  10.6 us
    ppermute x6, starting transfers between devices, pair_exchange(): return (lax.ppermute(first, axis, near), lax.ppermute(second, axis, far))  8.88 us
    unnamed x18, local copies, waits for them, and re-layouts  2.94 us
    ppermute x6, waiting for transfers between devices, pair_exchange(): return (lax.ppermute(first, axis, near), lax.ppermute(second, axis, far))  2.46 us
    ppermute x5, starting transfers between devices, gather_levels(): group.append(lax.ppermute(payload, axis, pairs))  1.2 us
  transfers between devices with their start and end apart: 11, of which 7 were waited for; matrix products, arithmetic and copies ran while one was open for 0% of the time, Pallas kernels for 13%

profile of v1, /device:TPU:0, one launch (start us, length us, event | category | flops | bytes accessed | tf_op | source)
XLA Modules:
  0.0 44.3 jit_solution(11664966668813712355)
XLA Ops:
  0.6 0.0 copy-start
  0.6 1.0 %copy-done = s32[8,8,16,128]{3,2,1,0:T(8,128)S(1)} copy-done((s32[8,8,16,128]{3,2,1,0:T(8,128)S(1)}, s32[8,8,16,128]{3,2,1,0:T(8,128)}, u32[]{:S(2)}) %copy-start) | copy-done | bytes 524312
  1.7 0.0 copy-start.2
  1.7 1.0 %copy-done.2 = f32[8,8,16,128]{3,2,1,0:T(8,128)S(1)} copy-done((f32[8,8,16,128]{3,2,1,0:T(8,128)S(1)}, f32[8,8,16,128]{3,2,1,0:T(8,128)}, u32[]{:S(2)}) %copy-start.2) | copy-done | bytes 524312
  2.7 0.0 copy-start.3
  2.7 0.8 %copy-done.3 = f32[8,16,128]{2,1,0:T(8,128)S(1)} copy-done((f32[8,16,128]{2,1,0:T(8,128)S(1)}, f32[8,16,128]{2,1,0:T(8,128)}, u32[]{:S(2)}) %copy-start.3) | copy-done | bytes 65560
  3.6 0.0 copy-start.5
  3.6 0.2 faces.1
  3.8 3.0 %collective-permute-start = (f32[16,16,128]{2,1,0:T(8,128)S(1)}, f32[16,16,128]{2,1,0:T(8,128)S(1)}, u32[]{:S(2)}, u32[]{:S(2)}) collective-permute-start(f32[16,16,128]{2,1,0:T(8,128)S(1)} %get-tuple-element.27), channel_id=1, source_target_pairs={{0,4},{4,0},{8,12},{12,8},{16,20},{20,16},{24,28},{28,24},{1,5},{5... | collective-permute-start | bytes 393224 | tf_op jit(solution)/shard_map/ppermute | solution.py:524
  6.8 3.6 %collective-permute-start.1 = (f32[16,16,128]{2,1,0:T(8,128)S(1)}, f32[16,16,128]{2,1,0:T(8,128)S(1)}, u32[]{:S(2)}, u32[]{:S(2)}) collective-permute-start(f32[16,16,128]{2,1,0:T(8,128)S(1)} %get-tuple-element.28), channel_id=1, source_target_pairs={{0,28},{4,8},{8,4},{12,16},{16,12},{20,24},{24,20},{28,0},{1,29},{... | collective-permute-start | bytes 393224 | tf_op jit(solution)/shard_map/ppermute | solution.py:524
  10.4 0.0 copy-start.6
  10.4 0.0 copy-start.7
  10.4 0.0 copy-start.8
  10.4 0.0 collective-permute-start.2
  10.4 0.0 copy-start.1
  10.4 1.6 %collective-permute-start.3 = (f32[17,8,128]{2,1,0:T(8,128)S(1)}, f32[17,8,128]{2,1,0:T(8,128)S(1)}, u32[]{:S(2)}, u32[]{:S(2)}) collective-permute-start(f32[17,8,128]{2,1,0:T(8,128)S(1)} %get-tuple-element.30), channel_id=1, source_target_pairs={{0,3},{1,2},{2,1},{3,0},{4,7},{5,6},{6,5},{7,4},{8,11},{9,10},{10,... | collective-permute-start | bytes 208904 | tf_op jit(solution)/shard_map/ppermute | solution.py:524
  12.0 0.0 copy-done.5
  12.0 0.0 copy-done.6
  12.1 0.0 copy-done.7
  12.1 0.0 copy-done.8
  12.1 5.6 %interior.1 = (f32[8,128,128]{2,1,0:T(8,128)S(1)}, f32[128,128]{1,0:T(8,128)S(1)}, f32[16,128]{1,0:T(8,128)S(1)}) custom-call(f32[8,128,128]{2,1,0:T(8,128)S(1)} %bitcast.9, s32[8,128,128]{2,1,0:T(8,128)S(1)} %bitcast.6, f32[128,128]{1,0:T(8,128)S(1)} %bitcast.11, s32[16,16]{1,0:T(8,128)S(1)} %copy-done.5, f32[4]{0:T(128)S(1)} %copy-done.7, ...), custom_call_target="tpu_custom_call" | custom-call | flops 20000000 | bytes 1048576 | tf_op jit(solution)/shard_map/interior/pallas_call | solution.py:20
  17.6 0.0 collective-permute-done.2.y_a
  17.6 0.0 collective-permute-done.3.y_b
  17.7 0.0 collective-permute-done.x_a
  17.7 0.0 collective-permute-done.1.x_b
  17.7 0.0 copy-done.1
  17.7 0.0 copy-start.4
  17.7 2.4 %outer.1 = (f32[8,128,128]{2,1,0:T(8,128)}, f32[128,128]{1,0:T(8,128)S(1)}, f32[8,128]{1,0:T(8,128)S(1)}, f32[8,128]{1,0:T(8,128)S(1)}) custom-call(f32[8,128,128]{2,1,0:T(8,128)S(1)} %get-tuple-element.24.new_in, f32[128,128]{1,0:T(8,128)S(1)} %get-tuple-element.25.diff_in, f32[16,128]{1,0:T(8,128)S(1)} %get-tuple-element.26.table, ...), custom_call_target="tpu_custom_call" | custom-call | flops 20000000 | bytes 1048576 | tf_op jit(solution)/shard_map/outer/pallas_call | solution.py:20
  20.1 0.1 collective-permute-start.4
  20.2 0.6 %collective-permute-start.5 = (f32[8,128]{1,0:T(8,128)S(1)}, f32[8,128]{1,0:T(8,128)S(1)}, u32[]{:S(2)}, u32[]{:S(2)}) collective-permute-start(f32[8,128]{1,0:T(8,128)S(1)} %get-tuple-element.34), channel_id=1, source_target_pairs={{0,3},{1,2},{2,1},{3,0},{4,7},{5,6},{6,5},{7,4},{8,11},{9,10},{10,... | collective-permute-start | bytes 12296 | tf_op jit(solution)/shard_map/ppermute | solution.py:524
  20.7 0.5 %collective-permute-done.4.halo_a = f32[8,128]{1,0:T(8,128)S(1)} collective-permute-done((f32[8,128]{1,0:T(8,128)S(1)}, f32[8,128]{1,0:T(8,128)S(1)}, u32[]{:S(2)}, u32[]{:S(2)}) %collective-permute-start.4) | collective-permute-done | bytes 4128 | tf_op jit(solution)/shard_map/ppermute | solution.py:524
  21.2 1.9 %collective-permute-done.5.halo_b = f32[8,128]{1,0:T(8,128)S(1)} collective-permute-done((f32[8,128]{1,0:T(8,128)S(1)}, f32[8,128]{1,0:T(8,128)S(1)}, u32[]{:S(2)}, u32[]{:S(2)}) %collective-permute-start.5) | collective-permute-done | bytes 4128 | tf_op jit(solution)/shard_map/ppermute | solution.py:524
  23.2 0.0 copy-done.4
  23.2 0.2 flux_x.1
  23.4 0.1 collective-permute-start.6
  23.5 4.2 %collective-permute-done.6.refs_1_ = f32[7,16,128]{2,1,0:T(8,128)S(1)} collective-permute-done((f32[7,16,128]{2,1,0:T(8,128)S(1)}, f32[7,16,128]{2,1,0:T(8,128)S(1)}, u32[]{:S(2)}, u32[]{:S(2)}) %collective-permute-start.6) | collective-permute-done | bytes 57376 | tf_op jit(solution)/shard_map/ppermute | solution.py:364
  27.7 0.1 collective-permute-start.7
  27.8 4.2 %collective-permute-done.7.refs_1_.refs_3_ = f32[7,16,128]{2,1,0:T(8,128)S(1)} collective-permute-done((f32[7,16,128]{2,1,0:T(8,128)S(1)}, f32[7,16,128]{2,1,0:T(8,128)S(1)}, u32[]{:S(2)}, u32[]{:S(2)}) %collective-permute-start.7) | collective-permute-done | bytes 57376 | tf_op jit(solution)/shard_map/ppermute | solution.py:364
  32.0 0.4 collective-permute-start.8
  32.4 0.1 inner_x.1
  32.5 4.7 %collective-permute-done.8.refs_5_ = f32[7,16,128]{2,1,0:T(8,128)S(1)} collective-permute-done((f32[7,16,128]{2,1,0:T(8,128)S(1)}, f32[7,16,128]{2,1,0:T(8,128)S(1)}, u32[]{:S(2)}, u32[]{:S(2)}) %collective-permute-start.8) | collective-permute-done | bytes 57376 | tf_op jit(solution)/shard_map/ppermute | solution.py:364
  37.2 0.2 flux_y.1
  37.4 0.1 collective-permute-start.9
  37.5 1.2 %collective-permute-done.9.refs_1_ = f32[7,8,128]{2,1,0:T(8,128)S(1)} collective-permute-done((f32[7,8,128]{2,1,0:T(8,128)S(1)}, f32[7,8,128]{2,1,0:T(8,128)S(1)}, u32[]{:S(2)}, u32[]{:S(2)}) %collective-permute-start.9) | collective-permute-done | bytes 28704 | tf_op jit(solution)/shard_map/ppermute | solution.py:364
  38.7 0.6 %collective-permute-start.10 = (f32[7,8,128]{2,1,0:T(8,128)S(1)}, f32[7,8,128]{2,1,0:T(8,128)S(1)}, u32[]{:S(2)}, u32[]{:S(2)}) collective-permute-start(f32[7,8,128]{2,1,0:T(8,128)S(1)} %join_gy.1.refs_2_), channel_id=1, source_target_pairs={{0,2},{1,3},{2,0},{3,1},{4,6},{5,7},{6,4},{7,5},{8,10},{9,11},{10,... | collective-permute-start | bytes 86024 | tf_op jit(solution)/shard_map/ppermute | solution.py:364
  39.3 0.2 inner_y.1
  39.5 3.1 %collective-permute-done.10.refs_3_ = f32[7,8,128]{2,1,0:T(8,128)S(1)} collective-permute-done((f32[7,8,128]{2,1,0:T(8,128)S(1)}, f32[7,8,128]{2,1,0:T(8,128)S(1)}, u32[]{:S(2)}, u32[]{:S(2)}) %collective-permute-start.10) | collective-permute-done | bytes 28704 | tf_op jit(solution)/shard_map/ppermute | solution.py:364
  42.7 1.7 %last.1 = f32[128,128]{1,0:T(8,128)} custom-call(f32[128,128]{1,0:T(8,128)S(1)} %get-tuple-element.32.diff, f32[128,128]{1,0:T(8,128)S(1)} %bitcast.13, f32[16,8,128]{2,1,0:T(8,128)S(1)} %get-tuple-element.42.base, f32[16,8,128]{2,1,0:T(8,128)S(1)} %get-tuple-element.43.first, f32[16,8,128]{2,1,0:T(8,128)S(1)} %get-tuple-element.44.last, ...), custom_call_target="tpu_custom_call" | custom-call | flops 20000000 | bytes 1048576 | tf_op jit(solution)/shard_map/last/pallas_call | solution.py:20
  (3 shorter events, 0.1 us)
Async XLA Ops:
  0.6 1.0 %copy-start = (s32[8,8,16,128]{3,2,1,0:T(8,128)S(1)}, s32[8,8,16,128]{3,2,1,0:T(8,128)}, u32[]{:S(2)}) copy-start(s32[8,8,16,128]{3,2,1,0:T(8,128)} %param.8) | copy-start | bytes 1572868
  1.7 1.0 %copy-start.2 = (f32[8,8,16,128]{3,2,1,0:T(8,128)S(1)}, f32[8,8,16,128]{3,2,1,0:T(8,128)}, u32[]{:S(2)}) copy-start(f32[8,8,16,128]{3,2,1,0:T(8,128)} %param.7) | copy-start | bytes 1572868
  2.7 0.8 %copy-start.3 = (f32[8,16,128]{2,1,0:T(8,128)S(1)}, f32[8,16,128]{2,1,0:T(8,128)}, u32[]{:S(2)}) copy-start(f32[8,16,128]{2,1,0:T(8,128)} %param.9) | copy-start | bytes 196612
  3.6 8.5 %copy-start.5 = (s32[16,16]{1,0:T(8,128)S(1)}, s32[16,16]{1,0:T(8,128)}, u32[]{:S(2)}) copy-start(s32[16,16]{1,0:T(8,128)} %pair_class.1) | copy-start | bytes 3076
  3.8 13.9 %collective-permute-start = (f32[16,16,128]{2,1,0:T(8,128)S(1)}, f32[16,16,128]{2,1,0:T(8,128)S(1)}, u32[]{:S(2)}, u32[]{:S(2)}) collective-permute-start(f32[16,16,128]{2,1,0:T(8,128)S(1)} %get-tuple-element.27), channel_id=1, source_target_pairs={{0,4},{4,0},{8,12},{12,8},{16,20},{20,16},{24,28},{28,24},{1,5},{5... | collective-permute-start | bytes 393224 | tf_op jit(solution)/shard_map/ppermute | solution.py:524
  6.8 10.8 %collective-permute-start.1 = (f32[16,16,128]{2,1,0:T(8,128)S(1)}, f32[16,16,128]{2,1,0:T(8,128)S(1)}, u32[]{:S(2)}, u32[]{:S(2)}) collective-permute-start(f32[16,16,128]{2,1,0:T(8,128)S(1)} %get-tuple-element.28), channel_id=1, source_target_pairs={{0,28},{4,8},{8,4},{12,16},{16,12},{20,24},{24,20},{28,0},{1,29},{... | collective-permute-start | bytes 393224 | tf_op jit(solution)/shard_map/ppermute | solution.py:524
  10.4 1.6 %copy-start.6 = (f32[16]{0:T(128)S(1)}, f32[16]{0:T(128)}, u32[]{:S(2)}) copy-start(f32[16]{0:T(128)} %diffusivity.3) | copy-start | bytes 196
  10.4 1.6 %copy-start.7 = (f32[4]{0:T(128)S(1)}, f32[4]{0:T(128)}, u32[]{:S(2)}) copy-start(f32[4]{0:T(128)} %mobility.1) | copy-start | bytes 52
  10.4 1.6 %copy-start.8 = (f32[16]{0:T(128)S(1)}, f32[16]{0:T(128)}, u32[]{:S(2)}) copy-start(f32[16]{0:T(128)} %drive.1) | copy-start | bytes 196
  10.4 7.2 %collective-permute-start.2 = (f32[17,8,128]{2,1,0:T(8,128)S(1)}, f32[17,8,128]{2,1,0:T(8,128)S(1)}, u32[]{:S(2)}, u32[]{:S(2)}) collective-permute-start(f32[17,8,128]{2,1,0:T(8,128)S(1)} %get-tuple-element.29), channel_id=1, source_target_pairs={{0,1},{1,0},{2,3},{3,2},{4,5},{5,4},{6,7},{7,6},{8,9},{9,8},{10,11... | collective-permute-start | bytes 208904 | tf_op jit(solution)/shard_map/ppermute | solution.py:524
  10.4 7.3 %copy-start.1 = (s32[8,8,16,128]{3,2,1,0:T(8,128)S(1)}, s32[8,8,16,128]{3,2,1,0:T(8,128)}, u32[]{:S(2)}) copy-start(s32[8,8,16,128]{3,2,1,0:T(8,128)} %param.8) | copy-start | bytes 1572868
  10.4 7.2 %collective-permute-start.3 = (f32[17,8,128]{2,1,0:T(8,128)S(1)}, f32[17,8,128]{2,1,0:T(8,128)S(1)}, u32[]{:S(2)}, u32[]{:S(2)}) collective-permute-start(f32[17,8,128]{2,1,0:T(8,128)S(1)} %get-tuple-element.30), channel_id=1, source_target_pairs={{0,3},{1,2},{2,1},{3,0},{4,7},{5,6},{6,5},{7,4},{8,11},{9,10},{10,... | collective-permute-start | bytes 208904 | tf_op jit(solution)/shard_map/ppermute | solution.py:524
  17.7 5.5 %copy-start.4 = (f32[8,16,128]{2,1,0:T(8,128)S(1)}, f32[8,16,128]{2,1,0:T(8,128)}, u32[]{:S(2)}) copy-start(f32[8,16,128]{2,1,0:T(8,128)} %param.9) | copy-start | bytes 196612
  20.1 1.2 %collective-permute-start.4 = (f32[8,128]{1,0:T(8,128)S(1)}, f32[8,128]{1,0:T(8,128)S(1)}, u32[]{:S(2)}, u32[]{:S(2)}) collective-permute-start(f32[8,128]{1,0:T(8,128)S(1)} %get-tuple-element.33), channel_id=1, source_target_pairs={{0,1},{1,0},{2,3},{3,2},{4,5},{5,4},{6,7},{7,6},{8,9},{9,8},{10,11... | collective-permute-start | bytes 12296 | tf_op jit(solution)/shard_map/ppermute | solution.py:524
  20.2 3.0 %collective-permute-start.5 = (f32[8,128]{1,0:T(8,128)S(1)}, f32[8,128]{1,0:T(8,128)S(1)}, u32[]{:S(2)}, u32[]{:S(2)}) collective-permute-start(f32[8,128]{1,0:T(8,128)S(1)} %get-tuple-element.34), channel_id=1, source_target_pairs={{0,3},{1,2},{2,1},{3,0},{4,7},{5,6},{6,5},{7,4},{8,11},{9,10},{10,... | collective-permute-start | bytes 12296 | tf_op jit(solution)/shard_map/ppermute | solution.py:524
  23.4 4.3 %collective-permute-start.6 = (f32[7,16,128]{2,1,0:T(8,128)S(1)}, f32[7,16,128]{2,1,0:T(8,128)S(1)}, u32[]{:S(2)}, u32[]{:S(2)}) collective-permute-start(f32[7,16,128]{2,1,0:T(8,128)S(1)} %get-tuple-element.40.refs_0_), channel_id=1, source_target_pairs={{0,4},{4,0},{8,12},{12,8},{16,20},{20,16},{24,28},{28,24},{1,5},{5... | collective-permute-start | bytes 172040 | tf_op jit(solution)/shard_map/ppermute | solution.py:364
  27.7 4.2 %collective-permute-start.7 = (f32[7,16,128]{2,1,0:T(8,128)S(1)}, f32[7,16,128]{2,1,0:T(8,128)S(1)}, u32[]{:S(2)}, u32[]{:S(2)}) collective-permute-start(f32[7,16,128]{2,1,0:T(8,128)S(1)} %join_gx.2.refs_0_.refs_2_), channel_id=1, source_target_pairs={{0,8},{4,12},{8,0},{12,4},{16,24},{20,28},{24,16},{28,20},{1,9},{5... | collective-permute-start | bytes 172040 | tf_op jit(solution)/shard_map/ppermute | solution.py:364
  32.0 5.2 %collective-permute-start.8 = (f32[7,16,128]{2,1,0:T(8,128)S(1)}, f32[7,16,128]{2,1,0:T(8,128)S(1)}, u32[]{:S(2)}, u32[]{:S(2)}) collective-permute-start(f32[7,16,128]{2,1,0:T(8,128)S(1)} %join_gx.3.refs_4_), channel_id=1, source_target_pairs={{0,16},{4,20},{8,24},{12,28},{16,0},{20,4},{24,8},{28,12},{1,17},{... | collective-permute-start | bytes 172040 | tf_op jit(solution)/shard_map/ppermute | solution.py:364
  37.4 1.3 %collective-permute-start.9 = (f32[7,8,128]{2,1,0:T(8,128)S(1)}, f32[7,8,128]{2,1,0:T(8,128)S(1)}, u32[]{:S(2)}, u32[]{:S(2)}) collective-permute-start(f32[7,8,128]{2,1,0:T(8,128)S(1)} %get-tuple-element.45.refs_0_), channel_id=1, source_target_pairs={{0,1},{1,0},{2,3},{3,2},{4,5},{5,4},{6,7},{7,6},{8,9},{9,8},{10,11... | collective-permute-start | bytes 86024 | tf_op jit(solution)/shard_map/ppermute | solution.py:364
  38.7 3.9 %collective-permute-start.10 = (f32[7,8,128]{2,1,0:T(8,128)S(1)}, f32[7,8,128]{2,1,0:T(8,128)S(1)}, u32[]{:S(2)}, u32[]{:S(2)}) collective-permute-start(f32[7,8,128]{2,1,0:T(8,128)S(1)} %join_gy.1.refs_2_), channel_id=1, source_target_pairs={{0,2},{1,3},{2,0},{3,1},{4,6},{5,7},{6,4},{7,5},{8,10},{9,11},{10,... | collective-permute-start | bytes 86024 | tf_op jit(solution)/shard_map/ppermute | solution.py:364

commit v2 on v1

--- a/solution.py
+++ b/solution.py
@@ -13,21 +13,27 @@
 
 VMEM = pl.BlockSpec(memory_space=pltpu.VMEM)
 SMEM = pl.BlockSpec(memory_space=pltpu.SMEM)
-
-
-def call(kernel, name, outs, ins, scratch=(), aliases={}, cost=20000, scalars=()):
+HBM = pl.BlockSpec(memory_space=pltpu.HBM)
+
+
+def call(kernel, name, outs, ins, scratch=(), aliases={}, cost=20000, scalars=(), far=()):
     f32 = jnp.float32
+    place = [SMEM if i in scalars else HBM if i in far else VMEM for i in range(len(ins))]
     return pl.pallas_call(
         kernel,
         name=name,
-        out_shape=[jax.ShapeDtypeStruct(s, f32) for s in outs],
-        in_specs=[SMEM if i in scalars else VMEM for i in range(len(ins))],
+        out_shape=[s if isinstance(s, jax.ShapeDtypeStruct) else jax.ShapeDtypeStruct(s, f32) for s in outs],
+        in_specs=place,
         out_specs=[VMEM] * len(outs),
-        scratch_shapes=[pltpu.VMEM(s, f32) for s in scratch],
+        scratch_shapes=[pltpu.VMEM(s, f32) if isinstance(s, tuple) else s for s in scratch],
         input_output_aliases=aliases,
         compiler_params=pltpu.CompilerParams(vmem_limit_bytes=12 << 20),
         cost_estimate=pl.CostEstimate(flops=cost * 1000, bytes_accessed=1 << 20, transcendentals=0),
     )(*ins)
+
+
+def far_away(array):
+    return pltpu.with_memory_space_constraint(array, pltpu.HBM)
 
 
 def lookup(table, index):
@@ -95,9 +101,24 @@
     return sums
 
 
-def faces_kernel(phases, shape, frac, ids, conc, x_a, x_b, y_a, y_b):
+def faces_kernel(phases, shape, frac_far, ids_far, conc_far, frac, ids, conc, x_a, x_b, y_a, y_b, sems):
     nx, ny, _ = shape
     slots = frac.shape[0]
+    half = slots // 2
+    copies = []
+    for k, (far, near) in enumerate(
+        [
+            (frac_far.at[:half], frac.at[:half]),
+            (ids_far.at[:half], ids.at[:half]),
+            (frac_far.at[half:], frac.at[half:]),
+            (ids_far.at[half:], ids.at[half:]),
+            (conc_far, conc),
+        ]
+    ):
+        copies.append(pltpu.make_async_copy(far, near, sems.at[k]))
+        copies[-1].start()
+    for copy in copies:
+        copy.wait()
     right = even("gx")
     for out, upper in ((x_a, right), (x_b, jnp.logical_not(right))):
         base = jnp.where(upper, (nx - 1) * ny, 0)
@@ -124,15 +145,48 @@
 
 
 def interior_kernel(
-    phases, shape, frac, ids, conc, pair_class, mobility, drive, diffusivity,
-    new_out, diff_out, table_out, dense,
+    phases, shape, frac, ids, conc, *rest
 ):
+    new_out, diff_out, table_out, diff_table_out, dense, pair_class, mobility, drive, diffusivity, sems = rest[4:]
+    copies = [
+        pltpu.make_async_copy(far, near, sems.at[k])
+        for k, (far, near) in enumerate(zip(rest[:4], (pair_class, mobility, drive, diffusivity)))
+    ]
+    for copy in copies:
+        copy.start()
     nx, ny, nz = shape
     slots = frac.shape[0]
     pitch = ny + 2 * SUB
     parts = ny // SUB
     per_row = nz // phases
     count = -(-phases // per_row)
+    nothing = jnp.zeros((SUB, nz), jnp.float32)
+
+    def clear(phase, carry):
+        for plane in range(nx + 2):
+            for part in range(parts + 2):
+                if plane in (0, nx + 1) or part in (0, parts + 1):
+                    dense[phase, plane * pitch + part * SUB : plane * pitch + (part + 1) * SUB, :] = nothing
+        return carry
+
+    lax.fori_loop(0, phases, clear, 0)
+
+    def build(x, carry):
+        for part in range(parts):
+            rows = pl.ds(pl.multiple_of(x * ny, SUB) + part * SUB, SUB)
+            held = pick_rows(
+                [ids[s, rows, :] for s in range(slots)],
+                [frac[s, rows, :] for s in range(slots)],
+                phases,
+            )
+            into = pl.ds(pl.multiple_of((x + 1) * pitch, SUB) + (part + 1) * SUB, SUB)
+            for phase in range(phases):
+                dense[phase, into, :] = held[phase]
+        return carry
+
+    lax.fori_loop(0, nx, build, 0)
+    for copy in copies:
+        copy.wait()
     lane = lax.broadcasted_iota(jnp.int32, (per_row, nz), 1)
     row = lax.broadcasted_iota(jnp.int32, (per_row, nz), 0)
     for t in range(count):
@@ -149,31 +203,7 @@
         table_out[t * SUB : (t + 1) * SUB, :] = jnp.broadcast_to(line, (SUB, nz))
     drive_table = scalar_table(drive, (SUB, nz))
     diff_table = scalar_table(diffusivity, (SUB, nz))
-    nothing = jnp.zeros((SUB, nz), jnp.float32)
-
-    def clear(phase, carry):
-        for plane in range(nx + 2):
-            for part in range(parts + 2):
-                if plane in (0, nx + 1) or part in (0, parts + 1):
-                    dense[phase, plane * pitch + part * SUB : plane * pitch + (part + 1) * SUB, :] = nothing
-        return carry
-
-    lax.fori_loop(0, phases, clear, 0)
-
-    def build(x, carry):
-        for part in range(parts):
-            rows = pl.ds(pl.multiple_of(x * ny, SUB) + part * SUB, SUB)
-            held = pick_rows(
-                [ids[s, rows, :] for s in range(slots)],
-                [frac[s, rows, :] for s in range(slots)],
-                phases,
-            )
-            into = pl.ds(pl.multiple_of((x + 1) * pitch, SUB) + (part + 1) * SUB, SUB)
-            for phase in range(phases):
-                dense[phase, into, :] = held[phase]
-        return carry
-
-    lax.fori_loop(0, nx, build, 0)
+    diff_table_out[...] = diff_table
 
     def update(x, carry):
         for part in range(parts):
@@ -208,14 +238,13 @@
 
 
 def outer_kernel(
-    phases, shape, new_in, diff_in, table, ids, x_a, x_b, y_a, y_b, diffusivity,
+    phases, shape, new_in, diff_in, table, ids, x_a, x_b, y_a, y_b, diff_table_in,
     new_out, diff_out, face_a, face_b,
 ):
     nx, ny, nz = shape
     slots = new_in.shape[0]
-    diff_table = scalar_table(diffusivity, (SUB, nz))
-    new_out[...] = new_in[...]
-    diff_out[...] = diff_in[...]
+    diff_table = diff_table_in[...]
+    del new_in, diff_in
 
     def add(rows, halo):
         slot_ids = [ids[s, rows, :] for s in range(slots)]
@@ -372,7 +401,7 @@
     return levels, refs
 
 
-def flux_x_kernel(shape, diff, conc, y_a, y_b, halo_a, halo_b, payload, source, applied):
+def flux_x_kernel(shape, diff, conc, y_a, y_b, halo_a, halo_b, _, payload, source, applied):
     nx, ny, nz = shape
     up = even("gy")
     place = lax.axis_index("gy")
@@ -458,7 +487,7 @@
             last_out[r, :] = l
 
 
-def flux_y_kernel(shape, levels, diff, base, first, last, applied, *refs):
+def flux_y_kernel(shape, levels, diff, base, first, last, applied, _, *refs):
     nx, ny, nz = shape
     payload, source, section = refs[-3:]
     lower, upper = solve_levels("gx", levels, refs[:-3])
@@ -488,33 +517,67 @@
         last_out[y] = last[y]
 
 
-def last_kernel(shape, levels, diff, conc, base, first, last, *refs):
-    nx, ny, nz = shape
-    out = refs[-1]
-    lower, upper = solve_levels("gy", levels, refs[:-1])
+def steps_of(nz):
+    count = 1
+    while 2**count < nz:
+        count += 1
+    return count
+
+
+def coefficients_z_kernel(shape, diff, conc, applied, start, left_out, right_out, unit_out):
+    nx, ny, nz = shape
     lane = lax.broadcasted_iota(jnp.int32, (nx, nz), 1)
+
+    state = []
     for y in range(ny):
         rows = pl.ds(y, nx, stride=ny)
         d, c = diff[rows, :], conc[rows, :]
         right = jnp.where(lane < nz - 1, 0.5 * (d + pltpu.roll(d, nz - 1, 1)), 0.0)
         left = pltpu.roll(right, 1, 1)
         flux = right * (pltpu.roll(c, nz - 1, 1) - c)
-        value = (base[y] + upper * last[y] - lower * first[y]) - (flux - pltpu.roll(flux, 1, 1))
+        applied[y] = flux - pltpu.roll(flux, 1, 1)
         mass = jnp.ones((nx, nz), jnp.float32)
-        shift = 1
-        while True:
-            unit = 1.0 / (mass + left + right)
-            mass, left, right, value = mass * unit, left * unit, right * unit, value * unit
-            value = (
-                value + left * pltpu.roll(value, shift, 1) + right * pltpu.roll(value, nz - shift, 1)
-            )
+        unit = 1.0 / (mass + left + right)
+        start[y] = unit
+        state.append((mass, left, right, unit))
+    for step in range(steps_of(nz)):
+        shift = 2**step
+        for y in range(ny):
+            mass, left, right, unit = state[y]
+            mass, left, right = mass * unit, left * unit, right * unit
             mass = mass + left * pltpu.roll(mass, shift, 1) + right * pltpu.roll(mass, nz - shift, 1)
-            if 2 * shift >= nz:
-                break
-            left = left * pltpu.roll(left, shift, 1)
-            right = right * pltpu.roll(right, nz - shift, 1)
-            shift *= 2
-        out[rows, :] = value / mass
+            wide_left = left * pltpu.roll(left, shift, 1)
+            wide_right = right * pltpu.roll(right, nz - shift, 1)
+            unit = 1.0 / (mass + wide_left + wide_right) if 2 * shift < nz else 1.0 / mass
+            left_out[step, y] = left * unit
+            right_out[step, y] = right * unit
+            unit_out[step, y] = unit
+            state[y] = mass, wide_left, wide_right, unit
+
+
+def last_kernel(shape, levels, applied, start, left, right, unit, base, first, last, *refs):
+    nx, ny, nz = shape
+    out = refs[-1]
+    lower, upper = solve_levels("gy", levels, refs[:-1])
+    values = [
+        ((base[y] + upper * last[y] - lower * first[y]) - applied[y]) * start[y] for y in range(ny)
+    ]
+    for step in range(steps_of(nz)):
+        shift = 2**step
+        values = [
+            unit[step, y] * v
+            + left[step, y] * pltpu.roll(v, shift, 1)
+            + right[step, y] * pltpu.roll(v, nz - shift, 1)
+            for y, v in enumerate(values)
+        ]
+    for y in range(ny):
+        out[pl.ds(y, nx, stride=ny), :] = values[y]
+
+
+def commit_kernel(new, out, sem):
+    copy = pltpu.make_async_copy(new, out, sem)
+    copy.start()
+    copy.wait()
 
 
 def pair_exchange(axis, first, second):
@@ -530,42 +593,69 @@
     shape = (nx, ny, nz)
     cells = nx * ny
     flat = (cells, nz)
-    frac = phase_frac.reshape(slots, cells, nz)
-    ids = phase_ids.reshape(slots, cells, nz)
-    field = conc.reshape(cells, nz)
-
-    x_a, x_b, y_a, y_b = call(
+    frac = far_away(phase_frac.reshape(slots, cells, nz))
+    ids = far_away(phase_ids.reshape(slots, cells, nz))
+    field = far_away(conc.reshape(cells, nz))
+
+    frac, ids, field, x_a, x_b, y_a, y_b = call(
         functools.partial(faces_kernel, phases, shape),
         "faces",
-        [(phases, ny, nz)] * 2 + [(phases + 1, nx, nz)] * 2,
+        [frac.shape, jax.ShapeDtypeStruct(ids.shape, ids.dtype), flat]
+        + [(phases, ny, nz)] * 2
+        + [(phases + 1, nx, nz)] * 2,
         [frac, ids, field],
+        scratch=[pltpu.SemaphoreType.DMA((5,))],
+        far=(0, 1, 2),
     )
     x_a, x_b = pair_exchange("gx", x_a, x_b)
     y_a, y_b = pair_exchange("gy", y_a, y_b)
     count = -(-phases // (nz // phases))
-    new, diffus, table = call(
+    small = [pair_class, mobility, drive, diffusivity]
+    new, diffus, table, diff_table = call(
         functools.partial(interior_kernel, phases, shape),
         "interior",
-        [(slots, cells, nz), flat, (count * SUB, nz)],
-        [frac, ids, field, pair_class, mobility, drive, diffusivity],
-        scratch=[(phases, (nx + 2) * (ny + 2 * SUB), nz)],
-        scalars=(4, 5, 6),
+        [(slots, cells, nz), flat, (count * SUB, nz), (SUB, nz)],
+        [frac, ids, field] + [far_away(v) for v in small],
+        scratch=[
+            (phases, (nx + 2) * (ny + 2 * SUB), nz),
+            pltpu.VMEM(pair_class.shape, pair_class.dtype),
+        ]
+        + [pltpu.SMEM(v.shape, v.dtype) for v in small[1:]]
+        + [pltpu.SemaphoreType.DMA((4,))],
+        far=(3, 4, 5, 6),
     )
     new, diffus, face_a, face_b = call(
         functools.partial(outer_kernel, phases, shape),
         "outer",
         [(slots, cells, nz), flat, (nx, nz), (nx, nz)],
-        [new, diffus, table, ids, x_a, x_b, y_a, y_b, diffusivity],
-        scalars=(8,),
+        [new, diffus, table, ids, x_a, x_b, y_a, y_b, diff_table],
+        aliases={0: 0, 1: 1},
     )
     face_a, face_b = pair_exchange("gy", face_a, face_b)
+    (new,) = pl.pallas_call(
+        commit_kernel,
+        name="commit",
+        out_shape=[jax.ShapeDtypeStruct(new.shape, new.dtype)],
+        in_specs=[VMEM],
+        out_specs=[HBM],
+        scratch_shapes=[pltpu.SemaphoreType.DMA],
+        compiler_params=pltpu.CompilerParams(vmem_limit_bytes=12 << 20),
+        cost_estimate=pl.CostEstimate(flops=20000000, bytes_accessed=1 << 20, transcendentals=0),
+    )(new)
     payload, source, applied = call(
         functools.partial(flux_x_kernel, shape),
         "flux_x",
         [(7, ny, nz), flat, flat],
-        [diffus, field, y_a, y_b, face_a, face_b],
+        [diffus, field, y_a, y_b, face_a, face_b, far_away(new)],
+        far=(6,),
     )
     levels, refs = gather_levels("gx", payload, (7, ny, nz))
+    applied_z, start, left, right, unit = call(
+        functools.partial(coefficients_z_kernel, shape),
+        "coefficients_z",
+        [(ny, nx, nz)] * 2 + [(steps_of(nz), ny, nx, nz)] * 3,
+        [diffus, field],
+    )
     base, first, last = call(
         functools.partial(inner_x_kernel, shape), "inner_x", [flat] * 3, [diffus, source]
     )
@@ -573,7 +663,7 @@
         functools.partial(flux_y_kernel, shape, levels),
         "flux_y",
         [(7, nx, nz), (ny, nx, nz)],
-        [diffus, base, first, last, applied] + refs,
+        [diffus, base, first, last, applied, applied_z] + refs,
         scratch=[flat],
     )
     levels, refs = gather_levels("gy", payload, (7, nx, nz))
@@ -584,7 +674,7 @@
         functools.partial(last_kernel, shape, levels),
         "last",
         [flat],
-        [diffus, field, base, first, last] + refs,
+        [applied_z, start, left, right, unit, base, first, last] + refs,
     )
     return new.reshape(slots, nx, ny, nz), out.reshape(nx, ny, nz)
 

time: 44.6 us -> 40.8 us (0.915)
  local copies, waits for them, and re-layouts: 2.94 us -> 0 us
  waiting for transfers between devices: 19.9 us -> 18.2 us
  Pallas kernels: 10.6 us -> 11.5 us
    unnamed x18 -> x0, local copies, waits for them, and re-layouts: 2.94 us -> none
    ppermute x5, waiting for transfers between devices: 17.4 us -> 16.5 us  [gather_levels(): group.append(lax.ppermute(payload, axis, pairs))]
    pallas_call x11 -> x13, Pallas kernels: 10.6 us -> 11.5 us  [the longest x12 10.7 us: call(): pl.pallas_call(kernel, name=name, out_shape=[s if isinstance(s, jax.Shape...]
    ppermute x6, waiting for transfers between devices: 2.46 us -> 1.68 us  [pair_exchange(): return (lax.ppermute(first, axis, near), lax.ppermute(second, axis, far))]
  transfers between devices with their start and end apart: 11 -> 11, of which waited for: 7 -> 6; matrix products, arithmetic and copies ran while one was open for 0% -> 0% of each run, Pallas kernels for 13% -> 18%
where the time goes in v2:
time: 40.8 us; the launch traced here: 40.6 us
  waiting for transfers between devices  18.2 us (45%)
  Pallas kernels  11.5 us (28%)
  starting transfers between devices  10.1 us (25%)
  between operations  0.77 us (2%)
    ppermute x5, waiting for transfers between devices, gather_levels(): group.append(lax.ppermute(payload, axis, pairs))  16.5 us
    pallas_call x12, Pallas kernels, call(): pl.pallas_call(kernel, name=name, out_shape=[s if isinstance(s, jax.Shape...  10.7 us
    ppermute x6, starting transfers between devices, pair_exchange(): return (lax.ppermute(first, axis, near), lax.ppermute(second, axis, far))  8.92 us
    ppermute x6, waiting for transfers between devices, pair_exchange(): return (lax.ppermute(first, axis, near), lax.ppermute(second, axis, far))  1.68 us
    ppermute x5, starting transfers between devices, gather_levels(): group.append(lax.ppermute(payload, axis, pairs))  1.16 us
  transfers between devices with their start and end apart: 11, of which 6 were waited for; matrix products, arithmetic and copies ran while one was open for 0% of the time, Pallas kernels for 18%

profile of v2, /device:TPU:0, one launch (start us, length us, event | category | flops | bytes accessed | tf_op | source)
XLA Modules:
  0.0 40.6 jit_solution(431578874768489983)
XLA Ops:
  0.6 1.5 %faces.1 = (f32[8,128,128]{2,1,0:T(8,128)S(1)}, s32[8,128,128]{2,1,0:T(8,128)S(1)}, f32[128,128]{1,0:T(8,128)S(1)}, f32[16,16,128]{2,1,0:T(8,128)S(1)}, f32[16,1...) custom-call(f32[8,128,128]{2,1,0:T(8,128)} %bitcast.6, s32[8,128,128]{2,1,0:T(8,128)} %bitcast.7, ...), custom_call_target="tpu_custom_call" | custom-call | flops 20000000 | bytes 1048576 | tf_op jit(solution)/shard_map/faces/pallas_call | solution.py:22
  2.1 3.0 %collective-permute-start = (f32[16,16,128]{2,1,0:T(8,128)S(1)}, f32[16,16,128]{2,1,0:T(8,128)S(1)}, u32[]{:S(2)}, u32[]{:S(2)}) collective-permute-start(f32[16,16,128]{2,1,0:T(8,128)S(1)} %get-tuple-element.39), channel_id=1, source_target_pairs={{0,4},{4,0},{8,12},{12,8},{16,20},{20,16},{24,28},{28,24},{1,5},{5... | collective-permute-start | bytes 393224 | tf_op jit(solution)/shard_map/ppermute | solution.py:587
  5.1 3.6 %collective-permute-start.1 = (f32[16,16,128]{2,1,0:T(8,128)S(1)}, f32[16,16,128]{2,1,0:T(8,128)S(1)}, u32[]{:S(2)}, u32[]{:S(2)}) collective-permute-start(f32[16,16,128]{2,1,0:T(8,128)S(1)} %get-tuple-element.40), channel_id=1, source_target_pairs={{0,28},{4,8},{8,4},{12,16},{16,12},{20,24},{24,20},{28,0},{1,29},{... | collective-permute-start | bytes 393224 | tf_op jit(solution)/shard_map/ppermute | solution.py:587
  8.7 0.0 collective-permute-start.2
  8.7 1.6 %collective-permute-start.3 = (f32[17,8,128]{2,1,0:T(8,128)S(1)}, f32[17,8,128]{2,1,0:T(8,128)S(1)}, u32[]{:S(2)}, u32[]{:S(2)}) collective-permute-start(f32[17,8,128]{2,1,0:T(8,128)S(1)} %get-tuple-element.42), channel_id=1, source_target_pairs={{0,3},{1,2},{2,1},{3,0},{4,7},{5,6},{6,5},{7,4},{8,11},{9,10},{10,... | collective-permute-start | bytes 208904 | tf_op jit(solution)/shard_map/ppermute | solution.py:587
  10.3 5.2 %interior.1 = (f32[8,128,128]{2,1,0:T(8,128)S(1)}, f32[128,128]{1,0:T(8,128)S(1)}, f32[16,128]{1,0:T(8,128)S(1)}, f32[8,128]{1,0:T(8,128)S(1)}) custom-call(f32[8,128,128]{2,1,0:T(8,128)S(1)} %get-tuple-element.33.frac, s32[8,128,128]{2,1,0:T(8,128)S(1)} %get-tuple-element.34.ids, f32[128,128]{1,0:T(8,128)S(1)} %get-tuple-element.35.conc, s32[16,16]{1,0:T(8,128)} %rest_0_.1, ...), custom_call_target="tpu_custom_call" | custom-call | flops 20000000 | bytes 1048576 | tf_op jit(solution)/shard_map/interior/pallas_call | solution.py:22
  15.6 0.0 collective-permute-done.2.y_a
  15.6 0.0 collective-permute-done.3.y_b
  15.6 0.0 collective-permute-done.x_a
  15.6 0.0 collective-permute-done.1.x_b
  15.6 1.0 %outer.1 = (f32[8,128,128]{2,1,0:T(8,128)S(1)}, f32[128,128]{1,0:T(8,128)S(1)}, f32[8,128]{1,0:T(8,128)S(1)}, f32[8,128]{1,0:T(8,128)S(1)}) custom-call(f32[8,128,128]{2,1,0:T(8,128)S(1)} %get-tuple-element.36.new_in, f32[128,128]{1,0:T(8,128)S(1)} %get-tuple-element.37.diff_in, ...), custom_call_target="tpu_custom_call", output_to_operand_aliasing={{0}: (0, {}), {1}: (1, {})} | custom-call | flops 20000000 | bytes 1048576 | tf_op jit(solution)/shard_map/outer/pallas_call | solution.py:22
  16.6 0.1 collective-permute-start.4
  16.7 0.6 %collective-permute-start.5 = (f32[8,128]{1,0:T(8,128)S(1)}, f32[8,128]{1,0:T(8,128)S(1)}, u32[]{:S(2)}, u32[]{:S(2)}) collective-permute-start(f32[8,128]{1,0:T(8,128)S(1)} %get-tuple-element.52), channel_id=1, source_target_pairs={{0,3},{1,2},{2,1},{3,0},{4,7},{5,6},{6,5},{7,4},{8,11},{9,10},{10,... | collective-permute-start | bytes 12296 | tf_op jit(solution)/shard_map/ppermute | solution.py:587
  17.3 0.8 %commit.1._ = f32[8,128,128]{2,1,0:T(8,128)} custom-call(f32[8,128,128]{2,1,0:T(8,128)S(1)} %get-tuple-element.44.new), custom_call_target="tpu_custom_call" | custom-call | flops 20000000 | bytes 1048576 | tf_op jit(solution)/shard_map/commit/pallas_call | solution.py:635
  18.1 0.0 collective-permute-done.4.halo_a
  18.2 1.7 %collective-permute-done.5.halo_b = f32[8,128]{1,0:T(8,128)S(1)} collective-permute-done((f32[8,128]{1,0:T(8,128)S(1)}, f32[8,128]{1,0:T(8,128)S(1)}, u32[]{:S(2)}, u32[]{:S(2)}) %collective-permute-start.5) | collective-permute-done | bytes 4128 | tf_op jit(solution)/shard_map/ppermute | solution.py:587
  19.8 0.2 flux_x.1
  20.0 0.1 collective-permute-start.6
  20.1 4.2 %collective-permute-done.6.refs_1_ = f32[7,16,128]{2,1,0:T(8,128)S(1)} collective-permute-done((f32[7,16,128]{2,1,0:T(8,128)S(1)}, f32[7,16,128]{2,1,0:T(8,128)S(1)}, u32[]{:S(2)}, u32[]{:S(2)}) %collective-permute-start.6) | collective-permute-done | bytes 57376 | tf_op jit(solution)/shard_map/ppermute | solution.py:393
  24.4 0.1 collective-permute-start.7
  24.5 4.2 %collective-permute-done.7.refs_1_.refs_3_ = f32[7,16,128]{2,1,0:T(8,128)S(1)} collective-permute-done((f32[7,16,128]{2,1,0:T(8,128)S(1)}, f32[7,16,128]{2,1,0:T(8,128)S(1)}, u32[]{:S(2)}, u32[]{:S(2)}) %collective-permute-start.7) | collective-permute-done | bytes 57376 | tf_op jit(solution)/shard_map/ppermute | solution.py:393
  28.6 0.4 collective-permute-start.8
  29.0 0.9 %coefficients_z.1 = (f32[16,8,128]{2,1,0:T(8,128)S(1)}, f32[16,8,128]{2,1,0:T(8,128)S(1)}, f32[7,16,8,128]{3,2,1,0:T(8,128)S(1)}, f32[7,16,8,128]{3,2,1,0:T(8,128)S(1)}, f32[7,16,8,128]{3,2,1,0:T(8,128)S(1)}) custom-call(f32[128,128]{1,0:T(8,128)S(1)} %get-tuple-element.45.diff, f32[128,128]{1,0:T(8,128)S(1)} %get-tuple-element.35.conc), custom_call_target="tpu_custom_call" | custom-call | flops 20000000 | bytes 1048576 | tf_op jit(solution)/shard_map/coefficients_z/pallas_call | solution.py:22
  30.0 0.1 inner_x.1
  30.1 3.8 %collective-permute-done.8.refs_5_ = f32[7,16,128]{2,1,0:T(8,128)S(1)} collective-permute-done((f32[7,16,128]{2,1,0:T(8,128)S(1)}, f32[7,16,128]{2,1,0:T(8,128)S(1)}, u32[]{:S(2)}, u32[]{:S(2)}) %collective-permute-start.8) | collective-permute-done | bytes 57376 | tf_op jit(solution)/shard_map/ppermute | solution.py:393
  33.8 0.2 flux_y.1
  34.1 0.1 collective-permute-start.9
  34.1 1.2 %collective-permute-done.9.refs_1_ = f32[7,8,128]{2,1,0:T(8,128)S(1)} collective-permute-done((f32[7,8,128]{2,1,0:T(8,128)S(1)}, f32[7,8,128]{2,1,0:T(8,128)S(1)}, u32[]{:S(2)}, u32[]{:S(2)}) %collective-permute-start.9) | collective-permute-done | bytes 28704 | tf_op jit(solution)/shard_map/ppermute | solution.py:393
  35.4 0.6 %collective-permute-start.10 = (f32[7,8,128]{2,1,0:T(8,128)S(1)}, f32[7,8,128]{2,1,0:T(8,128)S(1)}, u32[]{:S(2)}, u32[]{:S(2)}) collective-permute-start(f32[7,8,128]{2,1,0:T(8,128)S(1)} %join_gy.1.refs_2_), channel_id=1, source_target_pairs={{0,2},{1,3},{2,0},{3,1},{4,6},{5,7},{6,4},{7,5},{8,10},{9,11},{10,... | collective-permute-start | bytes 86024 | tf_op jit(solution)/shard_map/ppermute | solution.py:393
  35.9 0.2 inner_y.1
  36.1 3.2 %collective-permute-done.10.refs_3_ = f32[7,8,128]{2,1,0:T(8,128)S(1)} collective-permute-done((f32[7,8,128]{2,1,0:T(8,128)S(1)}, f32[7,8,128]{2,1,0:T(8,128)S(1)}, u32[]{:S(2)}, u32[]{:S(2)}) %collective-permute-start.10) | collective-permute-done | bytes 28704 | tf_op jit(solution)/shard_map/ppermute | solution.py:393
  39.3 1.3 %last.1 = f32[128,128]{1,0:T(8,128)} custom-call(f32[16,8,128]{2,1,0:T(8,128)S(1)} %get-tuple-element.46._.applied, f32[16,8,128]{2,1,0:T(8,128)S(1)} %get-tuple-element.47.start, f32[7,16,8,128]{3,2,1,0:T(8,128)S(1)} %get-tuple-element.48.left, f32[7,16,8,128]{3,2,1,0:T(8,128)S(1)} %get-tuple-element.49.right, ...), custom_call_target="tpu_custom_call" | custom-call | flops 20000000 | bytes 1048576 | tf_op jit(solution)/shard_map/last/pallas_call | solution.py:22
  (3 shorter events, 0.1 us)
Async XLA Ops:
  2.1 13.5 %collective-permute-start = (f32[16,16,128]{2,1,0:T(8,128)S(1)}, f32[16,16,128]{2,1,0:T(8,128)S(1)}, u32[]{:S(2)}, u32[]{:S(2)}) collective-permute-start(f32[16,16,128]{2,1,0:T(8,128)S(1)} %get-tuple-element.39), channel_id=1, source_target_pairs={{0,4},{4,0},{8,12},{12,8},{16,20},{20,16},{24,28},{28,24},{1,5},{5... | collective-permute-start | bytes 393224 | tf_op jit(solution)/shard_map/ppermute | solution.py:587
  5.1 10.5 %collective-permute-start.1 = (f32[16,16,128]{2,1,0:T(8,128)S(1)}, f32[16,16,128]{2,1,0:T(8,128)S(1)}, u32[]{:S(2)}, u32[]{:S(2)}) collective-permute-start(f32[16,16,128]{2,1,0:T(8,128)S(1)} %get-tuple-element.40), channel_id=1, source_target_pairs={{0,28},{4,8},{8,4},{12,16},{16,12},{20,24},{24,20},{28,0},{1,29},{... | collective-permute-start | bytes 393224 | tf_op jit(solution)/shard_map/ppermute | solution.py:587
  8.7 6.8 %collective-permute-start.2 = (f32[17,8,128]{2,1,0:T(8,128)S(1)}, f32[17,8,128]{2,1,0:T(8,128)S(1)}, u32[]{:S(2)}, u32[]{:S(2)}) collective-permute-start(f32[17,8,128]{2,1,0:T(8,128)S(1)} %get-tuple-element.41), channel_id=1, source_target_pairs={{0,1},{1,0},{2,3},{3,2},{4,5},{5,4},{6,7},{7,6},{8,9},{9,8},{10,11... | collective-permute-start | bytes 208904 | tf_op jit(solution)/shard_map/ppermute | solution.py:587
  8.7 6.9 %collective-permute-start.3 = (f32[17,8,128]{2,1,0:T(8,128)S(1)}, f32[17,8,128]{2,1,0:T(8,128)S(1)}, u32[]{:S(2)}, u32[]{:S(2)}) collective-permute-start(f32[17,8,128]{2,1,0:T(8,128)S(1)} %get-tuple-element.42), channel_id=1, source_target_pairs={{0,3},{1,2},{2,1},{3,0},{4,7},{5,6},{6,5},{7,4},{8,11},{9,10},{10,... | collective-permute-start | bytes 208904 | tf_op jit(solution)/shard_map/ppermute | solution.py:587
  16.6 1.5 %collective-permute-start.4 = (f32[8,128]{1,0:T(8,128)S(1)}, f32[8,128]{1,0:T(8,128)S(1)}, u32[]{:S(2)}, u32[]{:S(2)}) collective-permute-start(f32[8,128]{1,0:T(8,128)S(1)} %get-tuple-element.51), channel_id=1, source_target_pairs={{0,1},{1,0},{2,3},{3,2},{4,5},{5,4},{6,7},{7,6},{8,9},{9,8},{10,11... | collective-permute-start | bytes 12296 | tf_op jit(solution)/shard_map/ppermute | solution.py:587
  16.7 3.1 %collective-permute-start.5 = (f32[8,128]{1,0:T(8,128)S(1)}, f32[8,128]{1,0:T(8,128)S(1)}, u32[]{:S(2)}, u32[]{:S(2)}) collective-permute-start(f32[8,128]{1,0:T(8,128)S(1)} %get-tuple-element.52), channel_id=1, source_target_pairs={{0,3},{1,2},{2,1},{3,0},{4,7},{5,6},{6,5},{7,4},{8,11},{9,10},{10,... | collective-permute-start | bytes 12296 | tf_op jit(solution)/shard_map/ppermute | solution.py:587
  20.0 4.3 %collective-permute-start.6 = (f32[7,16,128]{2,1,0:T(8,128)S(1)}, f32[7,16,128]{2,1,0:T(8,128)S(1)}, u32[]{:S(2)}, u32[]{:S(2)}) collective-permute-start(f32[7,16,128]{2,1,0:T(8,128)S(1)} %get-tuple-element.58.refs_0_), channel_id=1, source_target_pairs={{0,4},{4,0},{8,12},{12,8},{16,20},{20,16},{24,28},{28,24},{1,5},{5... | collective-permute-start | bytes 172040 | tf_op jit(solution)/shard_map/ppermute | solution.py:393
  24.4 4.2 %collective-permute-start.7 = (f32[7,16,128]{2,1,0:T(8,128)S(1)}, f32[7,16,128]{2,1,0:T(8,128)S(1)}, u32[]{:S(2)}, u32[]{:S(2)}) collective-permute-start(f32[7,16,128]{2,1,0:T(8,128)S(1)} %join_gx.2.refs_0_.refs_2_), channel_id=1, source_target_pairs={{0,8},{4,12},{8,0},{12,4},{16,24},{20,28},{24,16},{28,20},{1,9},{5... | collective-permute-start | bytes 172040 | tf_op jit(solution)/shard_map/ppermute | solution.py:393
  28.6 5.2 %collective-permute-start.8 = (f32[7,16,128]{2,1,0:T(8,128)S(1)}, f32[7,16,128]{2,1,0:T(8,128)S(1)}, u32[]{:S(2)}, u32[]{:S(2)}) collective-permute-start(f32[7,16,128]{2,1,0:T(8,128)S(1)} %join_gx.3.refs_4_), channel_id=1, source_target_pairs={{0,16},{4,20},{8,24},{12,28},{16,0},{20,4},{24,8},{28,12},{1,17},{... | collective-permute-start | bytes 172040 | tf_op jit(solution)/shard_map/ppermute | solution.py:393
  34.1 1.3 %collective-permute-start.9 = (f32[7,8,128]{2,1,0:T(8,128)S(1)}, f32[7,8,128]{2,1,0:T(8,128)S(1)}, u32[]{:S(2)}, u32[]{:S(2)}) collective-permute-start(f32[7,8,128]{2,1,0:T(8,128)S(1)} %get-tuple-element.63.refs_0_), channel_id=1, source_target_pairs={{0,1},{1,0},{2,3},{3,2},{4,5},{5,4},{6,7},{7,6},{8,9},{9,8},{10,11... | collective-permute-start | bytes 86024 | tf_op jit(solution)/shard_map/ppermute | solution.py:393
  35.4 3.9 %collective-permute-start.10 = (f32[7,8,128]{2,1,0:T(8,128)S(1)}, f32[7,8,128]{2,1,0:T(8,128)S(1)}, u32[]{:S(2)}, u32[]{:S(2)}) collective-permute-start(f32[7,8,128]{2,1,0:T(8,128)S(1)} %join_gy.1.refs_2_), channel_id=1, source_target_pairs={{0,2},{1,3},{2,0},{3,1},{4,6},{5,7},{6,4},{7,5},{8,10},{9,11},{10,... | collective-permute-start | bytes 86024 | tf_op jit(solution)/shard_map/ppermute | solution.py:393

commit v3 on v2

--- a/solution.py
+++ b/solution.py
@@ -49,12 +49,9 @@
     )
 
 
-def scalar_table(ref, shape):
-    lane = lax.broadcasted_iota(jnp.int32, shape, 1)
-    table = jnp.zeros(shape, jnp.float32)
-    for k in range(ref.shape[0]):
-        table = jnp.where(lane == k, ref[k], table)
-    return table
+def lane_table(ref, nz):
+    row = jnp.concatenate([ref[...]] * (nz // ref.shape[1]), axis=1)
+    return jnp.broadcast_to(row, (SUB, nz))
 
 
 def even(axis):
@@ -72,67 +69,116 @@
 
 
 def pick_slots(ids, rows):
-    picked = [jnp.zeros(ids[0].shape, jnp.float32) for _ in ids]
-    for phase, row in enumerate(rows):
-        picked = [jnp.where(i == phase, row, t) for i, t in zip(ids, picked)]
+    rows = list(rows)
+    bits = range((len(rows) - 1).bit_length())
+    picked = []
+    for slot_id in ids:
+        level = rows
+        for bit in bits:
+            odd = (slot_id & (1 << bit)) != 0
+            level = [
+                jnp.where(odd, level[k + 1], level[k]) if k + 1 < len(level) else level[k]
+                for k in range(0, len(level), 2)
+            ]
+        picked.append(level[0])
     return picked
 
 
-def exchange(level, ids, tables, phases, source=None):
-    width = tables.shape[1]
-    per_row = width // phases
-    count = tables.shape[0] // SUB
-    lane_of = [lax.rem(i, per_row) * phases if per_row & (per_row - 1) else (i & (per_row - 1)) * phases for i in ids]
+def pair_base(phase, phases):
+    return phase * (2 * phases - 3 - phase) // 2 - 1
+
+
+def pair_table(pair_class, mobility, phases, nz):
+    wide = jnp.concatenate([pair_class[...]] * (nz // phases), axis=1)
+    options = lane_table(mobility, nz)
+    values = jnp.concatenate(
+        [lookup(options, wide[k : k + SUB]) for k in range(0, phases, SUB)], axis=0
+    )
+    lane = lax.broadcasted_iota(jnp.int32, (SUB, nz), 1)
+    table = jnp.zeros((SUB, nz), jnp.float32)
+    for p in range(phases - 1):
+        base = pair_base(p, phases)
+        row = jnp.broadcast_to(values[p : p + 1, :], (SUB, nz))
+        shift = base % phases
+        if shift:
+            row = pltpu.roll(row, shift, 1)
+        table = jnp.where((lane > base + p) & (lane < base + phases), row, table)
+    return table
+
+
+def pairs_of(count):
+    return [(a, b) for a in range(count) for b in range(a + 1, count)]
+
+
+def mobilities(ids, table, phases):
+    base = [lax.shift_right_arithmetic(i * (2 * phases - 3 - i), 1) - 1 for i in ids]
+    return [
+        lookup(table, jnp.minimum(base[a], base[b]) + jnp.maximum(ids[a], ids[b]))
+        for a, b in pairs_of(len(ids))
+    ]
+
+
+def exchange(level, mobs, source=None):
     sums = [jnp.zeros(level[0].shape, jnp.float32) for _ in level]
-    for a in range(len(level)):
-        above = [ids[a] >= t * per_row for t in range(1, count)]
-        for b in range(a + 1, len(level)):
-            index = lane_of[a] + ids[b]
-            mob = lookup(tables[0:SUB], index)
-            for t in range(1, count):
-                mob = jnp.where(above[t - 1], lookup(tables[t * SUB : (t + 1) * SUB], index), mob)
-            term = level[a] - level[b]
-            if source is not None:
-                frac, drive, conc = source
-                term = term + (conc * frac[a]) * (frac[b] * (drive[a] - drive[b]))
-            term = mob * term
-            sums[a] = sums[a] + term
-            sums[b] = sums[b] - term
+    for (a, b), mob in zip(pairs_of(len(level)), mobs):
+        term = level[a] - level[b]
+        if source is not None:
+            pulled, frac, drive = source
+            term = term + pulled[a] * (frac[b] * (drive[a] - drive[b]))
+        term = mob * term
+        sums[a] = sums[a] + term
+        sums[b] = sums[b] - term
     return sums
 
 
-def faces_kernel(phases, shape, frac_far, ids_far, conc_far, frac, ids, conc, x_a, x_b, y_a, y_b, sems):
+def plane_rows(shape, upper):
     nx, ny, _ = shape
-    slots = frac.shape[0]
-    half = slots // 2
+    return pl.ds(pl.multiple_of(jnp.where(upper, (nx - 1) * ny, 0), SUB), ny)
+
+
+def first_kernel(phases, shape, *refs):
+    nx, ny, nz = shape
+    count = (len(refs) - 5) // 2
+    far, near, outs, held_far, sems = refs[:count], refs[count:-5], refs[-5:-3], refs[-3:-1], refs[-1]
+    right = even("gx")
     copies = []
-    for k, (far, near) in enumerate(
-        [
-            (frac_far.at[:half], frac.at[:half]),
-            (ids_far.at[:half], ids.at[:half]),
-            (frac_far.at[half:], frac.at[half:]),
-            (ids_far.at[half:], ids.at[half:]),
-            (conc_far, conc),
-        ]
-    ):
-        copies.append(pltpu.make_async_copy(far, near, sems.at[k]))
-        copies[-1].start()
+    for k, upper in enumerate((right, jnp.logical_not(right))):
+        rows = plane_rows(shape, upper)
+        for source, target in zip(far[:2], held_far):
+            copies.append(
+                pltpu.make_async_copy(source.at[:, rows, :], target.at[k], sems.at[len(copies)])
+            )
+    for source, target in zip(far, near):
+        half = source.shape[0] // 2 if len(source.shape) == 3 else 0
+        for piece in ([slice(0, half), slice(half, None)] if half else [slice(None)]):
+            copies.append(
+                pltpu.make_async_copy(source.at[piece], target.at[piece], sems.at[len(copies)])
+            )
     for copy in copies:
-        copy.wait()
-    right = even("gx")
-    for out, upper in ((x_a, right), (x_b, jnp.logical_not(right))):
-        base = jnp.where(upper, (nx - 1) * ny, 0)
+        copy.start()
+    frac, ids = held_far
+    slots = frac.shape[1]
+    for k, out in enumerate(outs):
+        for copy in copies[2 * k : 2 * k + 2]:
+            copy.wait()
         for part in range(ny // SUB):
-            rows = pl.ds(pl.multiple_of(base + part * SUB, SUB), SUB)
+            rows = slice(part * SUB, (part + 1) * SUB)
             held = pick_rows(
-                [ids[s, rows, :] for s in range(slots)],
-                [frac[s, rows, :] for s in range(slots)],
+                [ids[k, s, rows, :] for s in range(slots)],
+                [frac[k, s, rows, :] for s in range(slots)],
                 phases,
             )
             for phase in range(phases):
-                out[phase, part * SUB : (part + 1) * SUB, :] = held[phase]
+                out[phase, rows, :] = held[phase]
+    for copy in copies[4:]:
+        copy.wait()
+
+
+def faces_kernel(phases, shape, frac, ids, conc, y_a, y_b):
+    nx, ny, _ = shape
+    slots = frac.shape[0]
     up = even("gy")
-    for out, upper in ((y_a, up), (y_b, jnp.logical_not(up))):
+    for out, upper in ((y_b, jnp.logical_not(up)), (y_a, up)):
         rows = pl.ds(jnp.where(upper, ny - 1, 0), nx, stride=ny)
         held = pick_rows(
             [ids[s, rows, :] for s in range(slots)],
@@ -144,29 +190,20 @@
         out[phases] = conc[rows, :]
 
 
-def interior_kernel(
-    phases, shape, frac, ids, conc, *rest
-):
-    new_out, diff_out, table_out, diff_table_out, dense, pair_class, mobility, drive, diffusivity, sems = rest[4:]
-    copies = [
-        pltpu.make_async_copy(far, near, sems.at[k])
-        for k, (far, near) in enumerate(zip(rest[:4], (pair_class, mobility, drive, diffusivity)))
-    ]
-    for copy in copies:
-        copy.start()
+def build_kernel(phases, shape, frac, ids, pair_class, mobility, dense, mob_out):
     nx, ny, nz = shape
     slots = frac.shape[0]
     pitch = ny + 2 * SUB
     parts = ny // SUB
-    per_row = nz // phases
-    count = -(-phases // per_row)
+    table = pair_table(pair_class, mobility, phases, nz)
     nothing = jnp.zeros((SUB, nz), jnp.float32)
 
     def clear(phase, carry):
         for plane in range(nx + 2):
             for part in range(parts + 2):
                 if plane in (0, nx + 1) or part in (0, parts + 1):
-                    dense[phase, plane * pitch + part * SUB : plane * pitch + (part + 1) * SUB, :] = nothing
+                    at = plane * pitch + part * SUB
+                    dense[phase, at : at + SUB, :] = nothing
         return carry
 
     lax.fori_loop(0, phases, clear, 0)
@@ -174,89 +211,128 @@
     def build(x, carry):
         for part in range(parts):
             rows = pl.ds(pl.multiple_of(x * ny, SUB) + part * SUB, SUB)
-            held = pick_rows(
-                [ids[s, rows, :] for s in range(slots)],
-                [frac[s, rows, :] for s in range(slots)],
-                phases,
-            )
+            slot_ids = [ids[s, rows, :] for s in range(slots)]
+            for k, mob in enumerate(mobilities(slot_ids, table, phases)):
+                mob_out[k, rows, :] = mob
+            held = pick_rows(slot_ids, [frac[s, rows, :] for s in range(slots)], phases)
             into = pl.ds(pl.multiple_of((x + 1) * pitch, SUB) + (part + 1) * SUB, SUB)
             for phase in range(phases):
                 dense[phase, into, :] = held[phase]
         return carry
 
-    lax.fori_loop(0, nx, build, 0)
-    for copy in copies:
-        copy.wait()
-    lane = lax.broadcasted_iota(jnp.int32, (per_row, nz), 1)
-    row = lax.broadcasted_iota(jnp.int32, (per_row, nz), 0)
-    for t in range(count):
-        block = pair_class[t * per_row : (t + 1) * per_row, :]
-        wide = jnp.concatenate([block] * per_row, axis=1)
-        values = jnp.zeros(wide.shape, jnp.float32)
-        for k in range(mobility.shape[0]):
-            values = jnp.where(wide == k, mobility[k], values)
-        line = jnp.sum(
-            jnp.where((lane >= row * phases) & (lane < (row + 1) * phases), values, 0.0),
-            axis=0,
-            keepdims=True,
-        )
-        table_out[t * SUB : (t + 1) * SUB, :] = jnp.broadcast_to(line, (SUB, nz))
-    drive_table = scalar_table(drive, (SUB, nz))
-    diff_table = scalar_table(diffusivity, (SUB, nz))
-    diff_table_out[...] = diff_table
+    lax.fori_loop(0, nx, build, 0, unroll=2 if nx % 2 == 0 else 1)
+
+
+def tables_of(phases, drive, diffusivity, nz):
+    return lane_table(drive, nz), lane_table(diffusivity, nz)
+
+
+def renew(laplacian, rows, mobs, frac, ids, conc, tables):
+    slots = frac.shape[0]
+    slot_ids = [ids[s, rows, :] for s in range(slots)]
+    slot_drive, slot_diff = [], []
+    for i in slot_ids:
+        slot_drive.append(lookup(tables[0], i))
+        slot_diff.append(lookup(tables[1], i))
+    curvature = pick_slots(slot_ids, laplacian)
+    slot_frac = [frac[s, rows, :] for s in range(slots)]
+    level = [c + KAPPA * f for c, f in zip(curvature, slot_frac)]
+    scaled = DRIVE * conc[rows, :]
+    pulled = [scaled * f for f in slot_frac]
+    sums = exchange(
+        level, [mobs[k, rows, :] for k in range(mobs.shape[0])], (pulled, slot_frac, slot_drive)
+    )
+    new = [f + t for f, t in zip(slot_frac, sums)]
+    diffus = jnp.ones(new[0].shape, jnp.float32)
+    for value, d in zip(new, slot_diff):
+        diffus = diffus + value * value * d
+    return new, diffus
+
+
+def laplacian_at(dense, phases, nz, at, pitch):
+    for phase in range(phases):
+        centre = dense[phase, at(0), :]
+        along_x = dense[phase, at(pitch), :] + dense[phase, at(-pitch), :]
+        along_y = dense[phase, at(1), :] + dense[phase, at(-1), :]
+        along_z = pltpu.roll(centre, nz - 1, 1) + pltpu.roll(centre, 1, 1)
+        yield (along_x + along_y + along_z) - 6.0 * centre
+
+
+def interior_kernel(
+    phases, shape, planes, dense, mobs, frac, ids, conc, drive, diffusivity, *refs
+):
+    nx, ny, nz = shape
+    new_out, diff_out = refs[-2:]
+    pitch = ny + 2 * SUB
+    tables = tables_of(phases, drive, diffusivity, nz)
 
     def update(x, carry):
-        for part in range(parts):
+        for part in range(ny // SUB):
             rows = pl.ds(pl.multiple_of(x * ny, SUB) + part * SUB, SUB)
-            at = pl.multiple_of((x + 1) * pitch, SUB) + (part + 1) * SUB
-
-            def laplacian():
-                for phase in range(phases):
-                    centre = dense[phase, pl.ds(at, SUB), :]
-                    along_x = dense[phase, pl.ds(at + pitch, SUB), :] + dense[phase, pl.ds(at - pitch, SUB), :]
-                    along_y = dense[phase, pl.ds(at + 1, SUB), :] + dense[phase, pl.ds(at - 1, SUB), :]
-                    along_z = pltpu.roll(centre, nz - 1, 1) + pltpu.roll(centre, 1, 1)
-                    yield (along_x + along_y + along_z) - 6.0 * centre
-
-            slot_ids = [ids[s, rows, :] for s in range(slots)]
-            curvature = pick_slots(slot_ids, laplacian())
-            slot_frac = [frac[s, rows, :] for s in range(slots)]
-            level = [c + KAPPA * f for c, f in zip(curvature, slot_frac)]
-            slot_drive = [lookup(drive_table, i) for i in slot_ids]
-            sums = exchange(
-                level, slot_ids, table_out, phases, (slot_frac, slot_drive, DRIVE * conc[rows, :])
+            base = pl.multiple_of((x + 1) * pitch, SUB) + (part + 1) * SUB
+            laplacian = laplacian_at(
+                dense, phases, nz, lambda shift, base=base: pl.ds(base + shift, SUB), pitch
             )
-            diffus = jnp.ones((SUB, nz), jnp.float32)
-            for s in range(slots):
-                new = slot_frac[s] + sums[s]
-                new_out[s, rows, :] = new
-                diffus = diffus + new * new * lookup(diff_table, slot_ids[s])
+            new, diffus = renew(laplacian, rows, mobs, frac, ids, conc, tables)
+            for s, value in enumerate(new):
+                new_out[s, rows, :] = value
             diff_out[rows, :] = diffus
         return carry
 
-    lax.fori_loop(0, nx, update, 0)
+    lax.fori_loop(planes[0], planes[1], update, 0)
+
+
+def edge_kernel(
+    phases, shape, dense, mobs, frac, ids, conc, drive, diffusivity, x_a, x_b, y_a, y_b, _,
+    face_a, face_b,
+):
+    nx, ny, nz = shape
+    pitch = ny + 2 * SUB
+    tables = tables_of(phases, drive, diffusivity, nz)
+    place = lax.broadcasted_iota(jnp.int32, (nx, nz), 0)
+    at_a = place == jnp.where(even("gx"), nx - 1, 0)
+    at_b = place == jnp.where(even("gx"), 0, nx - 1)
+    up = even("gy")
+    for face, halo, upper in ((face_a, y_a, up), (face_b, y_b, jnp.logical_not(up))):
+        y = jnp.where(upper, ny - 1, 0)
+        inner = laplacian_at(
+            dense,
+            phases,
+            nz,
+            lambda shift, y=y: pl.ds(pitch + SUB + y + shift, nx, stride=pitch),
+            pitch,
+        )
+
+        def whole(inner=inner, halo=halo, y=y):
+            for phase, value in enumerate(inner):
+                row_a = jnp.where(at_a, x_a[phase, pl.ds(y, 1), :], 0.0)
+                row_b = jnp.where(at_b, x_b[phase, pl.ds(y, 1), :], 0.0)
+                yield value + halo[phase] + (row_a + row_b)
+
+        _, diffus = renew(
+            whole(), pl.ds(y, nx, stride=ny), mobs, frac, ids, conc, tables
+        )
+        face[...] = diffus
 
 
 def outer_kernel(
-    phases, shape, new_in, diff_in, table, ids, x_a, x_b, y_a, y_b, diff_table_in,
-    new_out, diff_out, face_a, face_b,
+    phases, shape, new_in, diff_in, mobs, ids, x_a, x_b, y_a, y_b, diffusivity, new_out, diff_out
 ):
     nx, ny, nz = shape
     slots = new_in.shape[0]
-    diff_table = diff_table_in[...]
+    diff_table = lane_table(diffusivity, nz)
     del new_in, diff_in
 
     def add(rows, halo):
         slot_ids = [ids[s, rows, :] for s in range(slots)]
         level = pick_slots(slot_ids, (halo(p) for p in range(phases)))
-        sums = exchange(level, slot_ids, table, phases)
+        sums = exchange(level, [mobs[k, rows, :] for k in range(mobs.shape[0])])
         diffus = jnp.ones(sums[0].shape, jnp.float32)
         for s in range(slots):
             new = new_out[s, rows, :] + sums[s]
             new_out[s, rows, :] = new
             diffus = diffus + new * new * lookup(diff_table, slot_ids[s])
         diff_out[rows, :] = diffus
-        return diffus
 
     right = even("gx")
     for halo, upper in ((x_a, right), (x_b, jnp.logical_not(right))):
@@ -267,9 +343,9 @@
                 lambda p, halo=halo, part=part: halo[p, part * SUB : (part + 1) * SUB, :],
             )
     up = even("gy")
-    for halo, upper, face in ((y_a, up, face_a), (y_b, jnp.logical_not(up), face_b)):
+    for halo, upper in ((y_a, up), (y_b, jnp.logical_not(up))):
         rows = pl.ds(jnp.where(upper, ny - 1, 0), nx, stride=ny)
-        face[...] = add(rows, lambda p, halo=halo: halo[p])
+        add(rows, lambda p, halo=halo: halo[p])
 
 
 def chain_ends(source, face):
@@ -356,52 +432,66 @@
     return own, blocks
 
 
+def view(block, lower):
+    ends = ((block[1], block[4], block[6]), (block[0], block[2], block[5]))
+    return tuple(choose(list(pair), jnp.where(lower, 0, 1)) for pair in zip(*ends))
+
+
 def solve_levels(axis, levels, refs):
-    position = 0
-    groups = []
-    for level in levels:
-        groups.append(members(axis, level, refs[position : position + level[1]]))
-        position += level[1]
     zero = jnp.zeros(refs[0].shape[1:], jnp.float32)
     lower, upper = zero, zero
-    for own, blocks in groups[::-1]:
-        between = fluxes(blocks, lower, upper)
-        lower, upper = choose(between[:-1], own), choose(between[1:], own)
+    for k in range(len(levels) - 1, -1, -1):
+        level, pair = levels[k], refs[2 * k : 2 * k + 2]
+        if pair[1].shape[0] == 3:
+            number = lax.rem(lax.axis_index(axis) // level[0], level[1])
+            own = view(tuple(pair[0][q] for q in range(7)), number == 0)
+            other = tuple(pair[1][q] for q in range(3))
+            face = 0.5 * (own[2] + other[2])
+            flux = face * (other[0] - own[0]) / (1.0 + face * (own[1] + other[1]))
+            lower, upper = choose([zero, -flux], number), choose([flux, zero], number)
+        else:
+            number, blocks = members(axis, level, pair)
+            between = fluxes(blocks, lower, upper)
+            lower, upper = choose(between[:-1], number), choose(between[1:], number)
     return lower, upper
 
 
-def join_kernel(axis, level, *refs):
-    out = refs[-1]
-    _, blocks = members(axis, level, refs[:-1])
-    total = blocks[0]
-    for block in blocks[1:]:
-        total = join(total, block)
+def join_kernel(axis, level, above, *refs):
+    pair, outs = refs[:2], refs[-1:] if above is None else refs[-2:]
+    _, blocks = members(axis, level, pair)
+    total = join(*blocks)
     for q in range(7):
-        out[q] = total[q]
-
-
-def gather_levels(axis, payload, shape):
+        outs[0][q] = total[q]
+    if above is not None:
+        short = view(total, lax.rem(lax.axis_index(axis) // above, 2) == 0)
+        for q in range(3):
+            outs[1][q] = short[q]
+
+
+def gather_levels(axis, payload, shape, after=None):
     count = lax.axis_size(axis)
     levels, refs = [], []
-    stride = 1
+    stride, send = 1, payload
     while stride < count:
-        radix = 2
-        level = (stride, radix)
-        group = [payload]
-        for k in range(1, radix):
-            pairs = [(i, i ^ (k * stride)) for i in range(count)]
-            group.append(lax.ppermute(payload, axis, pairs))
-        levels.append(level)
-        refs += group
-        stride *= radix
+        pairs = [(i, i ^ stride) for i in range(count)]
+        levels.append((stride, 2))
+        refs += [payload, lax.ppermute(send, axis, pairs)]
+        stride *= 2
         if stride < count:
-            (payload,) = call(
-                functools.partial(join_kernel, axis, level), "join_" + axis, [shape], group
+            above = stride if 2 * stride == count else None
+            ins = refs[-2:] + ([after] if after is not None else [])
+            outs = call(
+                functools.partial(join_kernel, axis, levels[-1], above),
+                "join_" + axis,
+                [shape] + ([(3, *shape[1:])] if above else []),
+                ins,
+                far=range(2, len(ins)),
             )
+            payload, send, after = outs[0], outs[-1], None
     return levels, refs
 
 
-def flux_x_kernel(shape, diff, conc, y_a, y_b, halo_a, halo_b, _, payload, source, applied):
+def flux_x_kernel(shape, diff, conc, y_a, y_b, halo_a, halo_b, payload, source, applied):
     nx, ny, nz = shape
     up = even("gy")
     place = lax.axis_index("gy")
@@ -580,11 +670,15 @@
     copy.wait()
 
 
-def pair_exchange(axis, first, second):
+def exchange_near(axis, array):
     count = lax.axis_size(axis)
-    near = [(i, i ^ 1) for i in range(count)]
-    far = [(i, (i - 1) % count if i % 2 == 0 else (i + 1) % count) for i in range(count)]
-    return lax.ppermute(first, axis, near), lax.ppermute(second, axis, far)
+    return lax.ppermute(array, axis, [(i, i ^ 1) for i in range(count)])
+
+
+def exchange_far(axis, array):
+    count = lax.axis_size(axis)
+    pairs = [(i, (i - 1) % count if i % 2 == 0 else (i + 1) % count) for i in range(count)]
+    return lax.ppermute(array, axis, pairs)
 
 
 def body(phase_frac, phase_ids, conc, pair_class, mobility, drive, diffusivity):
@@ -597,41 +691,72 @@
     ids = far_away(phase_ids.reshape(slots, cells, nz))
     field = far_away(conc.reshape(cells, nz))
 
-    frac, ids, field, x_a, x_b, y_a, y_b = call(
+    small = [pair_class] + [v.reshape(1, -1) for v in (mobility, drive, diffusivity)]
+    ins = [frac, ids, field] + [far_away(v) for v in small]
+    frac, ids, field, classes, mobility, drive, diffusivity, x_a, x_b = call(
+        functools.partial(first_kernel, phases, shape),
+        "first",
+        [jax.ShapeDtypeStruct(v.shape, v.dtype) for v in ins] + [(phases, ny, nz)] * 2,
+        ins,
+        scratch=[
+            pltpu.VMEM((2, slots, ny, nz), jnp.float32),
+            pltpu.VMEM((2, slots, ny, nz), ids.dtype),
+            pltpu.SemaphoreType.DMA((len(ins) + 6,)),
+        ],
+        far=range(len(ins)),
+    )
+    x_a = exchange_near("gx", x_a)
+    x_b = exchange_far("gx", x_b)
+    y_a, y_b = call(
         functools.partial(faces_kernel, phases, shape),
         "faces",
-        [frac.shape, jax.ShapeDtypeStruct(ids.shape, ids.dtype), flat]
-        + [(phases, ny, nz)] * 2
-        + [(phases + 1, nx, nz)] * 2,
+        [(phases + 1, nx, nz)] * 2,
         [frac, ids, field],
-        scratch=[pltpu.SemaphoreType.DMA((5,))],
-        far=(0, 1, 2),
-    )
-    x_a, x_b = pair_exchange("gx", x_a, x_b)
-    y_a, y_b = pair_exchange("gy", y_a, y_b)
-    count = -(-phases // (nz // phases))
-    small = [pair_class, mobility, drive, diffusivity]
-    new, diffus, table, diff_table = call(
-        functools.partial(interior_kernel, phases, shape),
-        "interior",
-        [(slots, cells, nz), flat, (count * SUB, nz), (SUB, nz)],
-        [frac, ids, field] + [far_away(v) for v in small],
-        scratch=[
-            (phases, (nx + 2) * (ny + 2 * SUB), nz),
-            pltpu.VMEM(pair_class.shape, pair_class.dtype),
-        ]
-        + [pltpu.SMEM(v.shape, v.dtype) for v in small[1:]]
-        + [pltpu.SemaphoreType.DMA((4,))],
-        far=(3, 4, 5, 6),
-    )
-    new, diffus, face_a, face_b = call(
+    )
+    y_b = exchange_far("gy", y_b)
+    y_a = exchange_near("gy", y_a)
+    dense, mobs = call(
+        functools.partial(build_kernel, phases, shape),
+        "build",
+        [(phases, (nx + 2) * (ny + 2 * SUB), nz), (len(pairs_of(slots)), cells, nz)],
+        [frac, ids, classes, mobility],
+    )
+    fields = [dense, mobs, frac, ids, field, drive, diffusivity]
+    middle = nx // 2
+    new, diffus = call(
+        functools.partial(interior_kernel, phases, shape, (0, middle)),
+        "interior_low",
+        [(slots, cells, nz), flat],
+        fields,
+    )
+    faces = call(
+        functools.partial(edge_kernel, phases, shape),
+        "edge",
+        [(nx, nz)] * 2,
+        fields + [x_a, x_b, y_a, y_b, diffus],
+    )
+    face_b = exchange_far("gy", faces[1])
+    face_a = exchange_near("gy", faces[0])
+    new, diffus = call(
+        functools.partial(interior_kernel, phases, shape, (middle, nx)),
+        "interior_high",
+        [(slots, cells, nz), flat],
+        fields + [new, diffus, faces[0]],
+        aliases={7: 0, 8: 1},
+    )
+    new, diffus = call(
         functools.partial(outer_kernel, phases, shape),
         "outer",
-        [(slots, cells, nz), flat, (nx, nz), (nx, nz)],
-        [new, diffus, table, ids, x_a, x_b, y_a, y_b, diff_table],
+        [(slots, cells, nz), flat],
+        [new, diffus, mobs, ids, x_a, x_b, y_a, y_b, diffusivity],
         aliases={0: 0, 1: 1},
     )
-    face_a, face_b = pair_exchange("gy", face_a, face_b)
+    payload, source, applied = call(
+        functools.partial(flux_x_kernel, shape),
+        "flux_x",
+        [(7, ny, nz), flat, flat],
+        [diffus, field, y_a, y_b, face_a, face_b],
+    )
     (new,) = pl.pallas_call(
         commit_kernel,
         name="commit",
@@ -642,14 +767,7 @@
         compiler_params=pltpu.CompilerParams(vmem_limit_bytes=12 << 20),
         cost_estimate=pl.CostEstimate(flops=20000000, bytes_accessed=1 << 20, transcendentals=0),
     )(new)
-    payload, source, applied = call(
-        functools.partial(flux_x_kernel, shape),
-        "flux_x",
-        [(7, ny, nz), flat, flat],
-        [diffus, field, y_a, y_b, face_a, face_b, far_away(new)],
-        far=(6,),
-    )
-    levels, refs = gather_levels("gx", payload, (7, ny, nz))
+    levels, refs = gather_levels("gx", payload, (7, ny, nz), far_away(new))
     applied_z, start, left, right, unit = call(
         functools.partial(coefficients_z_kernel, shape),
         "coefficients_z",

time: 40.8 us -> 37.9 us (0.929)
  waiting for transfers between devices: 18.2 us -> 14.7 us
  starting transfers between devices: 10.1 us -> 11.1 us
    ppermute x11, waiting for transfers between devices: 18.2 us -> 14.7 us  [the longest x5 14.1 us: gather_levels(): refs += [payload, lax.ppermute(send, axis, pairs)]]
    ppermute x11, starting transfers between devices: 10.1 us -> 11.1 us  [the longest x3 5.8 us: exchange_far(): return lax.ppermute(array, axis, pairs)]
    pallas_call x12 -> x16, Pallas kernels: 10.7 us -> 10.4 us  [call(): pl.pallas_call(kernel, name=name, out_shape=[s if isinstance(s, jax.Shape...]
  transfers between devices with their start and end apart: 11 -> 11, of which waited for: 6 -> 6; matrix products, arithmetic and copies ran while one was open for 0% -> 0% of each run, Pallas kernels for 18% -> 19%
where the time goes in v3:
time: 37.9 us; the launch traced here: 37.8 us
  waiting for transfers between devices  14.7 us (39%)
  Pallas kernels  11.2 us (30%)
  starting transfers between devices  11.1 us (29%)
  between operations  0.77 us (2%)
    ppermute x5, waiting for transfers between devices, gather_levels(): refs += [payload, lax.ppermute(send, axis, pairs)]  14.1 us
    pallas_call x16, Pallas kernels, call(): pl.pallas_call(kernel, name=name, out_shape=[s if isinstance(s, jax.Shape...  10.4 us
    ppermute x3, starting transfers between devices, exchange_far(): return lax.ppermute(array, axis, pairs)  5.8 us
    ppermute x3, starting transfers between devices, exchange_near(): return lax.ppermute(array, axis, [(i, i ^ 1) for i in range(count)])  3.19 us
    ppermute x5, starting transfers between devices, gather_levels(): refs += [payload, lax.ppermute(send, axis, pairs)]  2.14 us
    pallas_call x1, Pallas kernels, body(): pl.pallas_call(commit_kernel, name='commit', out_shape=[jax.ShapeDtypeStr...  0.8 us
  transfers between devices with their start and end apart: 11, of which 6 were waited for; matrix products, arithmetic and copies ran while one was open for 0% of the time, Pallas kernels for 19%

profile of v3, /device:TPU:0, one launch (start us, length us, event | category | flops | bytes accessed | tf_op | source)
XLA Modules:
  0.0 37.8 jit_solution(11499862930308014791)
XLA Ops:
  0.6 1.5 %first.1 = (f32[8,128,128]{2,1,0:T(8,128)S(1)}, s32[8,128,128]{2,1,0:T(8,128)S(1)}, f32[128,128]{1,0:T(8,128)S(1)}, s32[16,16]{1,0:T(8,128)S(1)}, f32[1,4]{1,0:T...) custom-call(f32[8,128,128]{2,1,0:T(8,128)} %bitcast.9, ...), custom_call_target="tpu_custom_call" | custom-call | flops 20000000 | bytes 1048576 | tf_op jit(solution)/shard_map/first/pallas_call | solution.py:22
  2.1 3.0 %collective-permute-start = (f32[16,16,128]{2,1,0:T(8,128)S(1)}, f32[16,16,128]{2,1,0:T(8,128)S(1)}, u32[]{:S(2)}, u32[]{:S(2)}) collective-permute-start(f32[16,16,128]{2,1,0:T(8,128)S(1)} %get-tuple-element.54), channel_id=1, source_target_pairs={{0,4},{4,0},{8,12},{12,8},{16,20},{20,16},{24,28},{28,24},{1,5},{5... | collective-permute-start | bytes 393224 | tf_op jit(solution)/shard_map/ppermute | solution.py:675
  5.1 3.6 %collective-permute-start.1 = (f32[16,16,128]{2,1,0:T(8,128)S(1)}, f32[16,16,128]{2,1,0:T(8,128)S(1)}, u32[]{:S(2)}, u32[]{:S(2)}) collective-permute-start(f32[16,16,128]{2,1,0:T(8,128)S(1)} %get-tuple-element.55), channel_id=1, source_target_pairs={{0,28},{4,8},{8,4},{12,16},{16,12},{20,24},{24,20},{28,0},{1,29},{... | collective-permute-start | bytes 393224 | tf_op jit(solution)/shard_map/ppermute | solution.py:681
  8.7 0.1 faces.1
  8.8 0.1 collective-permute-start.2
  8.9 1.6 %collective-permute-start.3 = (f32[17,8,128]{2,1,0:T(8,128)S(1)}, f32[17,8,128]{2,1,0:T(8,128)S(1)}, u32[]{:S(2)}, u32[]{:S(2)}) collective-permute-start(f32[17,8,128]{2,1,0:T(8,128)S(1)} %get-tuple-element.57), channel_id=1, source_target_pairs={{0,3},{1,2},{2,1},{3,0},{4,7},{5,6},{6,5},{7,4},{8,11},{9,10},{10,... | collective-permute-start | bytes 208904 | tf_op jit(solution)/shard_map/ppermute | solution.py:681
  10.5 1.9 %build.1 = (f32[16,320,128]{2,1,0:T(8,128)S(1)}, f32[28,128,128]{2,1,0:T(8,128)S(1)}) custom-call(f32[8,128,128]{2,1,0:T(8,128)S(1)} %get-tuple-element.43.frac, s32[8,128,128]{2,1,0:T(8,128)S(1)} %get-tuple-element.44.ids, s32[16,16]{1,0:T(8,128)S(1)} %get-tuple-element.45.pair_class, f32[1,4]{1,0:T(1,128)S(1)} %get-tuple-element.46.mobility), custom_call_target="tpu_custom_call" | custom-call | flops 20000000 | bytes 1048576 | tf_op jit(solution)/shard_map/build/pallas_call | solution.py:22
  12.5 1.3 %interior_low.1 = (f32[8,128,128]{2,1,0:T(8,128)S(1)}, f32[128,128]{1,0:T(8,128)S(1)}) custom-call(f32[16,320,128]{2,1,0:T(8,128)S(1)} %get-tuple-element.47.dense, f32[28,128,128]{2,1,0:T(8,128)S(1)} %get-tuple-element.48.mobs, f32[8,128,128]{2,1,0:T(8,128)S(1)} %get-tuple-element.43.frac, s32[8,128,128]{2,1,0:T(8,128)S(1)} %get-tuple-element.44.ids, ...), custom_call_target="tpu_custom_call" | custom-call | flops 20000000 | bytes 1048576 | tf_op jit(solution)/shard_map/interior_low/pallas_call | solution.py:22
  13.8 0.0 collective-permute-done.2.y_a
  13.8 0.0 collective-permute-done.3.y_b
  13.8 0.0 collective-permute-done.x_a
  13.8 0.0 collective-permute-done.1.x_b
  13.9 0.7 %edge.1 = (f32[8,128]{1,0:T(8,128)S(1)}, f32[8,128]{1,0:T(8,128)S(1)}) custom-call(f32[16,320,128]{2,1,0:T(8,128)S(1)} %get-tuple-element.47.dense, f32[28,128,128]{2,1,0:T(8,128)S(1)} %get-tuple-element.48.mobs, f32[8,128,128]{2,1,0:T(8,128)S(1)} %get-tuple-element.43.frac, s32[8,128,128]{2,1,0:T(8,128)S(1)} %get-tuple-element.44.ids, ...), custom_call_target="tpu_custom_call" | custom-call | flops 20000000 | bytes 1048576 | tf_op jit(solution)/shard_map/edge/pallas_call | solution.py:22
  14.6 0.6 %collective-permute-start.5 = (f32[8,128]{1,0:T(8,128)S(1)}, f32[8,128]{1,0:T(8,128)S(1)}, u32[]{:S(2)}, u32[]{:S(2)}) collective-permute-start(f32[8,128]{1,0:T(8,128)S(1)} %get-tuple-element.68), channel_id=1, source_target_pairs={{0,3},{1,2},{2,1},{3,0},{4,7},{5,6},{6,5},{7,4},{8,11},{9,10},{10,... | collective-permute-start | bytes 12296 | tf_op jit(solution)/shard_map/ppermute | solution.py:681
  15.2 0.1 collective-permute-start.4
  15.3 1.3 %interior_high.1 = (f32[8,128,128]{2,1,0:T(8,128)S(1)}, f32[128,128]{1,0:T(8,128)S(1)}) custom-call(f32[16,320,128]{2,1,0:T(8,128)S(1)} %get-tuple-element.47.dense, f32[28,128,128]{2,1,0:T(8,128)S(1)} %get-tuple-element.48.mobs, f32[8,128,128]{2,1,0:T(8,128)S(1)} %get-tuple-element.43.frac, ...), custom_call_target="tpu_custom_call", output_to_operand_aliasing={{0}: (7, {}), {1}: (8, {})} | custom-call | flops 20000000 | bytes 1048576 | tf_op jit(solution)/shard_map/interior_high/pallas_call | solution.py:22
  16.6 0.5 %outer.1 = (f32[8,128,128]{2,1,0:T(8,128)S(1)}, f32[128,128]{1,0:T(8,128)S(1)}) custom-call(f32[8,128,128]{2,1,0:T(8,128)S(1)} %get-tuple-element.59.new_in, f32[128,128]{1,0:T(8,128)S(1)} %get-tuple-element.60.diff_in, f32[28,128,128]{2,1,0:T(8,128)S(1)} %get-tuple-element.48.mobs, ...), custom_call_target="tpu_custom_call", output_to_operand_aliasing={{0}: (0, {}), {1}: (1, {})} | custom-call | flops 20000000 | bytes 1048576 | tf_op jit(solution)/shard_map/outer/pallas_call | solution.py:22
  17.1 0.6 %collective-permute-done.5.halo_b = f32[8,128]{1,0:T(8,128)S(1)} collective-permute-done((f32[8,128]{1,0:T(8,128)S(1)}, f32[8,128]{1,0:T(8,128)S(1)}, u32[]{:S(2)}, u32[]{:S(2)}) %collective-permute-start.5) | collective-permute-done | bytes 4128 | tf_op jit(solution)/shard_map/ppermute | solution.py:681
  17.7 0.0 collective-permute-done.4.halo_a
  17.7 0.2 flux_x.1
  17.9 0.1 collective-permute-start.6
  18.0 0.8 %commit.1.refs_2_ = f32[8,128,128]{2,1,0:T(8,128)} custom-call(f32[8,128,128]{2,1,0:T(8,128)S(1)} %get-tuple-element.61.new), custom_call_target="tpu_custom_call" | custom-call | flops 20000000 | bytes 1048576 | tf_op jit(solution)/shard_map/commit/pallas_call | solution.py:760
  18.8 3.4 %collective-permute-done.6.refs_1_ = f32[7,16,128]{2,1,0:T(8,128)S(1)} collective-permute-done((f32[7,16,128]{2,1,0:T(8,128)S(1)}, f32[7,16,128]{2,1,0:T(8,128)S(1)}, u32[]{:S(2)}, u32[]{:S(2)}) %collective-permute-start.6) | collective-permute-done | bytes 57376 | tf_op jit(solution)/shard_map/ppermute | solution.py:478
  22.2 0.1 collective-permute-start.7
  22.2 4.2 %collective-permute-done.7.refs_1_.refs_3_ = f32[7,16,128]{2,1,0:T(8,128)S(1)} collective-permute-done((f32[7,16,128]{2,1,0:T(8,128)S(1)}, f32[7,16,128]{2,1,0:T(8,128)S(1)}, u32[]{:S(2)}, u32[]{:S(2)}) %collective-permute-start.7) | collective-permute-done | bytes 57376 | tf_op jit(solution)/shard_map/ppermute | solution.py:478
  26.4 0.9 %collective-permute-start.8 = (f32[3,16,128]{2,1,0:T(8,128)S(1)}, f32[3,16,128]{2,1,0:T(8,128)S(1)}, u32[]{:S(2)}, u32[]{:S(2)}) collective-permute-start(f32[3,16,128]{2,1,0:T(8,128)S(1)} %get-tuple-element.76), channel_id=1, source_target_pairs={{0,16},{4,20},{8,24},{12,28},{16,0},{20,4},{24,8},{28,12},{1,17},{... | collective-permute-start | bytes 73736 | tf_op jit(solution)/shard_map/ppermute | solution.py:478
  27.4 0.9 %coefficients_z.1 = (f32[16,8,128]{2,1,0:T(8,128)S(1)}, f32[16,8,128]{2,1,0:T(8,128)S(1)}, f32[7,16,8,128]{3,2,1,0:T(8,128)S(1)}, f32[7,16,8,128]{3,2,1,0:T(8,128)S(1)}, f32[7,16,8,128]{3,2,1,0:T(8,128)S(1)}) custom-call(f32[128,128]{1,0:T(8,128)S(1)} %get-tuple-element.62.diff, f32[128,128]{1,0:T(8,128)S(1)} %get-tuple-element.49.conc), custom_call_target="tpu_custom_call" | custom-call | flops 20000000 | bytes 1048576 | tf_op jit(solution)/shard_map/coefficients_z/pallas_call | solution.py:22
  28.3 0.1 inner_x.1
  28.4 2.8 %collective-permute-done.8.refs_5_ = f32[3,16,128]{2,1,0:T(8,128)S(1)} collective-permute-done((f32[3,16,128]{2,1,0:T(8,128)S(1)}, f32[3,16,128]{2,1,0:T(8,128)S(1)}, u32[]{:S(2)}, u32[]{:S(2)}) %collective-permute-start.8) | collective-permute-done | bytes 24608 | tf_op jit(solution)/shard_map/ppermute | solution.py:478
  31.2 0.2 flux_y.1
  31.5 0.1 collective-permute-start.9
  31.5 1.2 %collective-permute-done.9.refs_1_ = f32[7,8,128]{2,1,0:T(8,128)S(1)} collective-permute-done((f32[7,8,128]{2,1,0:T(8,128)S(1)}, f32[7,8,128]{2,1,0:T(8,128)S(1)}, u32[]{:S(2)}, u32[]{:S(2)}) %collective-permute-start.9) | collective-permute-done | bytes 28704 | tf_op jit(solution)/shard_map/ppermute | solution.py:478
  32.7 1.0 %collective-permute-start.10 = (f32[3,8,128]{2,1,0:T(8,128)S(1)}, f32[3,8,128]{2,1,0:T(8,128)S(1)}, u32[]{:S(2)}, u32[]{:S(2)}) collective-permute-start(f32[3,8,128]{2,1,0:T(8,128)S(1)} %get-tuple-element.83), channel_id=1, source_target_pairs={{0,2},{1,3},{2,0},{3,1},{4,6},{5,7},{6,4},{7,5},{8,10},{9,11},{10,... | collective-permute-start | bytes 36872 | tf_op jit(solution)/shard_map/ppermute | solution.py:478
  33.7 0.2 inner_y.1
  33.9 2.6 %collective-permute-done.10.refs_3_ = f32[3,8,128]{2,1,0:T(8,128)S(1)} collective-permute-done((f32[3,8,128]{2,1,0:T(8,128)S(1)}, f32[3,8,128]{2,1,0:T(8,128)S(1)}, u32[]{:S(2)}, u32[]{:S(2)}) %collective-permute-start.10) | collective-permute-done | bytes 12320 | tf_op jit(solution)/shard_map/ppermute | solution.py:478
  36.5 1.3 %last.1 = f32[128,128]{1,0:T(8,128)} custom-call(f32[16,8,128]{2,1,0:T(8,128)S(1)} %get-tuple-element.63._.applied, f32[16,8,128]{2,1,0:T(8,128)S(1)} %get-tuple-element.64.start, f32[7,16,8,128]{3,2,1,0:T(8,128)S(1)} %get-tuple-element.65.left, f32[7,16,8,128]{3,2,1,0:T(8,128)S(1)} %get-tuple-element.66.right, ...), custom_call_target="tpu_custom_call" | custom-call | flops 20000000 | bytes 1048576 | tf_op jit(solution)/shard_map/last/pallas_call | solution.py:22
  (3 shorter events, 0.1 us)
Async XLA Ops:
  2.1 11.7 %collective-permute-start = (f32[16,16,128]{2,1,0:T(8,128)S(1)}, f32[16,16,128]{2,1,0:T(8,128)S(1)}, u32[]{:S(2)}, u32[]{:S(2)}) collective-permute-start(f32[16,16,128]{2,1,0:T(8,128)S(1)} %get-tuple-element.54), channel_id=1, source_target_pairs={{0,4},{4,0},{8,12},{12,8},{16,20},{20,16},{24,28},{28,24},{1,5},{5... | collective-permute-start | bytes 393224 | tf_op jit(solution)/shard_map/ppermute | solution.py:675
  5.1 8.7 %collective-permute-start.1 = (f32[16,16,128]{2,1,0:T(8,128)S(1)}, f32[16,16,128]{2,1,0:T(8,128)S(1)}, u32[]{:S(2)}, u32[]{:S(2)}) collective-permute-start(f32[16,16,128]{2,1,0:T(8,128)S(1)} %get-tuple-element.55), channel_id=1, source_target_pairs={{0,28},{4,8},{8,4},{12,16},{16,12},{20,24},{24,20},{28,0},{1,29},{... | collective-permute-start | bytes 393224 | tf_op jit(solution)/shard_map/ppermute | solution.py:681
  8.8 5.0 %collective-permute-start.2 = (f32[17,8,128]{2,1,0:T(8,128)S(1)}, f32[17,8,128]{2,1,0:T(8,128)S(1)}, u32[]{:S(2)}, u32[]{:S(2)}) collective-permute-start(f32[17,8,128]{2,1,0:T(8,128)S(1)} %get-tuple-element.56), channel_id=1, source_target_pairs={{0,1},{1,0},{2,3},{3,2},{4,5},{5,4},{6,7},{7,6},{8,9},{9,8},{10,11... | collective-permute-start | bytes 208904 | tf_op jit(solution)/shard_map/ppermute | solution.py:675
  8.9 4.9 %collective-permute-start.3 = (f32[17,8,128]{2,1,0:T(8,128)S(1)}, f32[17,8,128]{2,1,0:T(8,128)S(1)}, u32[]{:S(2)}, u32[]{:S(2)}) collective-permute-start(f32[17,8,128]{2,1,0:T(8,128)S(1)} %get-tuple-element.57), channel_id=1, source_target_pairs={{0,3},{1,2},{2,1},{3,0},{4,7},{5,6},{6,5},{7,4},{8,11},{9,10},{10,... | collective-permute-start | bytes 208904 | tf_op jit(solution)/shard_map/ppermute | solution.py:681
  14.6 3.1 %collective-permute-start.5 = (f32[8,128]{1,0:T(8,128)S(1)}, f32[8,128]{1,0:T(8,128)S(1)}, u32[]{:S(2)}, u32[]{:S(2)}) collective-permute-start(f32[8,128]{1,0:T(8,128)S(1)} %get-tuple-element.68), channel_id=1, source_target_pairs={{0,3},{1,2},{2,1},{3,0},{4,7},{5,6},{6,5},{7,4},{8,11},{9,10},{10,... | collective-permute-start | bytes 12296 | tf_op jit(solution)/shard_map/ppermute | solution.py:681
  15.2 2.5 %collective-permute-start.4 = (f32[8,128]{1,0:T(8,128)S(1)}, f32[8,128]{1,0:T(8,128)S(1)}, u32[]{:S(2)}, u32[]{:S(2)}) collective-permute-start(f32[8,128]{1,0:T(8,128)S(1)} %get-tuple-element.58.refs_2_), channel_id=1, source_target_pairs={{0,1},{1,0},{2,3},{3,2},{4,5},{5,4},{6,7},{7,6},{8,9},{9,8},{10,11... | collective-permute-start | bytes 12296 | tf_op jit(solution)/shard_map/ppermute | solution.py:675
  17.9 4.2 %collective-permute-start.6 = (f32[7,16,128]{2,1,0:T(8,128)S(1)}, f32[7,16,128]{2,1,0:T(8,128)S(1)}, u32[]{:S(2)}, u32[]{:S(2)}) collective-permute-start(f32[7,16,128]{2,1,0:T(8,128)S(1)} %get-tuple-element.74.refs_0_), channel_id=1, source_target_pairs={{0,4},{4,0},{8,12},{12,8},{16,20},{20,16},{24,28},{28,24},{1,5},{5... | collective-permute-start | bytes 172040 | tf_op jit(solution)/shard_map/ppermute | solution.py:478
  22.2 4.2 %collective-permute-start.7 = (f32[7,16,128]{2,1,0:T(8,128)S(1)}, f32[7,16,128]{2,1,0:T(8,128)S(1)}, u32[]{:S(2)}, u32[]{:S(2)}) collective-permute-start(f32[7,16,128]{2,1,0:T(8,128)S(1)} %join_gx.2.refs_0_.refs_2_), channel_id=1, source_target_pairs={{0,8},{4,12},{8,0},{12,4},{16,24},{20,28},{24,16},{28,20},{1,9},{5... | collective-permute-start | bytes 172040 | tf_op jit(solution)/shard_map/ppermute | solution.py:478
  26.4 4.8 %collective-permute-start.8 = (f32[3,16,128]{2,1,0:T(8,128)S(1)}, f32[3,16,128]{2,1,0:T(8,128)S(1)}, u32[]{:S(2)}, u32[]{:S(2)}) collective-permute-start(f32[3,16,128]{2,1,0:T(8,128)S(1)} %get-tuple-element.76), channel_id=1, source_target_pairs={{0,16},{4,20},{8,24},{12,28},{16,0},{20,4},{24,8},{28,12},{1,17},{... | collective-permute-start | bytes 73736 | tf_op jit(solution)/shard_map/ppermute | solution.py:478
  31.5 1.3 %collective-permute-start.9 = (f32[7,8,128]{2,1,0:T(8,128)S(1)}, f32[7,8,128]{2,1,0:T(8,128)S(1)}, u32[]{:S(2)}, u32[]{:S(2)}) collective-permute-start(f32[7,8,128]{2,1,0:T(8,128)S(1)} %get-tuple-element.81.refs_0_), channel_id=1, source_target_pairs={{0,1},{1,0},{2,3},{3,2},{4,5},{5,4},{6,7},{7,6},{8,9},{9,8},{10,11... | collective-permute-start | bytes 86024 | tf_op jit(solution)/shard_map/ppermute | solution.py:478
  32.7 3.8 %collective-permute-start.10 = (f32[3,8,128]{2,1,0:T(8,128)S(1)}, f32[3,8,128]{2,1,0:T(8,128)S(1)}, u32[]{:S(2)}, u32[]{:S(2)}) collective-permute-start(f32[3,8,128]{2,1,0:T(8,128)S(1)} %get-tuple-element.83), channel_id=1, source_target_pairs={{0,2},{1,3},{2,0},{3,1},{4,6},{5,7},{6,4},{7,5},{8,10},{9,11},{10,... | collective-permute-start | bytes 36872 | tf_op jit(solution)/shard_map/ppermute | solution.py:478

commit v4 on v3

--- a/solution.py
+++ b/solution.py
@@ -7,24 +7,25 @@
 from jax.experimental.pallas import tpu as pltpu
 from jax.sharding import PartitionSpec as P
 
+
 KAPPA = 2.0
 DRIVE = 4.0
 SUB = 8
+UNROLL = 8
 
 VMEM = pl.BlockSpec(memory_space=pltpu.VMEM)
 SMEM = pl.BlockSpec(memory_space=pltpu.SMEM)
 HBM = pl.BlockSpec(memory_space=pltpu.HBM)
 
 
-def call(kernel, name, outs, ins, scratch=(), aliases={}, cost=20000, scalars=(), far=()):
+def call(kernel, outs, ins, scratch=(), aliases={}, cost=20000, scalars=(), far=(), out_far=False):
     f32 = jnp.float32
     place = [SMEM if i in scalars else HBM if i in far else VMEM for i in range(len(ins))]
     return pl.pallas_call(
         kernel,
-        name=name,
         out_shape=[s if isinstance(s, jax.ShapeDtypeStruct) else jax.ShapeDtypeStruct(s, f32) for s in outs],
         in_specs=place,
-        out_specs=[VMEM] * len(outs),
+        out_specs=[HBM if out_far else VMEM] * len(outs),
         scratch_shapes=[pltpu.VMEM(s, f32) if isinstance(s, tuple) else s for s in scratch],
         input_output_aliases=aliases,
         compiler_params=pltpu.CompilerParams(vmem_limit_bytes=12 << 20),
@@ -131,117 +132,115 @@
     return sums
 
 
-def plane_rows(shape, upper):
+def pitch_of(shape):
+    return shape[1] + 1 + shape[1] % 2
+
+
+def padded(shape):
+    return -(-shape[0] * pitch_of(shape) // SUB) * SUB
+
+
+def bordered(shape):
+    return -(-((shape[0] + 2) * pitch_of(shape) + 1) // SUB) * SUB
+
+
+def first_kernel(phases, shape, frac_far, ids_far, conc_far, *refs):
     nx, ny, _ = shape
-    return pl.ds(pl.multiple_of(jnp.where(upper, (nx - 1) * ny, 0), SUB), ny)
-
-
-def first_kernel(phases, shape, *refs):
-    nx, ny, nz = shape
-    count = (len(refs) - 5) // 2
-    far, near, outs, held_far, sems = refs[:count], refs[count:-5], refs[-5:-3], refs[-3:-1], refs[-1]
-    right = even("gx")
-    copies = []
-    for k, upper in enumerate((right, jnp.logical_not(right))):
-        rows = plane_rows(shape, upper)
-        for source, target in zip(far[:2], held_far):
-            copies.append(
-                pltpu.make_async_copy(source.at[:, rows, :], target.at[k], sems.at[len(copies)])
-            )
-    for source, target in zip(far, near):
-        half = source.shape[0] // 2 if len(source.shape) == 3 else 0
-        for piece in ([slice(0, half), slice(half, None)] if half else [slice(None)]):
-            copies.append(
-                pltpu.make_async_copy(source.at[piece], target.at[piece], sems.at[len(copies)])
-            )
+    small_far, (frac, ids, conc, *small), x_a, x_b, dense, sems = (
+        refs[:4], refs[4:11], refs[11], refs[12], refs[13], refs[14]
+    )
+    slots = frac.shape[0]
+    half = slots // 2
+    planes, rest = (slice(0, ny), slice((nx - 1) * ny, None)), slice(ny, (nx - 1) * ny)
+    pieces = [
+        (far.at[:, rows, :], near.at[:, rows, :])
+        for rows in planes
+        for far, near in ((frac_far, frac), (ids_far, ids))
+    ]
+    pieces += [
+        (far.at[part, rest, :], near.at[part, rest, :])
+        for part in (slice(0, half), slice(half, None))
+        for far, near in ((frac_far, frac), (ids_far, ids))
+    ]
+    pieces += [(conc_far, conc), *zip(small_far, small)]
+    copies = [
+        pltpu.make_async_copy(far, near, sems.at[k]) for k, (far, near) in enumerate(pieces)
+    ]
     for copy in copies:
         copy.start()
-    frac, ids = held_far
-    slots = frac.shape[1]
-    for k, out in enumerate(outs):
-        for copy in copies[2 * k : 2 * k + 2]:
-            copy.wait()
+    for phase in range(phases):
+        dense[phase] = jnp.zeros(dense.shape[1:], jnp.float32)
+    for copy in copies[:4]:
+        copy.wait()
+    right = even("gx")
+    for out, upper in ((x_a, right), (x_b, jnp.logical_not(right))):
+        base = jnp.where(upper, (nx - 1) * ny, 0)
         for part in range(ny // SUB):
-            rows = slice(part * SUB, (part + 1) * SUB)
+            rows = pl.ds(pl.multiple_of(base, SUB) + part * SUB, SUB)
             held = pick_rows(
-                [ids[k, s, rows, :] for s in range(slots)],
-                [frac[k, s, rows, :] for s in range(slots)],
+                [ids[s, rows, :] for s in range(slots)],
+                [frac[s, rows, :] for s in range(slots)],
                 phases,
             )
             for phase in range(phases):
-                out[phase, rows, :] = held[phase]
+                out[phase, part * SUB : (part + 1) * SUB, :] = held[phase]
     for copy in copies[4:]:
         copy.wait()
 
 
-def faces_kernel(phases, shape, frac, ids, conc, y_a, y_b):
+def faces_kernel(
+    phases, shape, frac, ids, conc, pair_class, mobility, drive, diffusivity, y_a, y_b, frac_y, ids_y, tables
+):
+    nx, ny, nz = shape
+    slots = frac.shape[0]
+    tables[0] = lane_table(drive, nz)
+    tables[1] = lane_table(diffusivity, nz)
+    tables[2] = pair_table(pair_class, mobility, phases, nz)
+    up = even("gy")
+    for k, (out, upper) in enumerate(((y_a, up), (y_b, jnp.logical_not(up)))):
+        rows = pl.ds(jnp.where(upper, ny - 1, 0), nx, stride=ny)
+        slot_ids = [ids[s, rows, :] for s in range(slots)]
+        slot_frac = [frac[s, rows, :] for s in range(slots)]
+        for s in range(slots):
+            ids_y[k, s] = slot_ids[s]
+            frac_y[k, s] = slot_frac[s]
+        for phase, row in enumerate(pick_rows(slot_ids, slot_frac, phases)):
+            out[phase] = row
+        out[phases] = conc[rows, :]
+
+
+def build_kernel(phases, shape, _, tables, frac, ids, dense, mob_out):
     nx, ny, _ = shape
     slots = frac.shape[0]
-    up = even("gy")
-    for out, upper in ((y_b, jnp.logical_not(up)), (y_a, up)):
-        rows = pl.ds(jnp.where(upper, ny - 1, 0), nx, stride=ny)
-        held = pick_rows(
-            [ids[s, rows, :] for s in range(slots)],
-            [frac[s, rows, :] for s in range(slots)],
-            phases,
-        )
-        for phase in range(phases):
-            out[phase] = held[phase]
-        out[phases] = conc[rows, :]
-
-
-def build_kernel(phases, shape, frac, ids, pair_class, mobility, dense, mob_out):
-    nx, ny, nz = shape
-    slots = frac.shape[0]
-    pitch = ny + 2 * SUB
-    parts = ny // SUB
-    table = pair_table(pair_class, mobility, phases, nz)
-    nothing = jnp.zeros((SUB, nz), jnp.float32)
-
-    def clear(phase, carry):
-        for plane in range(nx + 2):
-            for part in range(parts + 2):
-                if plane in (0, nx + 1) or part in (0, parts + 1):
-                    at = plane * pitch + part * SUB
-                    dense[phase, at : at + SUB, :] = nothing
-        return carry
-
-    lax.fori_loop(0, phases, clear, 0)
-
-    def build(x, carry):
-        for part in range(parts):
+    pitch = pitch_of(shape)
+    table = tables[2]
+
+    def plane(x, carry):
+        for part in range(ny // SUB):
             rows = pl.ds(pl.multiple_of(x * ny, SUB) + part * SUB, SUB)
             slot_ids = [ids[s, rows, :] for s in range(slots)]
+            into = pl.ds(x * pitch + part * SUB, SUB)
             for k, mob in enumerate(mobilities(slot_ids, table, phases)):
-                mob_out[k, rows, :] = mob
+                mob_out[k, into, :] = mob
             held = pick_rows(slot_ids, [frac[s, rows, :] for s in range(slots)], phases)
-            into = pl.ds(pl.multiple_of((x + 1) * pitch, SUB) + (part + 1) * SUB, SUB)
+            into = pl.ds((x + 1) * pitch + 1 + part * SUB, SUB)
             for phase in range(phases):
                 dense[phase, into, :] = held[phase]
         return carry
 
-    lax.fori_loop(0, nx, build, 0, unroll=2 if nx % 2 == 0 else 1)
-
-
-def tables_of(phases, drive, diffusivity, nz):
-    return lane_table(drive, nz), lane_table(diffusivity, nz)
-
-
-def renew(laplacian, rows, mobs, frac, ids, conc, tables):
-    slots = frac.shape[0]
-    slot_ids = [ids[s, rows, :] for s in range(slots)]
+    lax.fori_loop(0, nx, plane, 0, unroll=UNROLL if nx % UNROLL == 0 else 1)
+
+
+def renew(laplacian, slot_ids, slot_frac, mobs, conc, tables):
     slot_drive, slot_diff = [], []
     for i in slot_ids:
         slot_drive.append(lookup(tables[0], i))
         slot_diff.append(lookup(tables[1], i))
     curvature = pick_slots(slot_ids, laplacian)
-    slot_frac = [frac[s, rows, :] for s in range(slots)]
     level = [c + KAPPA * f for c, f in zip(curvature, slot_frac)]
-    scaled = DRIVE * conc[rows, :]
+    scaled = DRIVE * conc
     pulled = [scaled * f for f in slot_frac]
-    sums = exchange(
-        level, [mobs[k, rows, :] for k in range(mobs.shape[0])], (pulled, slot_frac, slot_drive)
-    )
+    sums = exchange(level, mobs, (pulled, slot_frac, slot_drive))
     new = [f + t for f, t in zip(slot_frac, sums)]
     diffus = jnp.ones(new[0].shape, jnp.float32)
     for value, d in zip(new, slot_diff):
@@ -258,48 +257,57 @@
         yield (along_x + along_y + along_z) - 6.0 * centre
 
 
-def interior_kernel(
-    phases, shape, planes, dense, mobs, frac, ids, conc, drive, diffusivity, *refs
-):
-    nx, ny, nz = shape
+def interior_kernel(phases, shape, planes, dense, mobs, tables, frac, ids, conc, *refs):
+    _, ny, nz = shape
+    slots = frac.shape[0]
     new_out, diff_out = refs[-2:]
-    pitch = ny + 2 * SUB
-    tables = tables_of(phases, drive, diffusivity, nz)
+    pitch = pitch_of(shape)
 
     def update(x, carry):
         for part in range(ny // SUB):
             rows = pl.ds(pl.multiple_of(x * ny, SUB) + part * SUB, SUB)
-            base = pl.multiple_of((x + 1) * pitch, SUB) + (part + 1) * SUB
+            wide = pl.ds(x * pitch + part * SUB, SUB)
+            base = (x + 1) * pitch + 1 + part * SUB
             laplacian = laplacian_at(
                 dense, phases, nz, lambda shift, base=base: pl.ds(base + shift, SUB), pitch
             )
-            new, diffus = renew(laplacian, rows, mobs, frac, ids, conc, tables)
+            new, diffus = renew(
+                laplacian,
+                [ids[s, rows, :] for s in range(slots)],
+                [frac[s, rows, :] for s in range(slots)],
+                [mobs[k, wide, :] for k in range(mobs.shape[0])],
+                conc[rows, :],
+                tables,
+            )
             for s, value in enumerate(new):
                 new_out[s, rows, :] = value
-            diff_out[rows, :] = diffus
+            diff_out[wide, :] = diffus
         return carry
 
-    lax.fori_loop(planes[0], planes[1], update, 0)
+    steps = planes[1] - planes[0]
+    lax.fori_loop(planes[0], planes[1], update, 0, unroll=2 if steps % 2 == 0 else 1)
 
 
 def edge_kernel(
-    phases, shape, dense, mobs, frac, ids, conc, drive, diffusivity, x_a, x_b, y_a, y_b, _,
-    face_a, face_b,
+    phases, shape, dense, mobs, tables, frac_y, ids_y, sent_a, sent_b, x_a, x_b, y_a, y_b, _,
+    face_a, face_b, new_y,
 ):
     nx, ny, nz = shape
-    pitch = ny + 2 * SUB
-    tables = tables_of(phases, drive, diffusivity, nz)
+    slots = frac_y.shape[1]
+    pitch = pitch_of(shape)
     place = lax.broadcasted_iota(jnp.int32, (nx, nz), 0)
     at_a = place == jnp.where(even("gx"), nx - 1, 0)
     at_b = place == jnp.where(even("gx"), 0, nx - 1)
     up = even("gy")
-    for face, halo, upper in ((face_a, y_a, up), (face_b, y_b, jnp.logical_not(up))):
+    for k, (face, halo, sent, upper) in enumerate(
+        ((face_a, y_a, sent_a, up), (face_b, y_b, sent_b, jnp.logical_not(up)))
+    ):
         y = jnp.where(upper, ny - 1, 0)
         inner = laplacian_at(
             dense,
             phases,
             nz,
-            lambda shift, y=y: pl.ds(pitch + SUB + y + shift, nx, stride=pitch),
+            lambda shift, y=y: pl.ds(pitch + 1 + y + shift, nx, stride=pitch),
             pitch,
         )
 
@@ -309,43 +317,49 @@
                 row_b = jnp.where(at_b, x_b[phase, pl.ds(y, 1), :], 0.0)
                 yield value + halo[phase] + (row_a + row_b)
 
-        _, diffus = renew(
-            whole(), pl.ds(y, nx, stride=ny), mobs, frac, ids, conc, tables
+        new, diffus = renew(
+            whole(),
+            [ids_y[k, s] for s in range(slots)],
+            [frac_y[k, s] for s in range(slots)],
+            [mobs[m, pl.ds(y, nx, stride=pitch), :] for m in range(mobs.shape[0])],
+            sent[phases],
+            tables,
         )
         face[...] = diffus
+        for s in range(slots):
+            new_y[k, s] = new[s]
 
 
 def outer_kernel(
-    phases, shape, new_in, diff_in, mobs, ids, x_a, x_b, y_a, y_b, diffusivity, new_out, diff_out
+    phases, shape, new_in, diff_in, mobs, tables, ids, x_a, x_b, face_a, face_b, new_y, new_out, diff_out
 ):
-    nx, ny, nz = shape
-    slots = new_in.shape[0]
-    diff_table = lane_table(diffusivity, nz)
     del new_in, diff_in
-
-    def add(rows, halo):
-        slot_ids = [ids[s, rows, :] for s in range(slots)]
-        level = pick_slots(slot_ids, (halo(p) for p in range(phases)))
-        sums = exchange(level, [mobs[k, rows, :] for k in range(mobs.shape[0])])
-        diffus = jnp.ones(sums[0].shape, jnp.float32)
-        for s in range(slots):
-            new = new_out[s, rows, :] + sums[s]
-            new_out[s, rows, :] = new
-            diffus = diffus + new * new * lookup(diff_table, slot_ids[s])
-        diff_out[rows, :] = diffus
-
+    nx, ny, _ = shape
+    slots = ids.shape[0]
+    pitch = pitch_of(shape)
     right = even("gx")
     for halo, upper in ((x_a, right), (x_b, jnp.logical_not(right))):
-        base = jnp.where(upper, (nx - 1) * ny, 0)
+        plane = jnp.where(upper, nx - 1, 0)
         for part in range(ny // SUB):
-            add(
-                pl.ds(pl.multiple_of(base + part * SUB, SUB), SUB),
-                lambda p, halo=halo, part=part: halo[p, part * SUB : (part + 1) * SUB, :],
+            rows = pl.ds(pl.multiple_of(plane * ny, SUB) + part * SUB, SUB)
+            wide = pl.ds(plane * pitch + part * SUB, SUB)
+            slot_ids = [ids[s, rows, :] for s in range(slots)]
+            level = pick_slots(
+                slot_ids, [halo[p, part * SUB : (part + 1) * SUB, :] for p in range(phases)]
             )
+            sums = exchange(level, [mobs[k, wide, :] for k in range(mobs.shape[0])])
+            diffus = jnp.ones(sums[0].shape, jnp.float32)
+            for s in range(slots):
+                new = new_out[s, rows, :] + sums[s]
+                new_out[s, rows, :] = new
+                diffus = diffus + new * new * lookup(tables[1], slot_ids[s])
+            diff_out[wide, :] = diffus
     up = even("gy")
-    for halo, upper in ((y_a, up), (y_b, jnp.logical_not(up))):
-        rows = pl.ds(jnp.where(upper, ny - 1, 0), nx, stride=ny)
-        add(rows, lambda p, halo=halo: halo[p])
+    for k, (face, upper) in enumerate(((face_a, up), (face_b, jnp.logical_not(up)))):
+        y = jnp.where(upper, ny - 1, 0)
+        for s in range(slots):
+            new_out[s, pl.ds(y, nx, stride=ny), :] = new_y[k, s]
+        diff_out[pl.ds(y, nx, stride=pitch), :] = face[...]
 
 
 def chain_ends(source, face):
@@ -482,7 +496,6 @@
             ins = refs[-2:] + ([after] if after is not None else [])
             outs = call(
                 functools.partial(join_kernel, axis, levels[-1], above),
-                "join_" + axis,
                 [shape] + ([(3, *shape[1:])] if above else []),
                 ins,
                 far=range(2, len(ins)),
@@ -507,27 +520,29 @@
     d_high = side(halo_a[...], halo_b[...], up)
     c_low = side(y_b[last], y_a[last], up)
     c_high = side(y_a[last], y_b[last], up)
-    d_prev, c_prev = diff[pl.ds(0, nx, stride=ny), :], conc[pl.ds(0, nx, stride=ny), :]
+    pitch = pitch_of(shape)
+    d_prev, c_prev = diff[pl.ds(0, nx, stride=pitch), :], conc[pl.ds(0, nx, stride=ny), :]
     below = has_low * (d_low + d_prev) * (c_prev - c_low)
     for y in range(ny):
         if y + 1 < ny:
-            d_next, c_next = diff[pl.ds(y + 1, nx, stride=ny), :], conc[pl.ds(y + 1, nx, stride=ny), :]
+            d_next, c_next = diff[pl.ds(y + 1, nx, stride=pitch), :], conc[pl.ds(y + 1, nx, stride=ny), :]
             above = 0.5 * (d_prev + d_next) * (c_next - c_prev)
         else:
             d_next, c_next = d_high, c_high
             above = has_high * (d_prev + d_next) * (c_next - c_prev)
-        applied[pl.ds(y, nx, stride=ny), :] = above - below
+        applied[pl.ds(y, nx, stride=pitch), :] = above - below
         d_prev, c_prev, below = d_next, c_next, above
 
     inside = lax.broadcasted_iota(jnp.int32, (ny, nz), 1) < nz - 1
     rows = [slice(x * ny, (x + 1) * ny) for x in range(nx)]
     values, d = [], []
     for x in range(nx):
-        here, c = diff[rows[x], :], conc[rows[x], :]
+        wide = slice(x * pitch, x * pitch + ny)
+        here, c = diff[wide, :], conc[rows[x], :]
         flux = jnp.where(
             inside, 0.5 * (here + pltpu.roll(here, nz - 1, 1)) * (pltpu.roll(c, nz - 1, 1) - c), 0.0
         )
-        value = (c + applied[rows[x], :]) + (flux - pltpu.roll(flux, 1, 1))
+        value = (c + applied[wide, :]) + (flux - pltpu.roll(flux, 1, 1))
         source[rows[x], :] = value
         values.append(value)
         d.append(here)
@@ -565,10 +580,11 @@
 
 
 def inner_x_kernel(shape, diff, source, base_out, first_out, last_out):
-    nx, ny, nz = shape
+    nx, ny, _ = shape
+    pitch = pitch_of(shape)
     for part in range(ny // SUB):
         rows = [slice(x * ny + part * SUB, x * ny + (part + 1) * SUB) for x in range(nx)]
-        d = [diff[r, :] for r in rows]
+        d = [diff[x * pitch + part * SUB : x * pitch + (part + 1) * SUB, :] for x in range(nx)]
         face = [0.5 * (a + b) for a, b in zip(d[:-1], d[1:])]
         base, first, last = inside_chain([source[r, :] for r in rows], face)
         for r, u, f, l in zip(rows, base, first, last):
@@ -578,14 +594,15 @@
 
 
 def flux_y_kernel(shape, levels, diff, base, first, last, applied, _, *refs):
-    nx, ny, nz = shape
+    nx, ny, _ = shape
+    pitch = pitch_of(shape)
     payload, source, section = refs[-3:]
     lower, upper = solve_levels("gx", levels, refs[:-3])
     for x in range(nx):
-        r = slice(x * ny, (x + 1) * ny)
-        section[r, :] = (base[r, :] + upper * last[r, :] - lower * first[r, :]) - applied[r, :]
-    values = [section[pl.ds(y, nx, stride=ny), :] for y in range(ny)]
-    d = [diff[pl.ds(y, nx, stride=ny), :] for y in range(ny)]
+        r, wide = slice(x * ny, (x + 1) * ny), slice(x * pitch, x * pitch + ny)
+        section[wide, :] = (base[r, :] + upper * last[r, :] - lower * first[r, :]) - applied[wide, :]
+    values = [section[pl.ds(y, nx, stride=pitch), :] for y in range(ny)]
+    d = [diff[pl.ds(y, nx, stride=pitch), :] for y in range(ny)]
     for y in range(ny):
         source[y] = values[y]
     face = [0.5 * (a + b) for a, b in zip(d[:-1], d[1:])]
@@ -597,8 +614,8 @@
 
 
 def inner_y_kernel(shape, diff, source, base_out, first_out, last_out):
-    nx, ny, nz = shape
-    d = [diff[pl.ds(y, nx, stride=ny), :] for y in range(ny)]
+    nx, ny, _ = shape
+    d = [diff[pl.ds(y, nx, stride=pitch_of(shape)), :] for y in range(ny)]
     face = [0.5 * (a + b) for a, b in zip(d[:-1], d[1:])]
     base, first, last = inside_chain([source[y] for y in range(ny)], face)
     for y in range(ny):
@@ -620,8 +637,7 @@
 
     state = []
     for y in range(ny):
-        rows = pl.ds(y, nx, stride=ny)
-        d, c = diff[rows, :], conc[rows, :]
+        d, c = diff[pl.ds(y, nx, stride=pitch_of(shape)), :], conc[pl.ds(y, nx, stride=ny), :]
         right = jnp.where(lane < nz - 1, 0.5 * (d + pltpu.roll(d, nz - 1, 1)), 0.0)
         left = pltpu.roll(right, 1, 1)
         flux = right * (pltpu.roll(c, nz - 1, 1) - c)
@@ -646,22 +662,30 @@
 
 
 def last_kernel(shape, levels, applied, start, left, right, unit, base, first, last, *refs):
-    nx, ny, nz = shape
-    out = refs[-1]
-    lower, upper = solve_levels("gy", levels, refs[:-1])
-    values = [
-        ((base[y] + upper * last[y] - lower * first[y]) - applied[y]) * start[y] for y in range(ny)
-    ]
-    for step in range(steps_of(nz)):
-        shift = 2**step
+    _, ny, nz = shape
+    out, held, sems = refs[-3:]
+    lower, upper = solve_levels("gy", levels, refs[:-3])
+    groups = [range(at, min(at + SUB, ny)) for at in range(0, ny, SUB)]
+    copies = []
+    for g, group in enumerate(groups):
         values = [
-            unit[step, y] * v
-            + left[step, y] * pltpu.roll(v, shift, 1)
-            + right[step, y] * pltpu.roll(v, nz - shift, 1)
-            for y, v in enumerate(values)
+            ((base[y] + upper * last[y] - lower * first[y]) - applied[y]) * start[y] for y in group
         ]
-    for y in range(ny):
-        out[pl.ds(y, nx, stride=ny), :] = values[y]
+        for step in range(steps_of(nz)):
+            shift = 2**step
+            values = [
+                unit[step, y] * v
+                + left[step, y] * pltpu.roll(v, shift, 1)
+                + right[step, y] * pltpu.roll(v, nz - shift, 1)
+                for y, v in zip(group, values)
+            ]
+        for y, value in zip(group, values):
+            held[:, y, :] = value
+        part = slice(group[0], group[-1] + 1)
+        copies.append(pltpu.make_async_copy(held.at[:, part, :], out.at[:, part, :], sems.at[g]))
+        copies[-1].start()
+    for copy in copies:
+        copy.wait()
 
 
 def commit_kernel(new, out, sem):
@@ -693,68 +717,62 @@
 
     small = [pair_class] + [v.reshape(1, -1) for v in (mobility, drive, diffusivity)]
     ins = [frac, ids, field] + [far_away(v) for v in small]
-    frac, ids, field, classes, mobility, drive, diffusivity, x_a, x_b = call(
+    wide, block = (padded(shape), nz), (phases, bordered(shape), nz)
+    frac, ids, field, *small, x_a, x_b, dense = call(
         functools.partial(first_kernel, phases, shape),
-        "first",
-        [jax.ShapeDtypeStruct(v.shape, v.dtype) for v in ins] + [(phases, ny, nz)] * 2,
+        [jax.ShapeDtypeStruct(v.shape, v.dtype) for v in ins]
+        + [(phases, ny, nz)] * 2
+        + [block],
         ins,
-        scratch=[
-            pltpu.VMEM((2, slots, ny, nz), jnp.float32),
-            pltpu.VMEM((2, slots, ny, nz), ids.dtype),
-            pltpu.SemaphoreType.DMA((len(ins) + 6,)),
-        ],
+        scratch=[pltpu.SemaphoreType.DMA((13,))],
         far=range(len(ins)),
     )
     x_a = exchange_near("gx", x_a)
     x_b = exchange_far("gx", x_b)
-    y_a, y_b = call(
+    sent_a, sent_b, frac_y, ids_y, tables = call(
         functools.partial(faces_kernel, phases, shape),
-        "faces",
-        [(phases + 1, nx, nz)] * 2,
-        [frac, ids, field],
-    )
-    y_b = exchange_far("gy", y_b)
-    y_a = exchange_near("gy", y_a)
+        [(phases + 1, nx, nz)] * 2
+        + [(2, slots, nx, nz), jax.ShapeDtypeStruct((2, slots, nx, nz), ids.dtype)]
+        + [(3, SUB, nz)],
+        [frac, ids, field, *small],
+    )
+    y_b = exchange_far("gy", sent_b)
+    y_a = exchange_near("gy", sent_a)
     dense, mobs = call(
         functools.partial(build_kernel, phases, shape),
-        "build",
-        [(phases, (nx + 2) * (ny + 2 * SUB), nz), (len(pairs_of(slots)), cells, nz)],
-        [frac, ids, classes, mobility],
-    )
-    fields = [dense, mobs, frac, ids, field, drive, diffusivity]
+        [block, (len(pairs_of(slots)), *wide)],
+        [dense, tables, frac, ids],
+        aliases={0: 0},
+    )
+    fields = [dense, mobs, tables, frac, ids, field]
     middle = nx // 2
     new, diffus = call(
         functools.partial(interior_kernel, phases, shape, (0, middle)),
-        "interior_low",
-        [(slots, cells, nz), flat],
+        [(slots, cells, nz), wide],
         fields,
     )
-    faces = call(
+    *faces, new_y = call(
         functools.partial(edge_kernel, phases, shape),
-        "edge",
-        [(nx, nz)] * 2,
-        fields + [x_a, x_b, y_a, y_b, diffus],
+        [(nx, nz)] * 2 + [(2, slots, nx, nz)],
+        [dense, mobs, tables, frac_y, ids_y, sent_a, sent_b, x_a, x_b, y_a, y_b, diffus],
     )
     face_b = exchange_far("gy", faces[1])
     face_a = exchange_near("gy", faces[0])
     new, diffus = call(
         functools.partial(interior_kernel, phases, shape, (middle, nx)),
-        "interior_high",
-        [(slots, cells, nz), flat],
+        [(slots, cells, nz), wide],
         fields + [new, diffus, faces[0]],
-        aliases={7: 0, 8: 1},
+        aliases={6: 0, 7: 1},
     )
     new, diffus = call(
         functools.partial(outer_kernel, phases, shape),
-        "outer",
-        [(slots, cells, nz), flat],
-        [new, diffus, mobs, ids, x_a, x_b, y_a, y_b, diffusivity],
+        [(slots, cells, nz), wide],
+        [new, diffus, mobs, tables, ids, x_a, x_b, *faces, new_y],
         aliases={0: 0, 1: 1},
     )
     payload, source, applied = call(
         functools.partial(flux_x_kernel, shape),
-        "flux_x",
-        [(7, ny, nz), flat, flat],
+        [(7, ny, nz), flat, wide],
         [diffus, field, y_a, y_b, face_a, face_b],
     )
     (new,) = pl.pallas_call(
@@ -770,35 +788,33 @@
     levels, refs = gather_levels("gx", payload, (7, ny, nz), far_away(new))
     applied_z, start, left, right, unit = call(
         functools.partial(coefficients_z_kernel, shape),
-        "coefficients_z",
         [(ny, nx, nz)] * 2 + [(steps_of(nz), ny, nx, nz)] * 3,
         [diffus, field],
     )
-    base, first, last = call(
-        functools.partial(inner_x_kernel, shape), "inner_x", [flat] * 3, [diffus, source]
-    )
+    base, first, last = call(functools.partial(inner_x_kernel, shape), [flat] * 3, [diffus, source])
     payload, source = call(
         functools.partial(flux_y_kernel, shape, levels),
-        "flux_y",
         [(7, nx, nz), (ny, nx, nz)],
         [diffus, base, first, last, applied, applied_z] + refs,
-        scratch=[flat],
+        scratch=[wide],
     )
     levels, refs = gather_levels("gy", payload, (7, nx, nz))
     base, first, last = call(
-        functools.partial(inner_y_kernel, shape), "inner_y", [(ny, nx, nz)] * 3, [diffus, source]
+        functools.partial(inner_y_kernel, shape), [(ny, nx, nz)] * 3, [diffus, source]
     )
     (out,) = call(
         functools.partial(last_kernel, shape, levels),
-        "last",
-        [flat],
+        [(nx, ny, nz)],
         [applied_z, start, left, right, unit, base, first, last] + refs,
-    )
-    return new.reshape(slots, nx, ny, nz), out.reshape(nx, ny, nz)
+        scratch=[(nx, ny, nz), pltpu.SemaphoreType.DMA((-(-ny // SUB),))],
+        out_far=True,
+    )
+    return new.reshape(slots, nx, ny, nz), out
 
 
 def solution(mesh):
     split = P(None, "gx", "gy", None)
+
     return jax.shard_map(
         body,
         mesh=mesh,

time: 37.9 us -> 37.1 us (0.979)
  starting transfers between devices: 11.1 us -> 12.7 us
  Pallas kernels: 11.2 us -> 9.61 us
  waiting for transfers between devices: 14.7 us -> 13.9 us
    pallas_call x16, Pallas kernels: 10.4 us -> 8.81 us  [call(): pl.pallas_call(kernel, out_shape=[s if isinstance(s, jax.ShapeDtypeStruct...]
    ppermute x5, starting transfers between devices: 2.14 us -> 2.84 us  [gather_levels(): refs += [payload, lax.ppermute(send, axis, pairs)]]
    ppermute x5, waiting for transfers between devices: 14.1 us -> 13.4 us  [gather_levels(): refs += [payload, lax.ppermute(send, axis, pairs)]]
    ppermute x3, starting transfers between devices: 5.8 us -> 6.4 us  [exchange_far(): return lax.ppermute(array, axis, pairs)]
  transfers between devices with their start and end apart: 11 -> 11, of which waited for: 6 -> 6; matrix products, arithmetic and copies ran while one was open for 0% -> 0% of each run, Pallas kernels for 19% -> 16%
where the time goes in v4:
time: 37.1 us; the launch traced here: 37 us
  waiting for transfers between devices  13.9 us (37%)
  starting transfers between devices  12.7 us (34%)
  Pallas kernels  9.61 us (26%)
  between operations  0.79 us (2%)
    ppermute x5, waiting for transfers between devices, gather_levels(): refs += [payload, lax.ppermute(send, axis, pairs)]  13.4 us
    pallas_call x16, Pallas kernels, call(): pl.pallas_call(kernel, out_shape=[s if isinstance(s, jax.ShapeDtypeStruct...  8.81 us
    ppermute x3, starting transfers between devices, exchange_far(): return lax.ppermute(array, axis, pairs)  6.4 us
    ppermute x3, starting transfers between devices, exchange_near(): return lax.ppermute(array, axis, [(i, i ^ 1) for i in range(count)])  3.44 us
    ppermute x5, starting transfers between devices, gather_levels(): refs += [payload, lax.ppermute(send, axis, pairs)]  2.84 us
    pallas_call x1, Pallas kernels, body(): pl.pallas_call(commit_kernel, name='commit', out_shape=[jax.ShapeDtypeStr...  0.8 us
  transfers between devices with their start and end apart: 11, of which 6 were waited for; matrix products, arithmetic and copies ran while one was open for 0% of the time, Pallas kernels for 16%

profile of v4, /device:TPU:0, one launch (start us, length us, event | category | flops | bytes accessed | tf_op | source)
XLA Modules:
  0.0 37.0 jit_solution(8527954698393960741)
XLA Ops:
  0.6 1.5 %shard_map.86 = (f32[8,128,128]{2,1,0:T(8,128)S(1)}, s32[8,128,128]{2,1,0:T(8,128)S(1)}, f32[128,128]{1,0:T(8,128)S(1)}, s32[16,16]{1,0:T(8,128)S(1)}, f32[1,4]{...) custom-call(f32[8,128,128]{2,1,0:T(8,128)} %bitcast.8, ...), custom_call_target="tpu_custom_call" | custom-call | flops 20000000 | bytes 1048576 | tf_op jit(solution)/shard_map/pallas_call | solution.py:24
  2.2 3.0 %collective-permute-start = (f32[16,16,128]{2,1,0:T(8,128)S(1)}, f32[16,16,128]{2,1,0:T(8,128)S(1)}, u32[]{:S(2)}, u32[]{:S(2)}) collective-permute-start(f32[16,16,128]{2,1,0:T(8,128)S(1)} %get-tuple-element.65), channel_id=1, source_target_pairs={{0,4},{4,0},{8,12},{12,8},{16,20},{20,16},{24,28},{28,24},{1,5},{5... | collective-permute-start | bytes 393224 | tf_op jit(solution)/shard_map/ppermute | solution.py:699
  5.2 3.6 %collective-permute-start.1 = (f32[16,16,128]{2,1,0:T(8,128)S(1)}, f32[16,16,128]{2,1,0:T(8,128)S(1)}, u32[]{:S(2)}, u32[]{:S(2)}) collective-permute-start(f32[16,16,128]{2,1,0:T(8,128)S(1)} %get-tuple-element.66), channel_id=1, source_target_pairs={{0,28},{4,8},{8,4},{12,16},{16,12},{20,24},{24,20},{28,0},{1,29},{... | collective-permute-start | bytes 393224 | tf_op jit(solution)/shard_map/ppermute | solution.py:705
  8.8 0.3 shard_map.87
  9.1 0.1 collective-permute-start.2
  9.2 1.6 %collective-permute-start.3 = (f32[17,8,128]{2,1,0:T(8,128)S(1)}, f32[17,8,128]{2,1,0:T(8,128)S(1)}, u32[]{:S(2)}, u32[]{:S(2)}) collective-permute-start(f32[17,8,128]{2,1,0:T(8,128)S(1)} %get-tuple-element.64.sent_b), channel_id=1, source_target_pairs={{0,3},{1,2},{2,1},{3,0},{4,7},{5,6},{6,5},{7,4},{8,11},{9,10},{10,... | collective-permute-start | bytes 208904 | tf_op jit(solution)/shard_map/ppermute | solution.py:705
  10.8 1.3 %shard_map.88 = (f32[16,176,128]{2,1,0:T(8,128)S(1)}, f32[28,136,128]{2,1,0:T(8,128)S(1)}) custom-call(f32[16,176,128]{2,1,0:T(8,128)S(1)} %get-tuple-element.48._, f32[3,8,128]{2,1,0:T(8,128)S(1)} %get-tuple-element.56.tables, f32[8,128,128]{2,1,0:T(8,128)S(1)} %get-tuple-element.49.frac, ...), custom_call_target="tpu_custom_call", output_to_operand_aliasing={{0}: (0, {})} | custom-call | flops 20000000 | bytes 1048576 | tf_op jit(solution)/shard_map/pallas_call | solution.py:24
  12.1 1.1 %shard_map.89 = (f32[8,128,128]{2,1,0:T(8,128)S(1)}, f32[136,128]{1,0:T(8,128)S(1)}) custom-call(f32[16,176,128]{2,1,0:T(8,128)S(1)} %get-tuple-element.57.dense, f32[28,136,128]{2,1,0:T(8,128)S(1)} %get-tuple-element.58.mobs, f32[3,8,128]{2,1,0:T(8,128)S(1)} %get-tuple-element.56.tables, f32[8,128,128]{2,1,0:T(8,128)S(1)} %get-tuple-element.49.frac, ...), custom_call_target="tpu_custom_call" | custom-call | flops 20000000 | bytes 1048576 | tf_op jit(solution)/shard_map/pallas_call | solution.py:24
  13.2 0.0 collective-permute-done.2.y_a
  13.2 0.0 collective-permute-done.3.y_b
  13.2 0.0 collective-permute-done.x_a
  13.2 0.0 collective-permute-done.1.x_b
  13.3 0.3 shard_map.90
  13.6 0.3 collective-permute-start.4
  13.9 1.2 %collective-permute-start.5 = (f32[8,128]{1,0:T(8,128)S(1)}, f32[8,128]{1,0:T(8,128)S(1)}, u32[]{:S(2)}, u32[]{:S(2)}) collective-permute-start(f32[8,128]{1,0:T(8,128)S(1)} %get-tuple-element.70.face_b), channel_id=1, source_target_pairs={{0,3},{1,2},{2,1},{3,0},{4,7},{5,6},{6,5},{7,4},{8,11},{9,10},{10,... | collective-permute-start | bytes 12296 | tf_op jit(solution)/shard_map/ppermute | solution.py:705
  15.1 1.1 %shard_map.91 = (f32[8,128,128]{2,1,0:T(8,128)S(1)}, f32[136,128]{1,0:T(8,128)S(1)}) custom-call(f32[16,176,128]{2,1,0:T(8,128)S(1)} %get-tuple-element.57.dense, f32[28,136,128]{2,1,0:T(8,128)S(1)} %get-tuple-element.58.mobs, f32[3,8,128]{2,1,0:T(8,128)S(1)} %get-tuple-element.56.tables, ...), custom_call_target="tpu_custom_call", output_to_operand_aliasing={{0}: (6, {}), {1}: (7, {})} | custom-call | flops 20000000 | bytes 1048576 | tf_op jit(solution)/shard_map/pallas_call | solution.py:24
  16.2 0.2 shard_map.92
  16.4 0.0 collective-permute-done.4.halo_a
  16.5 0.5 %collective-permute-done.5.halo_b = f32[8,128]{1,0:T(8,128)S(1)} collective-permute-done((f32[8,128]{1,0:T(8,128)S(1)}, f32[8,128]{1,0:T(8,128)S(1)}, u32[]{:S(2)}, u32[]{:S(2)}) %collective-permute-start.5) | collective-permute-done | bytes 4128 | tf_op jit(solution)/shard_map/ppermute | solution.py:705
  17.0 0.2 shard_map.94
  17.2 0.1 collective-permute-start.6
  17.2 0.8 %commit.1.refs_2_ = f32[8,128,128]{2,1,0:T(8,128)} custom-call(f32[8,128,128]{2,1,0:T(8,128)S(1)} %get-tuple-element.72.new), custom_call_target="tpu_custom_call" | custom-call | flops 20000000 | bytes 1048576 | tf_op jit(solution)/shard_map/commit/pallas_call | solution.py:778
  18.0 3.4 %collective-permute-done.6.refs_1_ = f32[7,16,128]{2,1,0:T(8,128)S(1)} collective-permute-done((f32[7,16,128]{2,1,0:T(8,128)S(1)}, f32[7,16,128]{2,1,0:T(8,128)S(1)}, u32[]{:S(2)}, u32[]{:S(2)}) %collective-permute-start.6) | collective-permute-done | bytes 57376 | tf_op jit(solution)/shard_map/ppermute | solution.py:492
  21.4 0.1 collective-permute-start.7
  21.5 4.2 %collective-permute-done.7.refs_1_.refs_3_ = f32[7,16,128]{2,1,0:T(8,128)S(1)} collective-permute-done((f32[7,16,128]{2,1,0:T(8,128)S(1)}, f32[7,16,128]{2,1,0:T(8,128)S(1)}, u32[]{:S(2)}, u32[]{:S(2)}) %collective-permute-start.7) | collective-permute-done | bytes 57376 | tf_op jit(solution)/shard_map/ppermute | solution.py:492
  25.7 1.0 %collective-permute-start.8 = (f32[3,16,128]{2,1,0:T(8,128)S(1)}, f32[3,16,128]{2,1,0:T(8,128)S(1)}, u32[]{:S(2)}, u32[]{:S(2)}) collective-permute-start(f32[3,16,128]{2,1,0:T(8,128)S(1)} %get-tuple-element.86), channel_id=1, source_target_pairs={{0,16},{4,20},{8,24},{12,28},{16,0},{20,4},{24,8},{28,12},{1,17},{... | collective-permute-start | bytes 73736 | tf_op jit(solution)/shard_map/ppermute | solution.py:492
  26.7 0.9 %shard_map.93 = (f32[16,8,128]{2,1,0:T(8,128)S(1)}, f32[16,8,128]{2,1,0:T(8,128)S(1)}, f32[7,16,8,128]{3,2,1,0:T(8,128)S(1)}, f32[7,16,8,128]{3,2,1,0:T(8,128)S(1)}, f32[7,16,8,128]{3,2,1,0:T(8,128)S(1)}) custom-call(f32[136,128]{1,0:T(8,128)S(1)} %get-tuple-element.73.diff, f32[128,128]{1,0:T(8,128)S(1)} %get-tuple-element.51.conc), custom_call_target="tpu_custom_call" | custom-call | flops 20000000 | bytes 1048576 | tf_op jit(solution)/shard_map/pallas_call | solution.py:24
  27.7 0.1 shard_map.95
  27.8 2.7 %collective-permute-done.8.refs_5_ = f32[3,16,128]{2,1,0:T(8,128)S(1)} collective-permute-done((f32[3,16,128]{2,1,0:T(8,128)S(1)}, f32[3,16,128]{2,1,0:T(8,128)S(1)}, u32[]{:S(2)}, u32[]{:S(2)}) %collective-permute-start.8) | collective-permute-done | bytes 24608 | tf_op jit(solution)/shard_map/ppermute | solution.py:492
  30.5 0.2 shard_map.98
  30.7 0.1 collective-permute-start.9
  30.8 1.2 %collective-permute-done.9.refs_1_ = f32[7,8,128]{2,1,0:T(8,128)S(1)} collective-permute-done((f32[7,8,128]{2,1,0:T(8,128)S(1)}, f32[7,8,128]{2,1,0:T(8,128)S(1)}, u32[]{:S(2)}, u32[]{:S(2)}) %collective-permute-start.9) | collective-permute-done | bytes 28704 | tf_op jit(solution)/shard_map/ppermute | solution.py:492
  32.0 1.6 %collective-permute-start.10 = (f32[3,8,128]{2,1,0:T(8,128)S(1)}, f32[3,8,128]{2,1,0:T(8,128)S(1)}, u32[]{:S(2)}, u32[]{:S(2)}) collective-permute-start(f32[3,8,128]{2,1,0:T(8,128)S(1)} %get-tuple-element.93), channel_id=1, source_target_pairs={{0,2},{1,3},{2,0},{3,1},{4,6},{5,7},{6,4},{7,5},{8,10},{9,11},{10,... | collective-permute-start | bytes 36872 | tf_op jit(solution)/shard_map/ppermute | solution.py:492
  33.6 0.2 shard_map.99
  33.7 2.0 %collective-permute-done.10.refs_3_ = f32[3,8,128]{2,1,0:T(8,128)S(1)} collective-permute-done((f32[3,8,128]{2,1,0:T(8,128)S(1)}, f32[3,8,128]{2,1,0:T(8,128)S(1)}, u32[]{:S(2)}, u32[]{:S(2)}) %collective-permute-start.10) | collective-permute-done | bytes 12320 | tf_op jit(solution)/shard_map/ppermute | solution.py:492
  35.7 1.3 %shard_map.101 = f32[8,16,128]{2,1,0:T(8,128)} custom-call(f32[16,8,128]{2,1,0:T(8,128)S(1)} %get-tuple-element.74._.applied, f32[16,8,128]{2,1,0:T(8,128)S(1)} %get-tuple-element.75.start, f32[7,16,8,128]{3,2,1,0:T(8,128)S(1)} %get-tuple-element.76.left, f32[7,16,8,128]{3,2,1,0:T(8,128)S(1)} %get-tuple-element.77.right, ...), custom_call_target="tpu_custom_call" | custom-call | flops 20000000 | bytes 1048576 | tf_op jit(solution)/shard_map/pallas_call | solution.py:24
  (3 shorter events, 0.1 us)
Async XLA Ops:
  2.2 11.1 %collective-permute-start = (f32[16,16,128]{2,1,0:T(8,128)S(1)}, f32[16,16,128]{2,1,0:T(8,128)S(1)}, u32[]{:S(2)}, u32[]{:S(2)}) collective-permute-start(f32[16,16,128]{2,1,0:T(8,128)S(1)} %get-tuple-element.65), channel_id=1, source_target_pairs={{0,4},{4,0},{8,12},{12,8},{16,20},{20,16},{24,28},{28,24},{1,5},{5... | collective-permute-start | bytes 393224 | tf_op jit(solution)/shard_map/ppermute | solution.py:699
  5.2 8.0 %collective-permute-start.1 = (f32[16,16,128]{2,1,0:T(8,128)S(1)}, f32[16,16,128]{2,1,0:T(8,128)S(1)}, u32[]{:S(2)}, u32[]{:S(2)}) collective-permute-start(f32[16,16,128]{2,1,0:T(8,128)S(1)} %get-tuple-element.66), channel_id=1, source_target_pairs={{0,28},{4,8},{8,4},{12,16},{16,12},{20,24},{24,20},{28,0},{1,29},{... | collective-permute-start | bytes 393224 | tf_op jit(solution)/shard_map/ppermute | solution.py:705
  9.1 4.1 %collective-permute-start.2 = (f32[17,8,128]{2,1,0:T(8,128)S(1)}, f32[17,8,128]{2,1,0:T(8,128)S(1)}, u32[]{:S(2)}, u32[]{:S(2)}) collective-permute-start(f32[17,8,128]{2,1,0:T(8,128)S(1)} %get-tuple-element.63.sent_a), channel_id=1, source_target_pairs={{0,1},{1,0},{2,3},{3,2},{4,5},{5,4},{6,7},{7,6},{8,9},{9,8},{10,11... | collective-permute-start | bytes 208904 | tf_op jit(solution)/shard_map/ppermute | solution.py:699
  9.2 4.1 %collective-permute-start.3 = (f32[17,8,128]{2,1,0:T(8,128)S(1)}, f32[17,8,128]{2,1,0:T(8,128)S(1)}, u32[]{:S(2)}, u32[]{:S(2)}) collective-permute-start(f32[17,8,128]{2,1,0:T(8,128)S(1)} %get-tuple-element.64.sent_b), channel_id=1, source_target_pairs={{0,3},{1,2},{2,1},{3,0},{4,7},{5,6},{6,5},{7,4},{8,11},{9,10},{10,... | collective-permute-start | bytes 208904 | tf_op jit(solution)/shard_map/ppermute | solution.py:705
  13.6 2.9 %collective-permute-start.4 = (f32[8,128]{1,0:T(8,128)S(1)}, f32[8,128]{1,0:T(8,128)S(1)}, u32[]{:S(2)}, u32[]{:S(2)}) collective-permute-start(f32[8,128]{1,0:T(8,128)S(1)} %get-tuple-element.67.refs_2_.face_a), channel_id=1, source_target_pairs={{0,1},{1,0},{2,3},{3,2},{4,5},{5,4},{6,7},{7,6},{8,9},{9,8},{10,11... | collective-permute-start | bytes 12296 | tf_op jit(solution)/shard_map/ppermute | solution.py:699
  13.9 3.0 %collective-permute-start.5 = (f32[8,128]{1,0:T(8,128)S(1)}, f32[8,128]{1,0:T(8,128)S(1)}, u32[]{:S(2)}, u32[]{:S(2)}) collective-permute-start(f32[8,128]{1,0:T(8,128)S(1)} %get-tuple-element.70.face_b), channel_id=1, source_target_pairs={{0,3},{1,2},{2,1},{3,0},{4,7},{5,6},{6,5},{7,4},{8,11},{9,10},{10,... | collective-permute-start | bytes 12296 | tf_op jit(solution)/shard_map/ppermute | solution.py:705
  17.2 4.2 %collective-permute-start.6 = (f32[7,16,128]{2,1,0:T(8,128)S(1)}, f32[7,16,128]{2,1,0:T(8,128)S(1)}, u32[]{:S(2)}, u32[]{:S(2)}) collective-permute-start(f32[7,16,128]{2,1,0:T(8,128)S(1)} %get-tuple-element.84.refs_0_), channel_id=1, source_target_pairs={{0,4},{4,0},{8,12},{12,8},{16,20},{20,16},{24,28},{28,24},{1,5},{5... | collective-permute-start | bytes 172040 | tf_op jit(solution)/shard_map/ppermute | solution.py:492
  21.4 4.2 %collective-permute-start.7 = (f32[7,16,128]{2,1,0:T(8,128)S(1)}, f32[7,16,128]{2,1,0:T(8,128)S(1)}, u32[]{:S(2)}, u32[]{:S(2)}) collective-permute-start(f32[7,16,128]{2,1,0:T(8,128)S(1)} %shard_map.96.refs_0_.refs_2_), channel_id=1, source_target_pairs={{0,8},{4,12},{8,0},{12,4},{16,24},{20,28},{24,16},{28,20},{1,9},{5... | collective-permute-start | bytes 172040 | tf_op jit(solution)/shard_map/ppermute | solution.py:492
  25.7 4.8 %collective-permute-start.8 = (f32[3,16,128]{2,1,0:T(8,128)S(1)}, f32[3,16,128]{2,1,0:T(8,128)S(1)}, u32[]{:S(2)}, u32[]{:S(2)}) collective-permute-start(f32[3,16,128]{2,1,0:T(8,128)S(1)} %get-tuple-element.86), channel_id=1, source_target_pairs={{0,16},{4,20},{8,24},{12,28},{16,0},{20,4},{24,8},{28,12},{1,17},{... | collective-permute-start | bytes 73736 | tf_op jit(solution)/shard_map/ppermute | solution.py:492
  30.7 1.3 %collective-permute-start.9 = (f32[7,8,128]{2,1,0:T(8,128)S(1)}, f32[7,8,128]{2,1,0:T(8,128)S(1)}, u32[]{:S(2)}, u32[]{:S(2)}) collective-permute-start(f32[7,8,128]{2,1,0:T(8,128)S(1)} %get-tuple-element.91.refs_0_), channel_id=1, source_target_pairs={{0,1},{1,0},{2,3},{3,2},{4,5},{5,4},{6,7},{7,6},{8,9},{9,8},{10,11... | collective-permute-start | bytes 86024 | tf_op jit(solution)/shard_map/ppermute | solution.py:492
  32.0 3.8 %collective-permute-start.10 = (f32[3,8,128]{2,1,0:T(8,128)S(1)}, f32[3,8,128]{2,1,0:T(8,128)S(1)}, u32[]{:S(2)}, u32[]{:S(2)}) collective-permute-start(f32[3,8,128]{2,1,0:T(8,128)S(1)} %get-tuple-element.93), channel_id=1, source_target_pairs={{0,2},{1,3},{2,0},{3,1},{4,6},{5,7},{6,4},{7,5},{8,10},{9,11},{10,... | collective-permute-start | bytes 36872 | tf_op jit(solution)/shard_map/ppermute | solution.py:492
